TPU v7x, 32 devices: a whole 2x2x4 slice. The times are simulated.
32 devices in a mesh: seq: 4 (over y, x), fsdp: 8 (over z, core).
Axes of the slice: x: 2, y: 2, z: 4, core: 2. Of those that a mesh axis runs over, the one named last changes fastest.
Arguments:
- tokens: bfloat16 [8, 1024, 2048], P('fsdp', 'seq'), may hold values from -6 to 6
- cotangent: bfloat16 [8, 1024, 2048], P('fsdp', 'seq'), may hold values from -6 to 6
- lengths: int32 [8], P('fsdp'), may hold values from 513 to 1024, as said below
- experts: int32 [8, 1024, 8], P('fsdp', 'seq'), may hold values from 0 to 15, all different within a row; in each aligned block of 256 rows (0 to 255, 256 to 511, ..., all dimensions but the last counted through in order) at most 136 rows name the same one
- attn_gain: bfloat16 [2048], P('fsdp'), may hold values from 0.25 to 1.75
- qkv_weight: bfloat16 [2048, 6144], P('fsdp'), may hold values from -0.125 to 0.125
- q_gain: bfloat16 [2048], P('fsdp'), may hold values from 0.25 to 1.75
- k_gain: bfloat16 [2048], P('fsdp'), may hold values from 0.25 to 1.75
- out_weight: bfloat16 [2048, 2048], P('fsdp'), may hold values from -2 to 2
- moe_gain: bfloat16 [2048], P('fsdp'), may hold values from 0.25 to 1.75
- router_weight: bfloat16 [2048, 16], P('fsdp'), may hold values from -0.0625 to 0.0625
- gate_up_weight: bfloat16 [16, 2048, 2048], P('seq', 'fsdp'), may hold values from -0.125 to 0.125
- down_weight: bfloat16 [16, 1024, 2048], P('seq', 'fsdp'), may hold values from -0.75 to 0.75
Outputs:
- block_out: bfloat16 [8, 1024, 2048], P('fsdp', 'seq')
- grad_tokens: bfloat16 [8, 1024, 2048], P('fsdp', 'seq')
- grad_attn_gain: float32 [2048], P('fsdp')
- grad_qkv_weight: float32 [2048, 6144], P('fsdp')
- grad_q_gain: float32 [2048], P('fsdp')
- grad_k_gain: float32 [2048], P('fsdp')
- grad_out_weight: float32 [2048, 2048], P('fsdp')
- grad_moe_gain: float32 [2048], P('fsdp')
- grad_router_weight: float32 [2048, 16], P('fsdp')
- grad_gate_up_weight: float32 [16, 2048, 2048], P('seq', 'fsdp')
- grad_down_weight: float32 [16, 1024, 2048], P('seq', 'fsdp')
Inputs may be any that keep to these rules, and one draw needn't show every extreme that they name: `lengths`: some sequence has all 1024 slots used. Each token names 8 different experts; within the 256 slots of one device no expert is named more than 136 times.
All inputs are finite; a program needn't handle non-finite values.
Results may differ from a plain program's by a relative error of at most 0.022.
Values may be sent and summed in bfloat16 or wider, within the bound.
A program may use at most 448 MiB of HBM per device.

v0:
```python
from functools import partial

import jax
import jax.numpy as jnp
from jax import lax
from jax.sharding import PartitionSpec as P

HEADS = 16
HEAD = 128
TOP = 8
CAP = 136


EPSILON = 1e-05
ROPE_BASE = 10000.0
NEG_FILL = -1e30


def rms_scale(values):
    return lax.rsqrt(jnp.mean(values * values, axis=-1, keepdims=True) + EPSILON)


def norm_back(grad_rows, unit_rows, scale_rows, gain_row):
    scaled = grad_rows * gain_row
    inner = jnp.mean(scaled * unit_rows, axis=-1, keepdims=True)
    return (scale_rows * (scaled - unit_rows * inner), jnp.sum(grad_rows * unit_rows, axis=0))


def rope_tables(positions):
    half_width = HEAD // 2
    frequency = ROPE_BASE ** (-(jnp.arange(half_width, dtype=jnp.float32) * 2.0 / HEAD))
    angles = positions[:, None] * frequency[None, :]
    return (
        jnp.concatenate([jnp.cos(angles), jnp.cos(angles)], -1),
        jnp.concatenate([jnp.sin(angles), jnp.sin(angles)], -1),
    )


def rotate(values, cosine_table, sine_table):
    half_width = values.shape[-1] // 2
    turned = jnp.concatenate([-values[..., half_width:], values[..., :half_width]], -1)
    return values * cosine_table[:, None, :] + turned * sine_table[:, None, :]


def rotate_back(grad_rows, cosine_table, sine_table):
    half_width = grad_rows.shape[-1] // 2
    sine_part = grad_rows * sine_table[:, None, :]
    return grad_rows * cosine_table[:, None, :] + jnp.concatenate(
        [sine_part[..., half_width:], -sine_part[..., :half_width]], -1
    )


def allowed_keys(block_start, row_count, key_count, length):
    query_place = block_start + jnp.arange(row_count, dtype=jnp.int32)
    key_place = jnp.arange(key_count, dtype=jnp.int32)
    return (key_place[None, :] <= query_place[:, None]) & (key_place[None, :] < length)


def attend_block(heads_in, length, row_count, block_start):
    queries, keys, values = heads_in
    query_block = lax.dynamic_slice_in_dim(queries, block_start, row_count, 0)
    scores = jnp.einsum(
        "qhd,khd->hqk", query_block, keys, preferred_element_type=jnp.float32
    ) * HEAD ** (-0.5)
    allowed = allowed_keys(block_start, row_count, keys.shape[0], length)
    scores = jnp.where(allowed[None], scores, NEG_FILL)
    row_max = jnp.max(scores, axis=-1, keepdims=True)
    exp_scores = jnp.exp(scores - row_max)
    denom_sum = jnp.sum(exp_scores, axis=-1, keepdims=True)
    probabilities = (exp_scores / denom_sum).astype(jnp.bfloat16)
    attended = jnp.einsum("hqk,khd->qhd", probabilities, values, preferred_element_type=jnp.float32)
    return (attended.astype(jnp.bfloat16), jnp.transpose((row_max + jnp.log(denom_sum))[..., 0]))


def attend_back(heads_in, grad_heads, log_sums, length, row_count, carried, block_start):
    queries, keys, values = heads_in
    grad_keys, grad_values = carried
    score_scale = HEAD ** (-0.5)
    query_block = lax.dynamic_slice_in_dim(queries, block_start, row_count, 0)
    grad_block = lax.dynamic_slice_in_dim(grad_heads, block_start, row_count, 0)
    sums_block = jnp.transpose(lax.dynamic_slice_in_dim(log_sums, block_start, row_count, 0))[
        :, :, None
    ]
    scores = (
        jnp.einsum("qhd,khd->hqk", query_block, keys, preferred_element_type=jnp.float32)
        * score_scale
    )
    allowed = allowed_keys(block_start, row_count, keys.shape[0], length)
    probabilities = jnp.where(allowed[None], jnp.exp(scores - sums_block), 0.0)
    low_probs = probabilities.astype(jnp.bfloat16)
    grad_probs = jnp.einsum("qhd,khd->hqk", grad_block, values, preferred_element_type=jnp.float32)
    grad_values = grad_values + jnp.einsum(
        "hqk,qhd->khd", low_probs, grad_block, preferred_element_type=jnp.float32
    )
    inner = jnp.sum(probabilities * grad_probs, axis=-1, keepdims=True)
    grad_scores = (probabilities * (grad_probs - inner)).astype(jnp.bfloat16)
    grad_query = (
        jnp.einsum("hqk,khd->qhd", grad_scores, keys, preferred_element_type=jnp.float32)
        * score_scale
    )
    grad_keys = (
        grad_keys
        + jnp.einsum("hqk,qhd->khd", grad_scores, query_block, preferred_element_type=jnp.float32)
        * score_scale
    )
    return ((grad_keys, grad_values), grad_query)


def expert_forward(row_block, weights):
    gate_up, down = weights
    half_width = down.shape[0]
    gate_up_out = jnp.dot(row_block, gate_up, preferred_element_type=jnp.float32)
    hidden = (jax.nn.silu(gate_up_out[:, :half_width]) * gate_up_out[:, half_width:]).astype(
        jnp.bfloat16
    )
    result = jnp.dot(hidden, down, preferred_element_type=jnp.float32).astype(jnp.bfloat16)
    return (gate_up_out, hidden, result)


def expert_backward(gate_up_out, grad_result, weights):
    gate_up, down = weights
    half_width = down.shape[0]
    grad_hidden = lax.dot_general(
        grad_result, down, (((1,), (1,)), ((), ())), preferred_element_type=jnp.float32
    )
    gate_part = gate_up_out[:, :half_width]
    up_part = gate_up_out[:, half_width:]
    sigmoid_gate = jax.nn.sigmoid(gate_part)
    grad_gate = grad_hidden * up_part * sigmoid_gate * (1.0 + gate_part * (1.0 - sigmoid_gate))
    grad_up = grad_hidden * gate_part * sigmoid_gate
    grad_mixed = jnp.concatenate([grad_gate, grad_up], -1).astype(jnp.bfloat16)
    grad_rows = lax.dot_general(
        grad_mixed, gate_up, (((1,), (1,)), ((), ())), preferred_element_type=jnp.float32
    ).astype(jnp.bfloat16)
    return (grad_rows, grad_mixed)


def local(
    tokens,
    cotangent,
    lengths,
    experts,
    attn_gain,
    qkv_weight,
    q_gain,
    k_gain,
    out_weight,
    moe_gain,
    router_weight,
    gate_up_weight,
    down_weight,
):
    seq_count = lax.axis_size("seq")
    seq_rank = lax.axis_index("seq")
    inputs = tokens[0].astype(jnp.float32)
    tok_count, model_width = inputs.shape
    local_count = gate_up_weight.shape[0]
    experts_count = local_count * seq_count
    length = lengths[0]
    positions = seq_rank * tok_count + jnp.arange(tok_count, dtype=jnp.int32)
    valid_mask = positions < length
    keep_mask = valid_mask.astype(jnp.float32)[:, None]
    gain_one, gain_q, gain_k, gain_two, router_full, qkv_full, out_full = (
        lax.all_gather(attn_gain, "fsdp", axis=0, tiled=True),
        lax.all_gather(q_gain, "fsdp", axis=0, tiled=True),
        lax.all_gather(k_gain, "fsdp", axis=0, tiled=True),
        lax.all_gather(moe_gain, "fsdp", axis=0, tiled=True),
        lax.all_gather(router_weight, "fsdp", axis=0, tiled=True),
        lax.all_gather(qkv_weight, "fsdp", axis=0, tiled=True),
        lax.all_gather(out_weight, "fsdp", axis=0, tiled=True),
    )
    gain_one = gain_one.astype(jnp.float32)
    gain_q = gain_q.astype(jnp.float32)
    gain_k = gain_k.astype(jnp.float32)
    gain_two = gain_two.astype(jnp.float32)
    scale_one = rms_scale(inputs)
    unit_one = inputs * scale_one
    normed = (unit_one * gain_one).astype(jnp.bfloat16)
    projected = jnp.dot(normed, qkv_full, preferred_element_type=jnp.float32)
    query_raw = projected[:, :model_width]
    key_raw = projected[:, model_width : 2 * model_width]
    value_raw = projected[:, 2 * model_width :]
    scale_q = rms_scale(query_raw)
    unit_q = query_raw * scale_q
    scale_k = rms_scale(key_raw)
    unit_k = key_raw * scale_k
    cosine_table, sine_table = rope_tables(positions.astype(jnp.float32))
    query_rot = rotate((unit_q * gain_q).reshape(tok_count, HEADS, HEAD), cosine_table, sine_table)
    key_rot = rotate((unit_k * gain_k).reshape(tok_count, HEADS, HEAD), cosine_table, sine_table)
    sent = jnp.stack([query_rot, key_rot, value_raw.reshape(tok_count, HEADS, HEAD)]).astype(
        jnp.bfloat16
    )
    by_head = lax.all_to_all(sent, "seq", split_axis=2, concat_axis=1, tiled=True)
    heads_in = (by_head[0], by_head[1], by_head[2])
    key_span = by_head.shape[1]
    heads_local = by_head.shape[2]
    row_count = min(512, key_span)
    block_starts = jnp.arange(key_span // row_count, dtype=jnp.int32) * row_count
    attended_blocks, sums_blocks = lax.map(
        partial(attend_block, heads_in, length, row_count), block_starts
    )
    attended_heads = attended_blocks.reshape(key_span, heads_local, HEAD)
    log_sums = sums_blocks.reshape(key_span, heads_local)
    attended = lax.all_to_all(
        attended_heads, "seq", split_axis=0, concat_axis=1, tiled=True
    ).reshape(tok_count, model_width)
    middle = inputs + jnp.dot(attended, out_full, preferred_element_type=jnp.float32) * keep_mask
    scale_two = rms_scale(middle)
    unit_two = middle * scale_two
    normed_two = (unit_two * gain_two).astype(jnp.bfloat16)
    logits = jnp.dot(normed_two, router_full, preferred_element_type=jnp.float32)
    chosen_ids = experts[0]
    chosen = jnp.take_along_axis(logits, chosen_ids, axis=1)
    row_max = jnp.max(chosen, axis=-1, keepdims=True)
    exp_chosen = jnp.exp(chosen - row_max)
    gates = exp_chosen / jnp.sum(exp_chosen, axis=-1, keepdims=True)
    expert_range = jnp.arange(experts_count, dtype=jnp.int32)
    id_match = (chosen_ids[:, :, None] == expert_range[None, None, :]).astype(jnp.float32)
    route_hits = (
        (chosen_ids[:, :, None] == expert_range[None, None, :]) & valid_mask[:, None, None]
    ).astype(jnp.int32)
    routed = jnp.sum(route_hits, axis=1)
    before = jnp.cumsum(routed, axis=0) - routed
    slot_of = jnp.minimum(before, CAP - 1)
    slot_pick = (routed.T[:, None, :] == 1) & (
        before.T[:, None, :] == jnp.arange(CAP, dtype=jnp.int32)[None, :, None]
    )
    take_rows = jnp.sum(
        slot_pick.astype(jnp.int32) * jnp.arange(tok_count, dtype=jnp.int32)[None, None, :], axis=-1
    )
    weight_all = jnp.sum(gates[:, :, None] * route_hits.astype(jnp.float32), axis=1)
    rows_all = jnp.take(normed_two, take_rows.reshape(-1), axis=0).reshape(
        experts_count, CAP, model_width
    )
    expert_rows = lax.all_to_all(rows_all, "seq", split_axis=0, concat_axis=1, tiled=True)
    weights_full = (
        lax.all_gather(gate_up_weight, "fsdp", axis=1, tiled=True),
        lax.all_gather(down_weight, "fsdp", axis=1, tiled=True),
    )

    def forward_step(carried, pieces):
        gate_up, down, row_block = pieces
        return (carried, expert_forward(row_block, (gate_up, down)))

    _, (gate_up_all, hidden_all, result_all) = lax.scan(
        forward_step, None, (weights_full[0], weights_full[1], expert_rows)
    )
    results = lax.all_to_all(result_all, "seq", split_axis=1, concat_axis=0, tiled=True)
    slot_chosen = jnp.take_along_axis(slot_of, chosen_ids, axis=1)
    flat_index = (chosen_ids * CAP + slot_chosen).reshape(-1)
    picked = (
        jnp.take(results.reshape(-1, model_width), flat_index, axis=0)
        .reshape(tok_count, TOP, model_width)
        .astype(jnp.float32)
    )
    moe_sum = jnp.sum(picked * (gates * keep_mask)[:, :, None], axis=1)
    block_out = (middle + moe_sum).astype(jnp.bfloat16)
    grad_out = cotangent[0].astype(jnp.float32) * keep_mask
    grad_gates = jnp.sum(picked * grad_out[:, None, :], axis=-1)
    grad_chosen = gates * (grad_gates - jnp.sum(gates * grad_gates, axis=-1, keepdims=True))
    grad_logits = jnp.sum(grad_chosen[:, :, None] * id_match, axis=1)
    router_wide = router_full.astype(jnp.float32)
    grad_normed_two = lax.dot_general(
        grad_logits, router_wide, (((1,), (1,)), ((), ())), precision=lax.Precision.HIGHEST
    )
    grad_router = lax.dot_general(
        normed_two.astype(jnp.float32),
        grad_logits,
        (((0,), (0,)), ((), ())),
        precision=lax.Precision.HIGHEST,
    )
    slot_weight = jnp.sum(slot_pick.astype(jnp.float32) * weight_all.T[:, None, :], axis=-1)
    grad_source = jnp.take(grad_out, take_rows.reshape(-1), axis=0).reshape(
        experts_count, CAP, model_width
    )
    grad_results = (grad_source * slot_weight[:, :, None]).astype(jnp.bfloat16)
    grad_in = lax.all_to_all(grad_results, "seq", split_axis=0, concat_axis=1, tiled=True)
    back_weights = (
        lax.all_gather(gate_up_weight, "fsdp", axis=1, tiled=True),
        lax.all_gather(down_weight, "fsdp", axis=1, tiled=True),
    )

    def back_step(carried, pieces):
        gate_up, down, row_block, gate_up_out, hidden, grad_result = pieces
        grad_rows, grad_mixed = expert_backward(gate_up_out, grad_result, (gate_up, down))
        grad_gate_up = lax.dot_general(
            row_block, grad_mixed, (((0,), (0,)), ((), ())), preferred_element_type=jnp.float32
        )
        grad_down = lax.dot_general(
            hidden, grad_result, (((0,), (0,)), ((), ())), preferred_element_type=jnp.float32
        )
        return (carried, (grad_rows, grad_gate_up, grad_down))

    _, (grad_rows_out, gate_up_grads, down_grads) = lax.scan(
        back_step,
        None,
        (back_weights[0], back_weights[1], expert_rows, gate_up_all, hidden_all, grad_in),
    )
    gate_up_sum, down_sum = (
        lax.psum_scatter(
            gate_up_grads.astype(jnp.bfloat16), "fsdp", scatter_dimension=1, tiled=True
        ).astype(jnp.float32),
        lax.psum_scatter(
            down_grads.astype(jnp.bfloat16), "fsdp", scatter_dimension=1, tiled=True
        ).astype(jnp.float32),
    )
    grad_rows_all = lax.all_to_all(grad_rows_out, "seq", split_axis=1, concat_axis=0, tiled=True)
    grad_back = (
        jnp.take(grad_rows_all.reshape(-1, model_width), flat_index, axis=0)
        .reshape(tok_count, TOP, model_width)
        .astype(jnp.float32)
    )
    grad_normed_two = grad_normed_two + jnp.sum(grad_back, axis=1) * keep_mask
    grad_middle_norm, grad_two = norm_back(grad_normed_two, unit_two, scale_two, gain_two)
    grad_middle = grad_out + grad_middle_norm
    grad_branch = (grad_middle * keep_mask).astype(jnp.bfloat16)
    grad_out_weight = lax.dot_general(
        attended, grad_branch, (((0,), (0,)), ((), ())), preferred_element_type=jnp.float32
    )
    grad_attended = lax.dot_general(
        grad_branch, out_full, (((1,), (1,)), ((), ())), preferred_element_type=jnp.float32
    ).astype(jnp.bfloat16)
    grad_heads = lax.all_to_all(
        grad_attended.reshape(tok_count, HEADS, HEAD),
        "seq",
        split_axis=1,
        concat_axis=0,
        tiled=True,
    )
    zero_heads = jnp.zeros((key_span, heads_local, HEAD), jnp.float32)
    (grad_key_heads, grad_value_heads), grad_query_blocks = lax.scan(
        partial(attend_back, heads_in, grad_heads, log_sums, length, row_count),
        (zero_heads, zero_heads),
        block_starts,
    )
    grad_query_heads = grad_query_blocks.reshape(key_span, heads_local, HEAD)
    grad_sent = jnp.stack([grad_query_heads, grad_key_heads, grad_value_heads]).astype(jnp.bfloat16)
    grad_by_token = lax.all_to_all(grad_sent, "seq", split_axis=1, concat_axis=2, tiled=True)
    grad_query_norm = rotate_back(
        grad_by_token[0].astype(jnp.float32), cosine_table, sine_table
    ).reshape(tok_count, model_width)
    grad_key_norm = rotate_back(
        grad_by_token[1].astype(jnp.float32), cosine_table, sine_table
    ).reshape(tok_count, model_width)
    grad_value = grad_by_token[2].astype(jnp.float32).reshape(tok_count, model_width)
    grad_query_raw, grad_qgain = norm_back(grad_query_norm, unit_q, scale_q, gain_q)
    grad_key_raw, grad_kgain = norm_back(grad_key_norm, unit_k, scale_k, gain_k)
    grad_projected = jnp.concatenate([grad_query_raw, grad_key_raw, grad_value], axis=1).astype(
        jnp.bfloat16
    )
    grad_qkv = lax.dot_general(
        normed, grad_projected, (((0,), (0,)), ((), ())), preferred_element_type=jnp.float32
    )
    grad_normed = lax.dot_general(
        grad_projected, qkv_full, (((1,), (1,)), ((), ())), preferred_element_type=jnp.float32
    )
    grad_inputs_norm, grad_one = norm_back(grad_normed, unit_one, scale_one, gain_one)
    grad_tokens = (grad_middle + grad_inputs_norm).astype(jnp.bfloat16)
    param_parts = (
        lax.psum_scatter(
            grad_one.astype(jnp.bfloat16), "fsdp", scatter_dimension=0, tiled=True
        ).astype(jnp.float32),
        lax.psum_scatter(
            grad_qgain.astype(jnp.bfloat16), "fsdp", scatter_dimension=0, tiled=True
        ).astype(jnp.float32),
        lax.psum_scatter(
            grad_kgain.astype(jnp.bfloat16), "fsdp", scatter_dimension=0, tiled=True
        ).astype(jnp.float32),
        lax.psum_scatter(
            grad_two.astype(jnp.bfloat16), "fsdp", scatter_dimension=0, tiled=True
        ).astype(jnp.float32),
        lax.psum_scatter(
            grad_router.astype(jnp.bfloat16), "fsdp", scatter_dimension=0, tiled=True
        ).astype(jnp.float32),
        lax.psum_scatter(
            grad_qkv.astype(jnp.bfloat16), "fsdp", scatter_dimension=0, tiled=True
        ).astype(jnp.float32),
        lax.psum_scatter(
            grad_out_weight.astype(jnp.bfloat16), "fsdp", scatter_dimension=0, tiled=True
        ).astype(jnp.float32),
    )
    param_parts = (
        lax.psum(param_parts[0].astype(jnp.bfloat16), "seq").astype(jnp.float32),
        lax.psum(param_parts[1].astype(jnp.bfloat16), "seq").astype(jnp.float32),
        lax.psum(param_parts[2].astype(jnp.bfloat16), "seq").astype(jnp.float32),
        lax.psum(param_parts[3].astype(jnp.bfloat16), "seq").astype(jnp.float32),
        lax.psum(param_parts[4].astype(jnp.bfloat16), "seq").astype(jnp.float32),
        lax.psum(param_parts[5].astype(jnp.bfloat16), "seq").astype(jnp.float32),
        lax.psum(param_parts[6].astype(jnp.bfloat16), "seq").astype(jnp.float32),
    )
    return (
        block_out[None],
        grad_tokens[None],
        param_parts[0],
        param_parts[5],
        param_parts[1],
        param_parts[2],
        param_parts[6],
        param_parts[3],
        param_parts[4],
        gate_up_sum,
        down_sum,
    )


def solution(mesh):
    in_specs = (
        P("fsdp", "seq", None),
        P("fsdp", "seq", None),
        P("fsdp"),
        P("fsdp", "seq", None),
        P("fsdp"),
        P("fsdp", None),
        P("fsdp"),
        P("fsdp"),
        P("fsdp", None),
        P("fsdp"),
        P("fsdp", None),
        P("seq", "fsdp", None),
        P("seq", "fsdp", None),
    )
    out_specs = (
        P("fsdp", "seq", None),
        P("fsdp", "seq", None),
        P("fsdp"),
        P("fsdp", None),
        P("fsdp"),
        P("fsdp"),
        P("fsdp", None),
        P("fsdp"),
        P("fsdp", None),
        P("seq", "fsdp", None),
        P("seq", "fsdp", None),
    )
    return jax.shard_map(local, mesh=mesh, in_specs=in_specs, out_specs=out_specs, check_vma=False)
```

profile of v0, /device:TPU:0, one launch (start us, length us, event | category | flops | bytes accessed | tf_op | source)
XLA Modules:
  0.0 2519.0 jit_solution(17940893591658366700)
XLA Ops:
  10.1 13.5 all-gather
  23.6 9.2 all-gather.1
  32.8 14.9 all-gather.2
  48.7 183.6 %all-gather.9.cloned.1.call-done = bf16[2048,6144]{1,0:T(8,128)(2,1)} async-done(((bf16[256,6144]{1,0:T(8,128)(2,1)}), bf16[2048,6144]{1,0:T(8,128)(2,1)}) %all-gather.9.cloned.1.call-update) | async-done | bytes 25165840 | tf_op jit(solution)/shard_map/all_gather | solution.py:169
  232.3 12.3 fusion.116
  260.5 9.0 all-gather.3
  271.8 24.8 all-to-all-done
  297.0 24.3 while.55
  330.5 12.6 all-to-all-done.1
  347.2 6.2 multiply_reduce_fusion.7
  355.0 9.6 gather_fusion
  364.6 8.0 broadcast_select_fusion
  378.6 97.6 %all-to-all-done.2 = bf16[16,136,2048]{2,1,0:T(8,128)(2,1)} async-done(((bf16[16,136,2048]{2,1,0:T(8,128)(2,1)}), bf16[16,136,2048]{2,1,0:T(8,128)(2,1)}, u32[]{:S(2)}, u32[]{:S(2)}) %all-to-all-start.2) | async-done | bytes 8912928 | tf_op jit(solution)/shard_map/all_to_all | solution.py:235
  476.2 10.3 copy.236
  486.5 267.2 %all-gather.13.cloned.1.call-done = bf16[4,2048,2048]{2,1,0:T(8,128)(2,1)} async-done(((bf16[4,256,2048]{2,1,0:T(8,128)(2,1)}), bf16[4,2048,2048]{2,1,0:T(8,128)(2,1)}) %all-gather.13.cloned.1.call-update) | async-done | bytes 33554448 | tf_op jit(solution)/shard_map/all_gather | solution.py:237
  758.3 75.0 %while.56 = (s32[]{:T(128)}, f32[4,544,2048]{2,1,0:T(8,128)}, bf16[4,544,1024]{2,1,0:T(8,128)(2,1)}, bf16[4,544,2048]{2,1,0:T(8,128)(2,1)}, bf16[4,544,2048]{2,1...) while((s32[]{:T(128)}, f32[4,544,2048]{2,1,0:T(8,128)}, ...), condition=%wide.region_13.14_spmd, body=%wide.region_12.13_spmd.sunk | while | flops 6849560576 | bytes 33754196 | solution.py:245
  758.3 11.0 bitcast_dynamic-update-slice_fusion.11
  771.1 6.0 fusion.200
  777.1 10.9 bitcast_dynamic-update-slice_fusion.11
  789.8 6.1 fusion.200
  795.9 10.9 bitcast_dynamic-update-slice_fusion.11
  814.5 10.9 bitcast_dynamic-update-slice_fusion.11
  827.2 6.0 fusion.200
  833.3 29.5 %copy.237 = bf16[4,544,2048]{2,0,1:T(4,128)(2,1)} copy(bf16[4,544,2048]{2,1,0:T(8,128)(2,1)} %get-tuple-element.208) | data formatting | bytes 17825792 | tf_op jit(solution)/shard_map/while | solution.py:245
  869.5 11.1 gather_fusion.1
  880.7 16.8 gather_fusion.2
  897.5 14.4 all_gather.37
  912.9 16.8 gather_fusion.3
  930.5 36.8 %all-to-all-done.3 = bf16[4,544,2048]{2,0,1:T(4,128)(2,1)} async-done(((bf16[4,544,2048]{2,0,1:T(4,128)(2,1)}), bf16[4,544,2048]{2,0,1:T(4,128)(2,1)}, u32[]{:S(2)}, u32[]{:S(2)}) %all-to-all-start.3) | async-done | bytes 8912928 | tf_op jit(solution)/shard_map/all_to_all | solution.py:248
  967.4 11.9 copy.238
  979.3 21.0 gather_fusion.4
  1007.6 9.8 multiply_convert_fusion.2
  1023.4 97.8 %all-to-all-done.4 = bf16[16,136,2048]{2,1,0:T(8,128)(2,1)} async-done(((bf16[16,136,2048]{2,1,0:T(8,128)(2,1)}), bf16[16,136,2048]{2,1,0:T(8,128)(2,1)}, u32[]{:S(2)}, u32[]{:S(2)}) %all-to-all-start.4) | async-done | bytes 8912928 | tf_op jit(solution)/shard_map/all_to_all | solution.py:277
  1121.2 8.9 copy.243
  1134.6 147.3 %while.57 = (s32[]{:T(128)}, bf16[4,544,2048]{2,1,0:T(8,128)(2,1)}, bf16[4,2048,2048]{2,1,0:T(8,128)(2,1)}, bf16[4,1024,2048]{2,1,0:T(8,128)(2,1)}, bf16[4,544,2...) while((s32[]{:T(128)}, bf16[4,544,2048]{2,1,0:T(8,128)(2,1)}, ...), condition=%wide.region_23.25_spmd, body=%wide.region_22.24_spmd.sunk | while | flops 13707476992 | bytes 103486096 | solution.py:294
  1144.8 10.8 bitcast_dynamic-update-slice_fusion.13
  1155.6 9.5 fusion.206
  1165.1 6.3 bitcast_dynamic-update-slice_fusion.14
  1181.6 10.8 bitcast_dynamic-update-slice_fusion.13
  1192.5 9.4 fusion.206
  1201.9 6.3 bitcast_dynamic-update-slice_fusion.14
  1218.4 10.8 bitcast_dynamic-update-slice_fusion.13
  1229.2 9.4 fusion.206
  1238.6 6.4 bitcast_dynamic-update-slice_fusion.14
  1255.2 10.8 bitcast_dynamic-update-slice_fusion.13
  1266.0 9.4 fusion.206
  1275.4 6.4 bitcast_dynamic-update-slice_fusion.14
  1281.9 29.5 %copy.244 = bf16[4,544,2048]{2,0,1:T(4,128)(2,1)} copy(bf16[4,544,2048]{2,1,0:T(8,128)(2,1)} %get-tuple-element.211) | data formatting | bytes 17825792 | tf_op jit(solution)/shard_map/while | solution.py:294
  1317.5 97.4 %all-to-all-done.5 = bf16[4,544,2048]{2,0,1:T(4,128)(2,1)} async-done(((bf16[4,544,2048]{2,0,1:T(4,128)(2,1)}), bf16[4,544,2048]{2,0,1:T(4,128)(2,1)}, u32[]{:S(2)}, u32[]{:S(2)}) %all-to-all-start.5) | async-done | bytes 8912928 | tf_op jit(solution)/shard_map/all_to_all | solution.py:307
  1414.8 12.0 copy.245
  1426.8 21.0 gather_fusion.5
  1447.9 17.6 convert_reduce_fusion
  1478.5 7.4 convolution_convert_fusion.1
  1494.0 50.6 %while.58 = (s32[]{:T(128)}, f32[1024,4,128]{0,2,1:T(8,128)S(1)}, f32[1024,4,128]{0,2,1:T(8,128)}, bf16[2,512,4,128]{3,1,0,2:T(8,128)(2,1)}, s32[2]{0:T(128)S(1)...) while((s32[]{:T(128)}, f32[1024,4,128]{0,2,1:T(8,128)S(1)}, ...), condition=%wide.region_28.30_spmd.clone, body=%wide.region_26.29_spmd.clone.sunk | while | flops 2719743488 | bytes 180419552 | solution.py:331
  1552.4 38.9 %all_to_all.129 = bf16[3,1024,4,128]{3,2,0,1:T(4,128)(2,1)S(1)} all-to-all(bf16[3,1024,4,128]{3,2,0,1:T(4,128)(2,1)S(1)} %copy.251), channel_id=1, replica_groups=mesh['seq'=4,'fsdp'=8] {'seq'}, dimensions={1} | all-to-all | bytes 6291456 | tf_op jit(solution)/shard_map/all_to_all | solution.py:338
  1613.6 13.6 convolution_convert_fusion
  1630.5 240.7 %reduce-scatter.6.cloned.1.call-done = bf16[256,6144]{1,0:T(8,128)(2,1)} async-done(((bf16[2048,6144]{1,0:T(8,128)(2,1)}), bf16[256,6144]{1,0:T(8,128)(2,1)}) %reduce-scatter.6.cloned.1.call-update) | async-done | bytes 3145744 | tf_op jit(solution)/shard_map/reduce_scatter | solution.py:375
  1873.2 14.1 fusion.102
  1887.3 26.0 %all-reduce.4 = (bf16[2048]{0:T(1024)(128)(2,1)S(1)}, bf16[2048]{0:T(1024)(128)(2,1)S(1)}, bf16[2048]{0:T(1024)(128)(2,1)S(1)}, bf16[2048]{0:T(1024)(128)(2,1)S(1)}) all-reduce(bf16[2048]{0:T(1024)(128)(2,1)S(1)} %get-tuple-element.264, ...), channel_id=2, replica_groups=mesh['seq'=4,'fsdp'=8] {'fsdp'}, use_global_device_ids=true, to_apply=%region_33.35.clone | all-reduce | flops 8192 | bytes 32768
  1913.7 16.1 all-reduce.5
  1935.8 136.0 %reduce-scatter.14.cloned.1.call-done = bf16[4,128,2048]{2,1,0:T(8,128)(2,1)} async-done(((bf16[4,1024,2048]{2,1,0:T(8,128)(2,1)}), bf16[4,128,2048]{2,1,0:T(8,128)(2,1)}) %reduce-scatter.14.cloned.1.call-update) | async-done | bytes 2097168 | tf_op jit(solution)/shard_map/reduce_scatter | solution.py:303
  2075.9 101.5 %all-reduce.9.cloned.1.call-done = (bf16[256,6144]{1,0:T(8,128)(2,1)}, bf16[256,2048]{1,0:T(8,128)(2,1)}) async-done(((bf16[256,6144]{1,0:T(8,128)(2,1)}, bf16[256,2048]{1,0:T(8,128)(2,1)}), (bf16[256,6144]{1,0:T(8,128)(2,1)}, bf16[256,2048]{1,0:T(8,128)(2,1)})) %all-reduce.9.cloned.1.call-update) | async-done | bytes 4194320 | tf_op jit(solution)/shard_map/psum | solution.py:388
  2184.4 320.7 %reduce-scatter.12.cloned.1.call-done = bf16[4,256,2048]{2,1,0:T(8,128)(2,1)} async-done(((bf16[4,2048,2048]{2,1,0:T(8,128)(2,1)}), bf16[4,256,2048]{2,1,0:T(8,128)(2,1)}) %reduce-scatter.12.cloned.1.call-update) | async-done | bytes 4194320 | tf_op jit(solution)/shard_map/reduce_scatter | solution.py:300
  2505.1 6.7 convert_element_type.262
  (428 shorter events, 272.0 us)
Async XLA Ops:
  7.2 225.2 %all-gather.9.cloned.1.call-start = ((), (), s32[]{:S(2)}) async-start(), calls=%async_computation.13 | async-start | bytes 28311552 | tf_op jit(solution)/shard_map/all_gather | solution.py:169
  7.9 339.2 %all-gather.11.cloned.1.call-start = ((), (), s32[]{:S(2)}) async-start(), calls=%async_computation.14 | async-start | bytes 9437184 | tf_op jit(solution)/shard_map/all_gather | solution.py:170
  8.7 477.8 %all-gather.15.cloned.1.call-start = ((), (), s32[]{:S(2)}) async-start(), calls=%async_computation.16 | async-start | bytes 18874368 | tf_op jit(solution)/shard_map/all_gather | solution.py:238
  9.4 14.1 copy-start.86
  9.4 23.3 copy-start.87
  9.4 38.9 %copy-start.18 = (bf16[1,256,2048]{2,1,0:T(8,128)(2,1)S(1)}, bf16[1,256,2048]{2,1,0:T(8,128)(2,1)}, u32[]{:S(2)}) copy-start(bf16[1,256,2048]{2,1,0:T(8,128)(2,1)} %param.23) | copy-start | bytes 3145732
  9.4 744.3 %all-gather.13.cloned.1.call-start = ((), (), s32[]{:S(2)}) async-start(), calls=%async_computation.15 | async-start | bytes 37748736 | tf_op jit(solution)/shard_map/all_gather | solution.py:237
  23.5 221.2 %copy-start.39 = (f32[8,1,256]{2,1,0:T(1,128)}, f32[8,1,256]{2,1,0:T(1,128)S(1)}, u32[]{:S(2)}) copy-start(f32[8,1,256]{2,1,0:T(1,128)S(1)} %convert_element_type.273) | copy-start | bytes 24580
  32.7 212.4 %copy-start.51 = (f32[8,1,256]{2,1,0:T(1,128)}, f32[8,1,256]{2,1,0:T(1,128)S(1)}, u32[]{:S(2)}) copy-start(f32[8,1,256]{2,1,0:T(1,128)S(1)} %convert_element_type.274) | copy-start | bytes 24580
  47.7 197.5 %copy-start.53 = (f32[8,1,256]{2,1,0:T(1,128)}, f32[8,1,256]{2,1,0:T(1,128)S(1)}, u32[]{:S(2)}) copy-start(f32[8,1,256]{2,1,0:T(1,128)S(1)} %convert_element_type.275) | copy-start | bytes 24580
  48.4 203.3 %copy-start.32 = (f32[256,128]{1,0:T(8,128)}, f32[256,128]{1,0:T(8,128)S(1)}, u32[]{:S(2)}) copy-start(f32[256,128]{1,0:T(8,128)S(1)} %get-tuple-element.402) | copy-start | bytes 393220
  48.4 203.3 %copy-start.34 = (f32[256,128]{1,0:T(8,128)}, f32[256,128]{1,0:T(8,128)S(1)}, u32[]{:S(2)}) copy-start(f32[256,128]{1,0:T(8,128)S(1)} %get-tuple-element.401) | copy-start | bytes 393220
  48.7 196.0 %copy-start.61 = (f32[256]{0:T(256)}, f32[256]{0:T(256)S(1)}, u32[]{:S(2)}) copy-start(f32[256]{0:T(256)S(1)} %add_rsqrt_fusion.3) | copy-start | bytes 3076
  256.0 13.6 copy-start.43
  256.0 40.6 %all-to-all-start = ((bf16[3,256,16,128]{3,1,0,2:T(8,128)(2,1)}), bf16[3,256,16,128]{3,1,0,2:T(8,128)(2,1)S(1)}, u32[]{:S(2)}, u32[]{:S(2)}) async-start(bf16[3,256,16,128]{3,1,0,2:T(8,128)(2,1)} %pad_maximum_fusion.3), calls=%async_computation | async-start | bytes 6291456 | tf_op jit(solution)/shard_map/all_to_all | solution.py:193
  269.5 83.9 %copy-start.55 = (f32[8,1,256]{2,1,0:T(1,128)}, f32[8,1,256]{2,1,0:T(1,128)S(1)}, u32[]{:S(2)}) copy-start(f32[8,1,256]{2,1,0:T(1,128)S(1)} %convert_element_type.276) | copy-start | bytes 24580
  269.5 77.6 %copy-start.63 = (f32[256]{0:T(256)}, f32[256]{0:T(256)S(1)}, u32[]{:S(2)}) copy-start(f32[256]{0:T(256)S(1)} %get-tuple-element.359) | copy-start | bytes 3076
  270.0 59.6 %copy-start.41 = (s32[256,16]{0,1:T(8,128)}, s32[256,16]{0,1:T(8,128)S(1)}, u32[]{:S(2)}) copy-start(s32[256,16]{0,1:T(8,128)S(1)} %convert_reduce_fusion.1) | copy-start | bytes 49156
  270.9 25.8 %copy-start.45 = (s32[16,2,128]{2,0,1:T(8,128)}, s32[16,2,128]{2,0,1:T(8,128)S(1)}, u32[]{:S(2)}) copy-start(s32[16,2,128]{2,0,1:T(8,128)S(1)} %reduce-window.6) | copy-start | bytes 49156
  271.8 57.9 %copy-start.49 = (s32[16,256]{1,0:T(8,128)}, s32[16,256]{1,0:T(8,128)S(1)}, u32[]{:S(2)}) copy-start(s32[16,256]{1,0:T(8,128)S(1)} %bitcast_subtract_fusion) | copy-start | bytes 49156
  321.3 8.3 copy-start.90
  321.3 24.1 copy-start.6
  321.3 24.1 copy-start.10
  321.3 24.1 copy-start.12
  321.3 24.1 copy-start.57
  325.3 17.8 all-to-all-start.1
  330.5 34.1 %copy-start.66 = (pred[16,136]{1,0:T(8,128)(4,1)}, pred[16,136]{1,0:T(8,128)(4,1)S(1)}, u32[]{:S(2)}) copy-start(pred[16,136]{1,0:T(8,128)(4,1)S(1)} %compare_and_fusion) | copy-start | bytes 6532
  353.4 11.2 copy-start.78
  355.0 9.7 copy-start
  372.7 103.5 %all-to-all-start.2 = ((bf16[16,136,2048]{2,1,0:T(8,128)(2,1)}), bf16[16,136,2048]{2,1,0:T(8,128)(2,1)}, u32[]{:S(2)}, u32[]{:S(2)}) async-start(bf16[16,136,2048]{2,1,0:T(8,128)(2,1)} %broadcast_select_fusion), calls=%async_computation.2 | async-start | bytes 17825792 | tf_op jit(solution)/shard_map/all_to_all | solution.py:235
  862.8 104.6 %all-to-all-start.3 = ((bf16[4,544,2048]{2,0,1:T(4,128)(2,1)}), bf16[4,544,2048]{2,0,1:T(4,128)(2,1)}, u32[]{:S(2)}, u32[]{:S(2)}) async-start(bf16[4,544,2048]{2,0,1:T(4,128)(2,1)} %copy.237), calls=%async_computation.3 | async-start | bytes 17825792 | tf_op jit(solution)/shard_map/all_to_all | solution.py:248
  869.4 11.2 copy-start.42
  869.5 11.2 copy-start.46
  869.5 11.1 copy-start.81
  880.7 16.8 copy-start.82
  880.7 31.8 %copy-start.1 = (bf16[256,2048]{1,0:T(8,128)(2,1)S(1)}, bf16[256,2048]{1,0:T(8,128)(2,1)}, u32[]{:S(2)}) copy-start(bf16[256,2048]{1,0:T(8,128)(2,1)} %copy-done) | copy-start | bytes 3145732
  911.9 88.4 %copy-start.71 = (pred[2048]{0:T(1024)(128)(4,1)}, pred[2048]{0:T(1024)(128)(4,1)S(1)}, u32[]{:S(2)}) copy-start(pred[2048]{0:T(1024)(128)(4,1)S(1)} %compare_and_fusion.1) | copy-start | bytes 6148
  912.5 66.8 %copy-start.59 = (s32[2048]{0:T(1024)}, s32[2048]{0:T(1024)S(1)}, u32[]{:S(2)}) copy-start(s32[2048]{0:T(1024)S(1)} %broadcast_clamp_fusion) | copy-start | bytes 24580
  1000.2 6.7 copy-start.50
  1000.3 7.3 copy-start.67
  1017.4 103.8 %all-to-all-start.4 = ((bf16[16,136,2048]{2,1,0:T(8,128)(2,1)}), bf16[16,136,2048]{2,1,0:T(8,128)(2,1)}, u32[]{:S(2)}, u32[]{:S(2)}) async-start(bf16[16,136,2048]{2,1,0:T(8,128)(2,1)} %multiply_convert_fusion.2), calls=%async_computation.4 | async-start | bytes 17825792 | tf_op jit(solution)/shard_map/all_to_all | solution.py:277
  1311.5 103.4 %all-to-all-start.5 = ((bf16[4,544,2048]{2,0,1:T(4,128)(2,1)}), bf16[4,544,2048]{2,0,1:T(4,128)(2,1)}, u32[]{:S(2)}, u32[]{:S(2)}) async-start(bf16[4,544,2048]{2,0,1:T(4,128)(2,1)} %copy.244), calls=%async_computation.5 | async-start | bytes 17825792 | tf_op jit(solution)/shard_map/all_to_all | solution.py:307
  1414.8 12.0 copy-start.60
  1426.8 21.1 copy-start.72
  1447.9 17.7 copy-start.15
  1447.9 17.7 copy-start.38
  1447.9 17.7 copy-start.47
  1447.9 17.7 copy-start.56
  1447.9 17.7 copy-start.65
  1447.9 17.7 copy-start.79
  1474.2 17.5 all-to-all-start.6
  1478.4 152.0 %reduce-scatter.8.cloned.1.call-start = ((), (), s32[]{:S(2)}) async-start(), calls=%async_computation.18 | async-start | bytes 9437184 | tf_op jit(solution)/shard_map/reduce_scatter | solution.py:378
  1485.9 8.0 copy-start.7
  1485.9 8.0 copy-start.58
  1485.9 8.0 copy-start.91
  1486.0 385.2 %reduce-scatter.6.cloned.1.call-start = ((), (), s32[]{:S(2)}) async-start(), calls=%async_computation.17 | async-start | bytes 28311552 | tf_op jit(solution)/shard_map/reduce_scatter | solution.py:375
  1613.4 13.8 copy-start.28
  1613.4 13.8 copy-start.29
  1627.3 286.4 %reduce-scatter.10.cloned.1.call-start = ((), (), s32[]{:S(2)}) async-start(), calls=%async_computation.19 | async-start | bytes 73728 | tf_op jit(solution)/shard_map/reduce_scatter | solution.py:372
  1629.6 442.1 %reduce-scatter.14.cloned.1.call-start = ((), (), s32[]{:S(2)}) async-start(), calls=%async_computation.21 | async-start | bytes 18874368 | tf_op jit(solution)/shard_map/reduce_scatter | solution.py:303
  1630.4 547.0 %all-reduce.9.cloned.1.call-start = ((), (), s32[]{:S(2)}) async-start(), calls=%async_computation.22 | async-start | bytes 8388608 | tf_op jit(solution)/shard_map/psum | solution.py:388
  1871.2 633.9 %reduce-scatter.12.cloned.1.call-start = ((), (), s32[]{:S(2)}) async-start(), calls=%async_computation.20 | async-start | bytes 37748736 | tf_op jit(solution)/shard_map/reduce_scatter | solution.py:300
  1873.2 14.2 copy-start.77
  1873.2 59.4 %copy-start.17 = (f32[256,2048]{1,0:T(8,128)S(1)}, f32[256,2048]{1,0:T(8,128)}, u32[]{:S(2)}) copy-start(f32[256,2048]{1,0:T(8,128)} %copy-done.16) | copy-start | bytes 6291460
  (60 other events, 203.7 us)
Sparse Core Ops, SparseCore 0:
  9.6 222.6 all-gather.8
  233.9 80.2 all-gather.10
  315.9 149.5 all-gather.14
  466.9 286.7 all-gather.12
  1486.1 88.1 reduce-scatter.7
  1627.4 243.7 reduce-scatter.5
  1874.0 28.9 reduce-scatter.9
  1905.4 166.3 reduce-scatter.13
  2075.3 102.0 all-reduce.8
  2179.6 325.4 reduce-scatter.11
where the time goes:
time: 2530 us; the launch traced here: 2520 us
  waiting for transfers between devices  1630 us (64%)
  matrix products  298 us (12%)
  local copies, waits for them, and re-layouts  272 us (11%)
  blocking collectives  142 us (6%)
  other arithmetic  118 us (5%)
  starting transfers between devices  36.4 us (1%)
    reduce_scatter x1, waiting for transfers between devices, local(): lax.psum_scatter(gate_up_grads.astype(jnp.bfloat16), 'fsdp', scatter_dime...  321 us
    all_gather x1, waiting for transfers between devices, local(): lax.all_gather(gate_up_weight, 'fsdp', axis=1, tiled=True)  267 us
    reduce_scatter x1, waiting for transfers between devices, local(): lax.psum_scatter(grad_qkv.astype(jnp.bfloat16), 'fsdp', scatter_dimension...  241 us
    all_gather x1, waiting for transfers between devices, local(): lax.all_gather(qkv_weight, 'fsdp', axis=0, tiled=True)  184 us
    reduce_scatter x1, waiting for transfers between devices, local(): lax.psum_scatter(down_grads.astype(jnp.bfloat16), 'fsdp', scatter_dimensi...  136 us
    psum x1, waiting for transfers between devices, local(): lax.psum(param_parts[5].astype(jnp.bfloat16), 'seq').astype(jnp.float32)  102 us
    all_to_all x1, waiting for transfers between devices, local(): lax.all_to_all(grad_results, 'seq', split_axis=0, concat_axis=1, tiled=True)  97.8 us
    all_to_all x1, waiting for transfers between devices, local(): lax.all_to_all(rows_all, 'seq', split_axis=0, concat_axis=1, tiled=True)  97.6 us
  transfers between devices with their start and end apart: 17, of which 13 were waited for; matrix products, arithmetic and copies ran while one was open for 10% of the time, Pallas kernels for 0%

commit v1 on v0

v1 whole, which is shorter than its diff:
```python
from functools import partial

import jax
import jax.numpy as jnp
from jax import lax
from jax.sharding import PartitionSpec as P

HEADS = 16
HEAD = 128
TOP = 8
CAP = 136


EPSILON = 1e-05
ROPE_BASE = 10000.0
NEG_FILL = -1e30


def round_up(count, unit):
    return -(-count // unit) * unit


def rms_scale(values):
    return lax.rsqrt(jnp.mean(values * values, axis=-1, keepdims=True) + EPSILON)


def norm_back(grad_rows, unit_rows, scale_rows, gain_row):
    scaled = grad_rows * gain_row
    inner = jnp.mean(scaled * unit_rows, axis=-1, keepdims=True)
    return (scale_rows * (scaled - unit_rows * inner), jnp.sum(grad_rows * unit_rows, axis=0))


def rope_tables(positions):
    half_width = HEAD // 2
    frequency = ROPE_BASE ** (-(jnp.arange(half_width, dtype=jnp.float32) * 2.0 / HEAD))
    angles = positions[:, None] * frequency[None, :]
    return (
        jnp.concatenate([jnp.cos(angles), jnp.cos(angles)], -1),
        jnp.concatenate([jnp.sin(angles), jnp.sin(angles)], -1),
    )


def rotate(values, cosine_table, sine_table):
    half_width = values.shape[-1] // 2
    turned = jnp.concatenate([-values[..., half_width:], values[..., :half_width]], -1)
    return values * cosine_table[:, None, :] + turned * sine_table[:, None, :]


def rotate_back(grad_rows, cosine_table, sine_table):
    half_width = grad_rows.shape[-1] // 2
    sine_part = grad_rows * sine_table[:, None, :]
    return grad_rows * cosine_table[:, None, :] + jnp.concatenate(
        [sine_part[..., half_width:], -sine_part[..., :half_width]], -1
    )


def from_peer(values, step):
    if step == 0:
        return values
    count = lax.axis_size("seq")
    return lax.ppermute(values, "seq", [(rank, rank ^ step) for rank in range(count)])


def gather_blocks(values):
    return jnp.stack([from_peer(values, step) for step in range(lax.axis_size("seq"))])


def return_blocks(blocks):
    return [from_peer(blocks[step], step) for step in range(lax.axis_size("seq"))]


def in_rank_order(parts):
    seq_rank = lax.axis_index("seq")
    buffer = jnp.zeros((len(parts),) + parts[0].shape, parts[0].dtype)
    for step, part in enumerate(parts):
        start = (seq_rank ^ step,) + (0,) * part.ndim
        buffer = lax.dynamic_update_slice(buffer, part[None], start)
    return buffer


def attend_block(heads_in, places, length, row_count, block_start):
    queries, keys, values = heads_in
    query_block = lax.dynamic_slice_in_dim(queries, block_start, row_count, 0)
    query_place = lax.dynamic_slice_in_dim(places, block_start, row_count, 0)
    scores = jnp.einsum(
        "qhd,khd->hqk", query_block, keys, preferred_element_type=jnp.float32
    ) * HEAD ** (-0.5)
    allowed = (places[None, :] <= query_place[:, None]) & (places[None, :] < length)
    scores = jnp.where(allowed[None], scores, NEG_FILL)
    row_max = jnp.max(scores, axis=-1, keepdims=True)
    exp_scores = jnp.exp(scores - row_max)
    denom_sum = jnp.sum(exp_scores, axis=-1, keepdims=True)
    probabilities = (exp_scores / denom_sum).astype(jnp.bfloat16)
    attended = jnp.einsum("hqk,khd->qhd", probabilities, values, preferred_element_type=jnp.float32)
    return (attended.astype(jnp.bfloat16), jnp.transpose((row_max + jnp.log(denom_sum))[..., 0]))


def attend_back(heads_in, grad_heads, log_sums, places, length, row_count, carried, block_start):
    queries, keys, values = heads_in
    grad_keys, grad_values = carried
    score_scale = HEAD ** (-0.5)
    query_block = lax.dynamic_slice_in_dim(queries, block_start, row_count, 0)
    query_place = lax.dynamic_slice_in_dim(places, block_start, row_count, 0)
    grad_block = lax.dynamic_slice_in_dim(grad_heads, block_start, row_count, 0)
    sums_block = jnp.transpose(lax.dynamic_slice_in_dim(log_sums, block_start, row_count, 0))[
        :, :, None
    ]
    scores = (
        jnp.einsum("qhd,khd->hqk", query_block, keys, preferred_element_type=jnp.float32)
        * score_scale
    )
    allowed = (places[None, :] <= query_place[:, None]) & (places[None, :] < length)
    probabilities = jnp.where(allowed[None], jnp.exp(scores - sums_block), 0.0)
    low_probs = probabilities.astype(jnp.bfloat16)
    grad_probs = jnp.einsum("qhd,khd->hqk", grad_block, values, preferred_element_type=jnp.float32)
    grad_values = grad_values + jnp.einsum(
        "hqk,qhd->khd", low_probs, grad_block, preferred_element_type=jnp.float32
    )
    inner = jnp.sum(probabilities * grad_probs, axis=-1, keepdims=True)
    grad_scores = (probabilities * (grad_probs - inner)).astype(jnp.bfloat16)
    grad_query = (
        jnp.einsum("hqk,khd->qhd", grad_scores, keys, preferred_element_type=jnp.float32)
        * score_scale
    )
    grad_keys = (
        grad_keys
        + jnp.einsum("hqk,qhd->khd", grad_scores, query_block, preferred_element_type=jnp.float32)
        * score_scale
    )
    return ((grad_keys, grad_values), grad_query)


def mixed_dot(form, left, right):
    return jnp.einsum(form, left, right, preferred_element_type=jnp.float32)


def expert_pass(rows, grad_result_rows, slot_weight, gate_up, down):
    half_width = down.shape[0]
    gate_up_out = mixed_dot("rd,df->rf", rows, gate_up)
    gate_part = gate_up_out[:, :half_width]
    up_part = gate_up_out[:, half_width:]
    sigmoid_gate = jax.nn.sigmoid(gate_part)
    hidden = (gate_part * sigmoid_gate * up_part).astype(jnp.bfloat16)
    result = mixed_dot("rf,fd->rd", hidden, down).astype(jnp.bfloat16)
    grad_result = (grad_result_rows.astype(jnp.float32) * slot_weight[:, None]).astype(jnp.bfloat16)
    grad_hidden = mixed_dot("rd,fd->rf", grad_result, down)
    grad_gate = grad_hidden * up_part * sigmoid_gate * (1.0 + gate_part * (1.0 - sigmoid_gate))
    grad_up = grad_hidden * gate_part * sigmoid_gate
    grad_mixed = jnp.concatenate([grad_gate, grad_up], -1).astype(jnp.bfloat16)
    grad_gate_up = mixed_dot("rd,rf->df", rows, grad_mixed).astype(jnp.bfloat16)
    grad_down = mixed_dot("rf,rd->fd", hidden, grad_result).astype(jnp.bfloat16)
    grad_rows = mixed_dot("rf,df->rd", grad_mixed, gate_up).astype(jnp.bfloat16)
    grad_slot = jnp.sum(
        result.astype(jnp.float32) * grad_result_rows.astype(jnp.float32), axis=-1
    )
    weighted = (result.astype(jnp.float32) * slot_weight[:, None]).astype(jnp.bfloat16)
    return (weighted, grad_slot, grad_rows, grad_gate_up, grad_down)


def sum_small(rows):
    fsdp_count = lax.axis_size("fsdp")
    pieces = rows.reshape(rows.shape[0], fsdp_count, -1)
    pieces = lax.all_to_all(pieces, "fsdp", split_axis=1, concat_axis=1, tiled=True)
    return jnp.sum(lax.all_gather(jnp.sum(pieces, axis=1), "seq", axis=0), axis=0)


def local(
    tokens,
    cotangent,
    lengths,
    experts,
    attn_gain,
    qkv_weight,
    q_gain,
    k_gain,
    out_weight,
    moe_gain,
    router_weight,
    gate_up_weight,
    down_weight,
):
    bf16, f32 = jnp.bfloat16, jnp.float32
    seq_count = lax.axis_size("seq")
    seq_rank = lax.axis_index("seq")
    own_tokens = tokens[0]
    tok_count, model_width = own_tokens.shape
    local_count = gate_up_weight.shape[0]
    experts_count = local_count * seq_count
    own_width = model_width // seq_count
    own_heads = own_width // HEAD
    key_span = seq_count * tok_count
    length = lengths[0]
    block_ranks = seq_rank ^ jnp.arange(seq_count, dtype=jnp.int32)
    places = (
        block_ranks[:, None] * tok_count + jnp.arange(tok_count, dtype=jnp.int32)[None, :]
    ).reshape(-1)
    valid_all = (places < length).reshape(seq_count, tok_count)
    keep_mask = valid_all[0].astype(f32)[:, None]

    own_qkv = lax.dynamic_index_in_dim(
        qkv_weight.reshape(-1, 3, seq_count, own_width), seq_rank, 2, False
    ).reshape(-1, 3 * own_width)
    qkv_own = lax.all_gather(own_qkv, "fsdp", axis=0, tiled=True)
    token_blocks = gather_blocks(own_tokens)
    small_rows = jnp.concatenate(
        [jnp.stack([attn_gain, q_gain, k_gain, moe_gain]), router_weight.T], axis=0
    )
    small_full = lax.all_gather(small_rows, "fsdp", axis=1, tiled=True)
    gain_one, gain_q, gain_k, gain_two = [small_full[i].astype(f32) for i in range(4)]
    router_rows = small_full[4:]
    gain_q = lax.dynamic_slice_in_dim(gain_q, seq_rank * own_width, own_width, 0)
    gain_k = lax.dynamic_slice_in_dim(gain_k, seq_rank * own_width, own_width, 0)
    out_cut = lax.dynamic_slice_in_dim(out_weight, seq_rank * own_width, own_width, 1)
    out_cut = lax.all_gather(out_cut, "fsdp", axis=0, tiled=True)
    out_full = in_rank_order([from_peer(out_cut, step) for step in range(seq_count)])
    weights = []
    for index in range(local_count):
        weights.append(
            (
                lax.all_gather(gate_up_weight[index], "fsdp", axis=0, tiled=True),
                lax.all_gather(down_weight[index], "fsdp", axis=0, tiled=True),
            )
        )
    id_blocks = gather_blocks(experts[0])
    cot_blocks = gather_blocks(cotangent[0])

    inputs_all = token_blocks.reshape(key_span, model_width).astype(f32)
    normed = (inputs_all * rms_scale(inputs_all) * gain_one).astype(bf16)
    projected = mixed_dot("td,de->te", normed, qkv_own)
    query_raw = projected[:, :own_width]
    key_raw = projected[:, own_width : 2 * own_width]
    value_raw = projected[:, 2 * own_width :]
    squares = jnp.stack([jnp.sum(query_raw * query_raw, -1), jnp.sum(key_raw * key_raw, -1)])

    def over_heads(parts):
        blocks = parts.reshape(2, seq_count, tok_count)
        total = blocks
        for step in range(1, seq_count):
            order = jnp.array([block ^ step for block in range(seq_count)])
            total = total + from_peer(blocks, step)[:, order]
        return total.reshape(2, key_span)

    scales = lax.rsqrt(over_heads(squares) / model_width + EPSILON)[:, :, None]
    unit_q = query_raw * scales[0]
    unit_k = key_raw * scales[1]
    cosine_table, sine_table = rope_tables(places.astype(f32))
    head_shape = (key_span, own_heads, HEAD)
    query_rot = rotate((unit_q * gain_q).reshape(head_shape), cosine_table, sine_table)
    key_rot = rotate((unit_k * gain_k).reshape(head_shape), cosine_table, sine_table)
    heads_in = (
        query_rot.astype(bf16),
        key_rot.astype(bf16),
        value_raw.reshape(head_shape).astype(bf16),
    )
    row_count = min(512, key_span)
    block_starts = jnp.arange(key_span // row_count, dtype=jnp.int32) * row_count
    attended_blocks, sums_blocks = lax.map(
        partial(attend_block, heads_in, places, length, row_count), block_starts
    )
    log_sums = sums_blocks.reshape(key_span, own_heads)
    attended_parts = return_blocks(attended_blocks.reshape(seq_count, tok_count, own_width))
    attended = jnp.transpose(in_rank_order(attended_parts), (1, 0, 2))

    inputs = own_tokens.astype(f32)
    branch = mixed_dot(
        "td,jdc->tjc", attended.reshape(tok_count, model_width), out_full
    ).reshape(tok_count, model_width)
    middle = inputs + branch * keep_mask
    scale_two = rms_scale(middle)
    unit_two = middle * scale_two
    normed_two = (unit_two * gain_two).astype(bf16)

    row_blocks = gather_blocks(normed_two)
    logits = mixed_dot("btd,ed->bte", row_blocks, router_rows)
    expert_range = jnp.arange(experts_count, dtype=jnp.int32)
    named = jnp.any(id_blocks[..., None] == expert_range, axis=2)
    chosen = jnp.where(named, logits, NEG_FILL)
    exp_chosen = jnp.where(named, jnp.exp(chosen - jnp.max(chosen, -1, keepdims=True)), 0.0)
    gates = exp_chosen / jnp.sum(exp_chosen, axis=-1, keepdims=True)
    routed = (named & valid_all[..., None]).astype(jnp.int32)
    before = jnp.cumsum(routed, axis=1) - routed
    local_routed = lax.dynamic_slice_in_dim(routed, seq_rank * local_count, local_count, 2)
    local_before = lax.dynamic_slice_in_dim(before, seq_rank * local_count, local_count, 2)
    local_gates = lax.dynamic_slice_in_dim(gates, seq_rank * local_count, local_count, 2)
    slots = round_up(CAP, 16)
    slot_place = jnp.where(local_routed == 1, local_before, -1)
    slot_place = jnp.transpose(slot_place, (2, 0, 1))
    local_gates = jnp.transpose(local_gates, (2, 0, 1))
    slot_hit = slot_place[:, :, None, :] == jnp.arange(slots, dtype=jnp.int32)[:, None]
    slot_pick = slot_hit.astype(bf16)
    slot_gates = jnp.sum(jnp.where(slot_hit, local_gates[:, :, None, :], 0.0), axis=-1)

    weighted_rows, grad_row_sets, grad_slots, gate_up_sums, down_sums = [], [], [], [], []
    for index in range(local_count):
        pick = slot_pick[index]
        rows = mixed_dot("bct,btd->bcd", pick, row_blocks).astype(bf16)
        grad_source = mixed_dot("bct,btd->bcd", pick, cot_blocks).astype(bf16)
        weighted, grad_slot, grad_rows, grad_gate_up, grad_down = expert_pass(
            rows.reshape(seq_count * slots, model_width),
            grad_source.reshape(seq_count * slots, model_width),
            slot_gates[index].reshape(-1),
            *weights[index],
        )
        weighted_rows.append(weighted.reshape(seq_count, slots, model_width))
        grad_row_sets.append(grad_rows.reshape(seq_count, slots, model_width))
        grad_slots.append(
            jnp.sum(
                jnp.where(slot_hit[index], grad_slot.reshape(seq_count, slots)[:, :, None], 0.0), 1
            )
        )
        gate_up_sums.append(lax.psum_scatter(grad_gate_up, "fsdp", scatter_dimension=0, tiled=True))
        down_sums.append(lax.psum_scatter(grad_down, "fsdp", scatter_dimension=0, tiled=True))
    pick_all = jnp.concatenate([slot_pick[index] for index in range(local_count)], axis=1)
    grad_partial = mixed_dot("bct,bcd->btd", pick_all, jnp.concatenate(grad_row_sets, axis=1))
    grad_back = return_blocks(grad_partial.astype(bf16))
    grad_gates = in_rank_order(return_blocks(jnp.stack(grad_slots, axis=1)))
    moe_partial = mixed_dot("bct,bcd->btd", pick_all, jnp.concatenate(weighted_rows, axis=1))
    moe_parts = return_blocks(moe_partial.astype(bf16))
    moe_sum = sum(part.astype(f32) for part in moe_parts)
    block_out = (middle + moe_sum).astype(bf16)

    own_gates = gates[0]
    grad_gates = jnp.transpose(grad_gates, (2, 0, 1)).reshape(tok_count, experts_count)
    grad_logits = own_gates * (
        grad_gates - jnp.sum(own_gates * grad_gates, axis=-1, keepdims=True)
    )
    grad_out = cotangent[0].astype(f32) * keep_mask
    grad_normed_two = jnp.einsum(
        "te,ed->td", grad_logits, router_rows.astype(f32), precision=lax.Precision.HIGHEST
    ) + sum(part.astype(f32) for part in grad_back)
    grad_router = jnp.einsum(
        "te,td->ed", grad_logits, normed_two.astype(f32), precision=lax.Precision.HIGHEST
    )
    grad_middle_norm, grad_two = norm_back(grad_normed_two, unit_two, scale_two, gain_two)
    grad_middle = grad_out + grad_middle_norm
    grad_branch = (grad_middle * keep_mask).astype(bf16)
    grad_attended = mixed_dot(
        "tjc,jdc->td", grad_branch.reshape(tok_count, seq_count, own_width), out_full
    ).astype(bf16)
    grad_cut = mixed_dot("td,tc->dc", attended.reshape(tok_count, model_width), grad_branch)
    grad_cut = grad_cut.astype(bf16).reshape(model_width, seq_count, own_width)
    grad_cut = [
        from_peer(lax.dynamic_index_in_dim(grad_cut, seq_rank ^ step, 1, False), step)
        for step in range(seq_count)
    ]
    grad_cut = sum(part.astype(f32) for part in grad_cut).astype(bf16)

    cut_heads = grad_attended.reshape(tok_count, seq_count, own_width)
    grad_heads = jnp.stack(
        [
            from_peer(lax.dynamic_index_in_dim(cut_heads, seq_rank ^ step, 1, False), step)
            for step in range(seq_count)
        ]
    ).reshape(head_shape)
    zero_heads = jnp.zeros(head_shape, f32)
    (grad_keys, grad_values), grad_queries = lax.scan(
        partial(attend_back, heads_in, grad_heads, log_sums, places, length, row_count),
        (zero_heads, zero_heads),
        block_starts,
    )
    low = lambda rows: rows.reshape(head_shape).astype(bf16).astype(f32)
    grad_qn = rotate_back(low(grad_queries), cosine_table, sine_table).reshape(key_span, own_width)
    grad_kn = rotate_back(low(grad_keys), cosine_table, sine_table).reshape(key_span, own_width)
    scaled_q = grad_qn * gain_q
    scaled_k = grad_kn * gain_k
    inners = over_heads(
        jnp.stack([jnp.sum(scaled_q * unit_q, -1), jnp.sum(scaled_k * unit_k, -1)])
    )
    inners = (inners / model_width)[:, :, None]
    grad_projected = jnp.concatenate(
        [
            scales[0] * (scaled_q - unit_q * inners[0]),
            scales[1] * (scaled_k - unit_k * inners[1]),
            grad_values.reshape(key_span, own_width),
        ],
        axis=1,
    ).astype(bf16)
    grad_qkv = mixed_dot("td,te->de", normed, grad_projected).astype(bf16)
    grad_normed = mixed_dot("te,de->td", grad_projected, qkv_own).astype(bf16)
    grad_normed = sum(
        part.astype(f32)
        for part in return_blocks(grad_normed.reshape(seq_count, tok_count, model_width))
    )
    scale_one = rms_scale(inputs)
    grad_inputs_norm, grad_one = norm_back(grad_normed, inputs * scale_one, scale_one, gain_one)
    grad_tokens = (grad_middle + grad_inputs_norm).astype(bf16)

    qkv_sum = lax.psum_scatter(grad_qkv, "fsdp", scatter_dimension=0, tiled=True)
    qkv_sum = in_rank_order([from_peer(qkv_sum, step) for step in range(seq_count)])
    qkv_sum = jnp.transpose(
        qkv_sum.reshape(seq_count, -1, 3, own_width), (1, 2, 0, 3)
    ).reshape(-1, 3 * model_width)
    out_sum = lax.psum_scatter(grad_cut, "fsdp", scatter_dimension=0, tiled=True)
    out_sum = in_rank_order([from_peer(out_sum, step) for step in range(seq_count)])
    out_sum = jnp.transpose(out_sum, (1, 0, 2)).reshape(-1, model_width)
    early = sum_small(jnp.concatenate([grad_router, grad_two[None]], axis=0))
    placed = lambda row: lax.dynamic_update_slice(
        jnp.zeros((model_width,), f32), row, (seq_rank * own_width,)
    )
    late = sum_small(
        jnp.stack(
            [
                grad_one,
                placed(jnp.sum(grad_qn * unit_q, axis=0)),
                placed(jnp.sum(grad_kn * unit_k, axis=0)),
            ]
        )
    )
    return (
        block_out[None],
        grad_tokens[None],
        late[0],
        qkv_sum.astype(f32),
        late[1],
        late[2],
        out_sum.astype(f32),
        early[experts_count],
        early[:experts_count].T,
        jnp.stack(gate_up_sums).astype(f32),
        jnp.stack(down_sums).astype(f32),
    )


def solution(mesh):
    in_specs = (
        P("fsdp", "seq", None),
        P("fsdp", "seq", None),
        P("fsdp"),
        P("fsdp", "seq", None),
        P("fsdp"),
        P("fsdp", None),
        P("fsdp"),
        P("fsdp"),
        P("fsdp", None),
        P("fsdp"),
        P("fsdp", None),
        P("seq", "fsdp", None),
        P("seq", "fsdp", None),
    )
    out_specs = (
        P("fsdp", "seq", None),
        P("fsdp", "seq", None),
        P("fsdp"),
        P("fsdp", None),
        P("fsdp"),
        P("fsdp"),
        P("fsdp", None),
        P("fsdp"),
        P("fsdp", None),
        P("seq", "fsdp", None),
        P("seq", "fsdp", None),
    )
    return jax.shard_map(local, mesh=mesh, in_specs=in_specs, out_specs=out_specs, check_vma=False)
```

time: 2530 us -> 1570 us (0.62)
  waiting for transfers between devices: 1630 us -> 866 us
  local copies, waits for them, and re-layouts: 272 us -> 129 us
  blocking collectives: 142 us -> 52.5 us
  matrix products: 298 us -> 340 us
  other arithmetic: 118 us -> 83.6 us
  starting transfers between devices: 36.4 us -> 69.6 us
    all_to_all x7 -> x2, waiting for transfers between devices: 373 us -> 13 us  [sum_small(): lax.all_to_all(pieces, 'fsdp', split_axis=1, concat_axis=1, tiled=True)]
    all_gather x4 -> x10, waiting for transfers between devices: 451 us -> 148 us  [the longest x4 103 us: local(): lax.all_gather(down_weight[index], 'fsdp', axis=0, tiled=True)]
    ppermute x0 -> x48, waiting for transfers between devices: none -> 280 us  [from_peer(): lax.ppermute(values, 'seq', [(rank, rank ^ step) for rank in range(count)])]
    reduce_scatter x5 -> x10, waiting for transfers between devices: 697 us -> 421 us  [the longest x4 335 us: local(): lax.psum_scatter(grad_gate_up, 'fsdp', scatter_dimension=0, tiled=True)]
    psum x1 -> x0, waiting for transfers between devices: 102 us -> none  [local(): lax.psum(param_parts[5].astype(jnp.bfloat16), 'seq').astype(jnp.float32)]
    gather x10 -> x6, local copies, waits for them, and re-layouts: 96.8 us -> 3.8 us  [over_heads(): total = total + from_peer(blocks, step)[:, order]]
    while x44 -> x65, local copies, waits for them, and re-layouts: 72.3 us -> 8.49 us  [the longest x1 29.5 us: local(): lax.scan(back_step, None, (back_weights[0], back_weights[1], expert_rows,...]
    ppermute x0 -> x48, starting transfers between devices: none -> 61.1 us  [from_peer(): lax.ppermute(values, 'seq', [(rank, rank ^ step) for rank in range(count)])]
  transfers between devices with their start and end apart: 17 -> 70, of which waited for: 13 -> 32; matrix products, arithmetic and copies ran while one was open for 10% -> 30% of each run, Pallas kernels for 0% -> 0%
where the time goes in v1:
time: 1570 us
  waiting for transfers between devices  866 us (55%)
  matrix products  340 us (22%)
  local copies, waits for them, and re-layouts  129 us (8%)
  other arithmetic  83.6 us (5%)
  starting transfers between devices  69.6 us (4%)
  blocking collectives  52.5 us (3%)
  between operations  17.2 us (1%)
    reduce_scatter x4, waiting for transfers between devices, local(): lax.psum_scatter(grad_gate_up, 'fsdp', scatter_dimension=0, tiled=True)  335 us
    dot_general x40, matrix products, mixed_dot(): return jnp.einsum(form, left, right, preferred_element_type=jnp.float32)  294 us
    ppermute x48, waiting for transfers between devices, from_peer(): lax.ppermute(values, 'seq', [(rank, rank ^ step) for rank in range(count)])  280 us
    all_gather x4, waiting for transfers between devices, local(): lax.all_gather(down_weight[index], 'fsdp', axis=0, tiled=True)  103 us
    reduce_scatter x4, waiting for transfers between devices, local(): lax.psum_scatter(grad_down, 'fsdp', scatter_dimension=0, tiled=True)  86.7 us
    ppermute x48, starting transfers between devices, from_peer(): lax.ppermute(values, 'seq', [(rank, rank ^ step) for rank in range(count)])  61.1 us
    all_gather x4, waiting for transfers between devices, local(): lax.all_gather(gate_up_weight[index], 'fsdp', axis=0, tiled=True)  45.5 us
    unnamed x289, local copies, waits for them, and re-layouts  40.4 us
  transfers between devices with their start and end apart: 70, of which 32 were waited for; matrix products, arithmetic and copies ran while one was open for 30% of the time, Pallas kernels for 0%

profile of v1, /device:TPU:0, one launch (start us, length us, event | category | flops | bytes accessed | tf_op | source)
XLA Modules:
  0.0 1566.7 jit_solution(14907921530102275856)
XLA Ops:
  35.6 14.4 all_gather.45
  56.5 41.9 %collective-permute-done.13 = s32[256,8]{0,1:T(8,128)S(1)} collective-permute-done((s32[256,8]{0,1:T(8,128)S(1)}, s32[256,8]{0,1:T(8,128)S(1)}, u32[]{:S(2)}, u32[]{:S(2)}) %collective-permute-start.13) | collective-permute-done | bytes 8224 | tf_op jit(solution)/shard_map/ppermute | solution.py:61
  107.4 16.5 %collective-permute-done.22 = bf16[256,2048]{1,0:T(8,128)(2,1)} collective-permute-done((bf16[256,2048]{1,0:T(8,128)(2,1)}, bf16[256,2048]{1,0:T(8,128)(2,1)}, u32[]{:S(2)}, u32[]{:S(2)}) %collective-permute-start.22) | collective-permute-done | bytes 1048608 | tf_op jit(solution)/shard_map/ppermute | solution.py:61
  134.8 12.9 collective-permute-done
  169.0 29.5 %collective-permute-done.9 = bf16[2048,512]{0,1:T(8,128)(2,1)S(1)} collective-permute-done((bf16[2048,512]{0,1:T(8,128)(2,1)}, bf16[2048,512]{0,1:T(8,128)(2,1)S(1)}, u32[]{:S(2)}, u32[]{:S(2)}) %collective-permute-start.9) | collective-permute-done | bytes 2097184 | tf_op jit(solution)/shard_map/ppermute | solution.py:61
  200.0 46.2 %collective-permute-done.10 = bf16[2048,512]{0,1:T(8,128)(2,1)S(1)} collective-permute-done((bf16[2048,512]{0,1:T(8,128)(2,1)}, bf16[2048,512]{0,1:T(8,128)(2,1)S(1)}, u32[]{:S(2)}, u32[]{:S(2)}) %collective-permute-start.10) | collective-permute-done | bytes 2097184 | tf_op jit(solution)/shard_map/ppermute | solution.py:61
  247.7 10.3 fusion.231
  272.1 25.2 %while.28 = (s32[]{:T(128)}, bf16[2,512,4,128]{3,2,1,0:T(4,128)(2,1)}, f32[2,512,4]{1,2,0:T(4,128)S(1)}, s32[2]{0:T(128)S(1)}, s32[1024]{0:T(1024)S(1)}, /*index...) while((s32[]{:T(128)}, ...), condition=%wide.region_6.7_spmd.clone, body=%wide.region_3.6_spmd.clone.sunk | while | flops 1100218368 | bytes 39940364 | solution.py:257
  317.4 6.4 multiply_reduce_fusion.7
  332.2 18.9 %collective-permute-done.17 = bf16[256,2048]{1,0:T(8,128)(2,1)S(1)} collective-permute-done((bf16[256,2048]{1,0:T(8,128)(2,1)S(1)}, bf16[256,2048]{1,0:T(8,128)(2,1)S(1)}, u32[]{:S(2)}, u32[]{:S(2)}) %collective-permute-start.17) | collective-permute-done | bytes 1048608 | tf_op jit(solution)/shard_map/ppermute | solution.py:61
  351.1 16.7 %collective-permute-done.16 = bf16[256,2048]{1,0:T(8,128)(2,1)S(1)} collective-permute-done((bf16[256,2048]{1,0:T(8,128)(2,1)S(1)}, bf16[256,2048]{1,0:T(8,128)(2,1)S(1)}, u32[]{:S(2)}, u32[]{:S(2)}) %collective-permute-start.16) | collective-permute-done | bytes 1048608 | tf_op jit(solution)/shard_map/ppermute | solution.py:61
  383.3 9.6 fusion.54
  393.0 9.9 fusion.58
  402.9 10.1 fusion.62
  412.9 9.7 multiply_convert_fusion.2
  422.7 27.2 %all-gather.37.cloned.1.call-done = bf16[1,1024,2048]{2,1,0:T(8,128)(2,1)} async-done(((bf16[1,128,2048]{2,1,0:T(8,128)(2,1)}), bf16[1,1024,2048]{2,1,0:T(8,128)(2,1)}) %all-gather.37.cloned.1.call-update) | async-done | bytes 4194320 | tf_op jit(solution)/shard_map/all_gather | solution.py:221
  449.9 8.0 multiply_convert_fusion.4
  457.9 39.3 %all-gather.33.cloned.1.call-done = bf16[1,1024,2048]{2,1,0:T(8,128)(2,1)} async-done(((bf16[1,128,2048]{2,1,0:T(8,128)(2,1)}), bf16[1,1024,2048]{2,1,0:T(8,128)(2,1)}) %all-gather.33.cloned.1.call-update) | async-done | bytes 4194320 | tf_op jit(solution)/shard_map/all_gather | solution.py:221
  497.2 8.9 multiply_convert_fusion.6
  506.2 11.3 fusion.116
  517.5 10.3 fusion.113
  527.9 6.4 fusion.110
  534.3 45.5 %all-gather.27.cloned.1.call-done = bf16[1,2048,2048]{2,1,0:T(8,128)(2,1)} async-done(((bf16[1,256,2048]{2,1,0:T(8,128)(2,1)}), bf16[1,2048,2048]{2,1,0:T(8,128)(2,1)}) %all-gather.27.cloned.1.call-update) | async-done | bytes 8388624 | tf_op jit(solution)/shard_map/all_gather | solution.py:220
  579.7 10.4 fusion.66
  590.1 36.4 %all-gather.29.cloned.1.call-done = bf16[1,1024,2048]{2,1,0:T(8,128)(2,1)} async-done(((bf16[1,128,2048]{2,1,0:T(8,128)(2,1)}), bf16[1,1024,2048]{2,1,0:T(8,128)(2,1)}) %all-gather.29.cloned.1.call-update) | async-done | bytes 4194320 | tf_op jit(solution)/shard_map/all_gather | solution.py:221
  626.5 8.0 multiply_convert_fusion.8
  634.6 6.4 fusion.107
  641.0 6.2 fusion.101
  658.8 7.1 fusion.80
  665.9 7.5 fusion.78
  673.5 7.1 fusion.76
  684.3 6.3 fusion.104
  693.5 6.5 collective-permute-done.24
  706.7 4.8 multiply_reduce_fusion.2
  711.6 17.2 %collective-permute-done.20 = bf16[256,2048]{1,0:T(8,128)(2,1)} collective-permute-done((bf16[256,2048]{1,0:T(8,128)(2,1)}, bf16[256,2048]{1,0:T(8,128)(2,1)}, u32[]{:S(2)}, u32[]{:S(2)}) %collective-permute-start.20) | collective-permute-done | bytes 1048608 | tf_op jit(solution)/shard_map/ppermute | solution.py:61
  728.8 20.7 %collective-permute-done.19 = bf16[256,2048]{1,0:T(8,128)(2,1)} collective-permute-done((bf16[256,2048]{1,0:T(8,128)(2,1)}, bf16[256,2048]{1,0:T(8,128)(2,1)}, u32[]{:S(2)}, u32[]{:S(2)}) %collective-permute-start.19) | collective-permute-done | bytes 1048608 | tf_op jit(solution)/shard_map/ppermute | solution.py:61
  749.4 5.7 multiply_convert_fusion.15
  755.1 5.8 convolution_convert_fusion.4
  760.9 5.7 fusion.134
  773.5 5.7 dynamic-slice_bitcast_fusion.3
  789.2 49.4 %while.29 = (s32[]{:T(128)}, f32[1024,4,128]{0,2,1:T(8,128)S(1)}, f32[1024,4,128]{0,2,1:T(8,128)}, bf16[2,512,4,128]{3,1,0,2:T(8,128)(2,1)}, s32[2]{0:T(128)S(1)...) while((s32[]{:T(128)}, f32[1024,4,128]{0,2,1:T(8,128)S(1)}, ...), condition=%wide.region_27.28_spmd.clone, body=%wide.region_25.27_spmd.clone.sunk | while | flops 2719744000 | bytes 206656144 | solution.py:356
  842.7 31.8 %collective-permute-done.43 = bf16[2048,512]{0,1:T(8,128)(2,1)} collective-permute-done((bf16[2048,512]{0,1:T(8,128)(2,1)}, bf16[2048,512]{0,1:T(8,128)(2,1)}, u32[]{:S(2)}, u32[]{:S(2)}) %collective-permute-start.43) | collective-permute-done | bytes 2097184 | tf_op jit(solution)/shard_map/ppermute | solution.py:61
  874.5 6.8 fusion.84
  906.7 9.3 convolution_convert_fusion.5
  917.3 6.8 convolution_convert_fusion.7
  925.4 6.9 convolution_convert_fusion.8
  933.6 6.9 convolution_convert_fusion.9
  941.8 6.9 convolution_convert_fusion.10
  950.0 10.8 convolution_convert_fusion
  962.1 10.8 convolution_convert_fusion.1
  974.3 10.7 convolution_convert_fusion.2
  986.3 10.8 convolution_convert_fusion.3
  999.5 10.3 convolution_convert_fusion.6
  1022.2 11.4 all-to-all-done.1
  1033.7 30.2 %all-gather.11 = f32[4,17,256]{2,1,0:T(8,128)S(1)} all-gather(f32[1,17,256]{2,1,0:T(8,128)S(1)} %bitcast.599), channel_id=11, replica_groups=mesh['seq'=4,'fsdp'=8] {'seq'}, dimensions={0}, use_global_device_ids=true | all-gather | bytes 87040 | tf_op jit(solution)/shard_map/all_gather | solution.py:164
  1078.7 8.0 all-gather.10
  1106.3 36.1 %reduce-scatter.25.cloned.1.call-done = bf16[128,2048]{1,0:T(8,128)(2,1)} async-done(((bf16[1024,2048]{1,0:T(8,128)(2,1)}), bf16[128,2048]{1,0:T(8,128)(2,1)}) %reduce-scatter.25.cloned.1.call-update) | async-done | bytes 524304 | tf_op jit(solution)/shard_map/reduce_scatter | solution.py:312
  1142.3 50.6 %reduce-scatter.23.cloned.1.call-done = bf16[128,2048]{1,0:T(8,128)(2,1)} async-done(((bf16[1024,2048]{1,0:T(8,128)(2,1)}), bf16[128,2048]{1,0:T(8,128)(2,1)}) %reduce-scatter.23.cloned.1.call-update) | async-done | bytes 524304 | tf_op jit(solution)/shard_map/reduce_scatter | solution.py:312
  1213.1 6.6 copy.287
  1219.7 63.9 %reduce-scatter.21.cloned.1.call-done = bf16[256,2048]{1,0:T(8,128)(2,1)} async-done(((bf16[2048,2048]{1,0:T(8,128)(2,1)}), bf16[256,2048]{1,0:T(8,128)(2,1)}) %reduce-scatter.21.cloned.1.call-update) | async-done | bytes 1048592 | tf_op jit(solution)/shard_map/reduce_scatter | solution.py:311
  1283.7 90.2 %reduce-scatter.19.cloned.1.call-done = bf16[256,2048]{1,0:T(8,128)(2,1)} async-done(((bf16[2048,2048]{1,0:T(8,128)(2,1)}), bf16[256,2048]{1,0:T(8,128)(2,1)}) %reduce-scatter.19.cloned.1.call-update) | async-done | bytes 1048592 | tf_op jit(solution)/shard_map/reduce_scatter | solution.py:311
  1373.8 90.3 %reduce-scatter.17.cloned.1.call-done = bf16[256,2048]{1,0:T(8,128)(2,1)} async-done(((bf16[2048,2048]{1,0:T(8,128)(2,1)}), bf16[256,2048]{1,0:T(8,128)(2,1)}) %reduce-scatter.17.cloned.1.call-update) | async-done | bytes 1048592 | tf_op jit(solution)/shard_map/reduce_scatter | solution.py:311
  1464.1 90.2 %reduce-scatter.15.cloned.1.call-done = bf16[256,2048]{1,0:T(8,128)(2,1)} async-done(((bf16[2048,2048]{1,0:T(8,128)(2,1)}), bf16[256,2048]{1,0:T(8,128)(2,1)}) %reduce-scatter.15.cloned.1.call-update) | async-done | bytes 1048592 | tf_op jit(solution)/shard_map/reduce_scatter | solution.py:311
  1554.3 5.3 maximum_convert_fusion.1
  (718 shorter events, 351.9 us)
Async XLA Ops:
  7.2 142.5 %all-gather.25.cloned.1.call-start = ((), (), s32[]{:S(2)}) async-start(), calls=%async_computation.13 | async-start | bytes 2359296 | tf_op jit(solution)/shard_map/all_gather | solution.py:214
  9.3 238.4 %all-gather.23.cloned.1.call-start = ((), (), s32[]{:S(2)}) async-start(), calls=%async_computation.12 | async-start | bytes 7077888 | tf_op jit(solution)/shard_map/all_gather | solution.py:203
  16.1 367.3 %all-gather.39.cloned.1.call-start = ((), (), s32[]{:S(2)}) async-start(), calls=%async_computation.30 | async-start | bytes 9437184 | tf_op jit(solution)/shard_map/all_gather | solution.py:220
  20.6 372.4 %all-gather.35.cloned.1.call-start = ((), (), s32[]{:S(2)}) async-start(), calls=%async_computation.28 | async-start | bytes 9437184 | tf_op jit(solution)/shard_map/all_gather | solution.py:220
  21.1 381.7 %all-gather.31.cloned.1.call-start = ((), (), s32[]{:S(2)}) async-start(), calls=%async_computation.26 | async-start | bytes 9437184 | tf_op jit(solution)/shard_map/all_gather | solution.py:220
  21.7 391.2 %all-gather.41.cloned.1.call-start = ((), (), s32[]{:S(2)}) async-start(), calls=%async_computation.31 | async-start | bytes 4718592 | tf_op jit(solution)/shard_map/all_gather | solution.py:221
  23.7 426.2 %all-gather.37.cloned.1.call-start = ((), (), s32[]{:S(2)}) async-start(), calls=%async_computation.29 | async-start | bytes 4718592 | tf_op jit(solution)/shard_map/all_gather | solution.py:221
  24.5 472.8 %all-gather.33.cloned.1.call-start = ((), (), s32[]{:S(2)}) async-start(), calls=%async_computation.27 | async-start | bytes 4718592 | tf_op jit(solution)/shard_map/all_gather | solution.py:221
  25.2 554.5 %all-gather.27.cloned.1.call-start = ((), (), s32[]{:S(2)}) async-start(), calls=%async_computation.24 | async-start | bytes 9437184 | tf_op jit(solution)/shard_map/all_gather | solution.py:220
  26.0 600.6 %all-gather.29.cloned.1.call-start = ((), (), s32[]{:S(2)}) async-start(), calls=%async_computation.25 | async-start | bytes 4718592 | tf_op jit(solution)/shard_map/all_gather | solution.py:221
  26.0 108.8 %collective-permute-start.2 = (bf16[256,2048]{1,0:T(8,128)(2,1)S(1)}, bf16[256,2048]{1,0:T(8,128)(2,1)S(1)}, u32[]{:S(2)}, u32[]{:S(2)}) collective-permute-start(bf16[256,2048]{1,0:T(8,128)(2,1)S(1)} %bitcast.539), channel_id=1, source_target_pairs={{0,24},{8,16},{16,8},{24,0},{1,25},{9,17},{17,9},{25,1},{2,26},{10... | collective-permute-start | bytes 3145736 | tf_op jit(solution)/shard_map/ppermute | solution.py:61
  30.0 104.8 %collective-permute-start.1 = (bf16[256,2048]{1,0:T(8,128)(2,1)S(1)}, bf16[256,2048]{1,0:T(8,128)(2,1)S(1)}, u32[]{:S(2)}, u32[]{:S(2)}) collective-permute-start(bf16[256,2048]{1,0:T(8,128)(2,1)S(1)} %bitcast.540), channel_id=1, source_target_pairs={{0,16},{8,24},{16,0},{24,8},{1,17},{9,25},{17,1},{25,9},{2,18},{10... | collective-permute-start | bytes 3145736 | tf_op jit(solution)/shard_map/ppermute | solution.py:61
  30.5 23.7 %collective-permute-start.14 = (s32[256,8]{0,1:T(8,128)S(1)}, s32[256,8]{0,1:T(8,128)S(1)}, u32[]{:S(2)}, u32[]{:S(2)}) collective-permute-start(s32[256,8]{0,1:T(8,128)S(1)} %bitcast.635), channel_id=1, source_target_pairs={{0,24},{8,16},{16,8},{24,0},{1,25},{9,17},{17,9},{25,1},{2,26},{10... | collective-permute-start | bytes 24584 | tf_op jit(solution)/shard_map/ppermute | solution.py:61
  32.0 66.4 %collective-permute-start.13 = (s32[256,8]{0,1:T(8,128)S(1)}, s32[256,8]{0,1:T(8,128)S(1)}, u32[]{:S(2)}, u32[]{:S(2)}) collective-permute-start(s32[256,8]{0,1:T(8,128)S(1)} %bitcast.636), channel_id=1, source_target_pairs={{0,16},{8,24},{16,0},{24,8},{1,17},{9,25},{17,1},{25,9},{2,18},{10... | collective-permute-start | bytes 24584 | tf_op jit(solution)/shard_map/ppermute | solution.py:61
  32.1 68.0 %collective-permute-start.12 = (s32[256,8]{0,1:T(8,128)S(1)}, s32[256,8]{0,1:T(8,128)S(1)}, u32[]{:S(2)}, u32[]{:S(2)}) collective-permute-start(s32[256,8]{0,1:T(8,128)S(1)} %bitcast.637), channel_id=1, source_target_pairs={{0,8},{8,0},{16,24},{24,16},{1,9},{9,1},{17,25},{25,17},{2,10},{10... | collective-permute-start | bytes 24584 | tf_op jit(solution)/shard_map/ppermute | solution.py:61
  34.0 1052.7 %reduce-scatter.13.cloned.1.call-start = ((), (), s32[]{:S(2)}) async-start(), calls=%async_computation.15 | async-start | bytes 2359296 | tf_op jit(solution)/shard_map/reduce_scatter | solution.py:393
  54.2 50.8 %collective-permute-start.23 = (bf16[256,2048]{1,0:T(8,128)(2,1)}, bf16[256,2048]{1,0:T(8,128)(2,1)}, u32[]{:S(2)}, u32[]{:S(2)}) collective-permute-start(bf16[256,2048]{1,0:T(8,128)(2,1)} %bitcast.566), channel_id=1, source_target_pairs={{0,24},{8,16},{16,8},{24,0},{1,25},{9,17},{17,9},{25,1},{2,26},{10... | collective-permute-start | bytes 3145736 | tf_op jit(solution)/shard_map/ppermute | solution.py:61
  98.4 25.5 %collective-permute-start.22 = (bf16[256,2048]{1,0:T(8,128)(2,1)}, bf16[256,2048]{1,0:T(8,128)(2,1)}, u32[]{:S(2)}, u32[]{:S(2)}) collective-permute-start(bf16[256,2048]{1,0:T(8,128)(2,1)} %bitcast.567), channel_id=1, source_target_pairs={{0,16},{8,24},{16,0},{24,8},{1,17},{9,25},{17,1},{25,9},{2,18},{10... | collective-permute-start | bytes 3145736 | tf_op jit(solution)/shard_map/ppermute | solution.py:61
  100.1 26.3 %collective-permute-start.21 = (bf16[256,2048]{1,0:T(8,128)(2,1)}, bf16[256,2048]{1,0:T(8,128)(2,1)}, u32[]{:S(2)}, u32[]{:S(2)}) collective-permute-start(bf16[256,2048]{1,0:T(8,128)(2,1)} %bitcast.568), channel_id=1, source_target_pairs={{0,8},{8,0},{16,24},{24,16},{1,9},{9,1},{17,25},{25,17},{2,10},{10... | collective-permute-start | bytes 3145736 | tf_op jit(solution)/shard_map/ppermute | solution.py:61
  105.0 42.8 %collective-permute-start = (bf16[256,2048]{1,0:T(8,128)(2,1)S(1)}, bf16[256,2048]{1,0:T(8,128)(2,1)S(1)}, u32[]{:S(2)}, u32[]{:S(2)}) collective-permute-start(bf16[256,2048]{1,0:T(8,128)(2,1)S(1)} %bitcast.541), channel_id=1, source_target_pairs={{0,8},{8,0},{16,24},{24,16},{1,9},{9,1},{17,25},{25,17},{2,10},{10... | collective-permute-start | bytes 3145736 | tf_op jit(solution)/shard_map/ppermute | solution.py:61
  149.7 48.8 %collective-permute-start.9 = (bf16[2048,512]{0,1:T(8,128)(2,1)}, bf16[2048,512]{0,1:T(8,128)(2,1)S(1)}, u32[]{:S(2)}, u32[]{:S(2)}) collective-permute-start(bf16[2048,512]{0,1:T(8,128)(2,1)} %all-gather.25.cloned.1.call-done), channel_id=1, source_target_pairs={{0,8},{8,0},{16,24},{24,16},{1,9},{9,1},{17,25},{25,17},{2,10},{10... | collective-permute-start | bytes 6291464 | tf_op jit(solution)/shard_map/ppermute | solution.py:61
  154.7 91.5 %collective-permute-start.10 = (bf16[2048,512]{0,1:T(8,128)(2,1)}, bf16[2048,512]{0,1:T(8,128)(2,1)S(1)}, u32[]{:S(2)}, u32[]{:S(2)}) collective-permute-start(bf16[2048,512]{0,1:T(8,128)(2,1)} %all-gather.25.cloned.1.call-done), channel_id=1, source_target_pairs={{0,16},{8,24},{16,0},{24,8},{1,17},{9,25},{17,1},{25,9},{2,18},{10... | collective-permute-start | bytes 6291464 | tf_op jit(solution)/shard_map/ppermute | solution.py:61
  159.9 146.8 %collective-permute-start.11 = (bf16[2048,512]{0,1:T(8,128)(2,1)}, bf16[2048,512]{0,1:T(8,128)(2,1)}, u32[]{:S(2)}, u32[]{:S(2)}) collective-permute-start(bf16[2048,512]{0,1:T(8,128)(2,1)} %all-gather.25.cloned.1.call-done), channel_id=1, source_target_pairs={{0,24},{8,16},{16,8},{24,0},{1,25},{9,17},{17,9},{25,1},{2,26},{10... | collective-permute-start | bytes 6291464 | tf_op jit(solution)/shard_map/ppermute | solution.py:61
  303.2 8.2 collective-permute-start.6
  303.8 11.3 collective-permute-start.7
  305.1 11.0 collective-permute-start.8
  324.2 27.0 %collective-permute-start.17 = (bf16[256,2048]{1,0:T(8,128)(2,1)S(1)}, bf16[256,2048]{1,0:T(8,128)(2,1)S(1)}, u32[]{:S(2)}, u32[]{:S(2)}) collective-permute-start(bf16[256,2048]{1,0:T(8,128)(2,1)S(1)} %multiply_convert_fusion.16), channel_id=1, source_target_pairs={{0,24},{8,16},{16,8},{24,0},{1,25},{9,17},{17,9},{25,1},{2,26},{10... | collective-permute-start | bytes 3145736 | tf_op jit(solution)/shard_map/ppermute | solution.py:61
  325.7 42.1 %collective-permute-start.16 = (bf16[256,2048]{1,0:T(8,128)(2,1)S(1)}, bf16[256,2048]{1,0:T(8,128)(2,1)S(1)}, u32[]{:S(2)}, u32[]{:S(2)}) collective-permute-start(bf16[256,2048]{1,0:T(8,128)(2,1)S(1)} %multiply_convert_fusion.16), channel_id=1, source_target_pairs={{0,16},{8,24},{16,0},{24,8},{1,17},{9,25},{17,1},{25,9},{2,18},{10... | collective-permute-start | bytes 3145736 | tf_op jit(solution)/shard_map/ppermute | solution.py:61
  326.6 41.2 %collective-permute-start.15 = (bf16[256,2048]{1,0:T(8,128)(2,1)S(1)}, bf16[256,2048]{1,0:T(8,128)(2,1)S(1)}, u32[]{:S(2)}, u32[]{:S(2)}) collective-permute-start(bf16[256,2048]{1,0:T(8,128)(2,1)S(1)} %multiply_convert_fusion.16), channel_id=1, source_target_pairs={{0,8},{8,0},{16,24},{24,16},{1,9},{9,1},{17,25},{25,17},{2,10},{10... | collective-permute-start | bytes 3145736 | tf_op jit(solution)/shard_map/ppermute | solution.py:61
  650.9 54.1 %collective-permute-start.29 = (bf16[256,2048]{1,0:T(8,128)(2,1)}, bf16[256,2048]{1,0:T(8,128)(2,1)}, u32[]{:S(2)}, u32[]{:S(2)}) collective-permute-start(bf16[256,2048]{1,0:T(8,128)(2,1)} %get-tuple-element.480), channel_id=1, source_target_pairs={{0,24},{8,16},{16,8},{24,0},{1,25},{9,17},{17,9},{25,1},{2,26},{10... | collective-permute-start | bytes 3145736 | tf_op jit(solution)/shard_map/ppermute | solution.py:61
  653.3 53.4 %collective-permute-start.28 = (bf16[256,2048]{1,0:T(8,128)(2,1)}, bf16[256,2048]{1,0:T(8,128)(2,1)}, u32[]{:S(2)}, u32[]{:S(2)}) collective-permute-start(bf16[256,2048]{1,0:T(8,128)(2,1)} %get-tuple-element.481), channel_id=1, source_target_pairs={{0,16},{8,24},{16,0},{24,8},{1,17},{9,25},{17,1},{25,9},{2,18},{10... | collective-permute-start | bytes 3145736 | tf_op jit(solution)/shard_map/ppermute | solution.py:61
  653.8 52.8 %collective-permute-start.27 = (bf16[256,2048]{1,0:T(8,128)(2,1)}, bf16[256,2048]{1,0:T(8,128)(2,1)}, u32[]{:S(2)}, u32[]{:S(2)}) collective-permute-start(bf16[256,2048]{1,0:T(8,128)(2,1)} %get-tuple-element.479), channel_id=1, source_target_pairs={{0,8},{8,0},{16,24},{24,16},{1,9},{9,1},{17,25},{25,17},{2,10},{10... | collective-permute-start | bytes 3145736 | tf_op jit(solution)/shard_map/ppermute | solution.py:61
  681.3 18.7 %collective-permute-start.24 = (f32[4,256]{1,0:T(4,128)S(1)}, f32[4,256]{1,0:T(4,128)S(1)}, u32[]{:S(2)}, u32[]{:S(2)}) collective-permute-start(f32[4,256]{1,0:T(4,128)S(1)} %get-tuple-element.534), channel_id=1, source_target_pairs={{0,8},{8,0},{16,24},{24,16},{1,9},{9,1},{17,25},{25,17},{2,10},{10... | collective-permute-start | bytes 12296 | tf_op jit(solution)/shard_map/ppermute | solution.py:61
  682.8 18.7 %collective-permute-start.25 = (f32[4,256]{1,0:T(4,128)S(1)}, f32[4,256]{1,0:T(4,128)S(1)}, u32[]{:S(2)}, u32[]{:S(2)}) collective-permute-start(f32[4,256]{1,0:T(4,128)S(1)} %get-tuple-element.533), channel_id=1, source_target_pairs={{0,16},{8,24},{16,0},{24,8},{1,17},{9,25},{17,1},{25,9},{2,18},{10... | collective-permute-start | bytes 12296 | tf_op jit(solution)/shard_map/ppermute | solution.py:61
  701.5 27.3 %collective-permute-start.20 = (bf16[256,2048]{1,0:T(8,128)(2,1)}, bf16[256,2048]{1,0:T(8,128)(2,1)}, u32[]{:S(2)}, u32[]{:S(2)}) collective-permute-start(bf16[256,2048]{1,0:T(8,128)(2,1)} %get-tuple-element.483), channel_id=1, source_target_pairs={{0,24},{8,16},{16,8},{24,0},{1,25},{9,17},{17,9},{25,1},{2,26},{10... | collective-permute-start | bytes 3145736 | tf_op jit(solution)/shard_map/ppermute | solution.py:61
  704.5 44.9 %collective-permute-start.19 = (bf16[256,2048]{1,0:T(8,128)(2,1)}, bf16[256,2048]{1,0:T(8,128)(2,1)}, u32[]{:S(2)}, u32[]{:S(2)}) collective-permute-start(bf16[256,2048]{1,0:T(8,128)(2,1)} %get-tuple-element.484), channel_id=1, source_target_pairs={{0,16},{8,24},{16,0},{24,8},{1,17},{9,25},{17,1},{25,9},{2,18},{10... | collective-permute-start | bytes 3145736 | tf_op jit(solution)/shard_map/ppermute | solution.py:61
  705.0 44.4 %collective-permute-start.18 = (bf16[256,2048]{1,0:T(8,128)(2,1)S(1)}, bf16[256,2048]{1,0:T(8,128)(2,1)}, u32[]{:S(2)}, u32[]{:S(2)}) collective-permute-start(bf16[256,2048]{1,0:T(8,128)(2,1)S(1)} %get-tuple-element.482), channel_id=1, source_target_pairs={{0,8},{8,0},{16,24},{24,16},{1,9},{9,1},{17,25},{25,17},{2,10},{10... | collective-permute-start | bytes 3145736 | tf_op jit(solution)/shard_map/ppermute | solution.py:61
  769.7 11.9 collective-permute-start.32
  771.2 14.3 collective-permute-start.31
  772.2 13.3 collective-permute-start.30
  779.2 63.4 %collective-permute-start.44 = (bf16[2048,512]{0,1:T(8,128)(2,1)}, bf16[2048,512]{0,1:T(8,128)(2,1)}, u32[]{:S(2)}, u32[]{:S(2)}) collective-permute-start(bf16[2048,512]{0,1:T(8,128)(2,1)} %get-tuple-element.458), channel_id=1, source_target_pairs={{0,24},{8,16},{16,8},{24,0},{1,25},{9,17},{17,9},{25,1},{2,26},{10... | collective-permute-start | bytes 6291464 | tf_op jit(solution)/shard_map/ppermute | solution.py:61
  780.7 93.7 %collective-permute-start.43 = (bf16[2048,512]{0,1:T(8,128)(2,1)}, bf16[2048,512]{0,1:T(8,128)(2,1)}, u32[]{:S(2)}, u32[]{:S(2)}) collective-permute-start(bf16[2048,512]{0,1:T(8,128)(2,1)} %get-tuple-element.459), channel_id=1, source_target_pairs={{0,16},{8,24},{16,0},{24,8},{1,17},{9,25},{17,1},{25,9},{2,18},{10... | collective-permute-start | bytes 6291464 | tf_op jit(solution)/shard_map/ppermute | solution.py:61
  781.6 92.9 %collective-permute-start.42 = (bf16[2048,512]{0,1:T(8,128)(2,1)}, bf16[2048,512]{0,1:T(8,128)(2,1)}, u32[]{:S(2)}, u32[]{:S(2)}) collective-permute-start(bf16[2048,512]{0,1:T(8,128)(2,1)} %get-tuple-element.457), channel_id=1, source_target_pairs={{0,8},{8,0},{16,24},{24,16},{1,9},{9,1},{17,25},{25,17},{2,10},{10... | collective-permute-start | bytes 6291464 | tf_op jit(solution)/shard_map/ppermute | solution.py:61
  881.3 219.3 %reduce-scatter.11.cloned.1.call-start = ((), (), s32[]{:S(2)}) async-start(), calls=%async_computation.14 | async-start | bytes 7077888 | tf_op jit(solution)/shard_map/reduce_scatter | solution.py:388
  891.6 7.0 collective-permute-start.35
  916.1 190.2 %reduce-scatter.29.cloned.1.call-start = ((), (), s32[]{:S(2)}) async-start(), calls=%async_computation.23 | async-start | bytes 4718592 | tf_op jit(solution)/shard_map/reduce_scatter | solution.py:312
  924.2 182.1 %reduce-scatter.27.cloned.1.call-start = ((), (), s32[]{:S(2)}) async-start(), calls=%async_computation.22 | async-start | bytes 4718592 | tf_op jit(solution)/shard_map/reduce_scatter | solution.py:312
  932.3 210.0 %reduce-scatter.25.cloned.1.call-start = ((), (), s32[]{:S(2)}) async-start(), calls=%async_computation.21 | async-start | bytes 4718592 | tf_op jit(solution)/shard_map/reduce_scatter | solution.py:312
  940.6 252.4 %reduce-scatter.23.cloned.1.call-start = ((), (), s32[]{:S(2)}) async-start(), calls=%async_computation.20 | async-start | bytes 4718592 | tf_op jit(solution)/shard_map/reduce_scatter | solution.py:312
  948.7 334.9 %reduce-scatter.21.cloned.1.call-start = ((), (), s32[]{:S(2)}) async-start(), calls=%async_computation.19 | async-start | bytes 9437184 | tf_op jit(solution)/shard_map/reduce_scatter | solution.py:311
  960.8 413.0 %reduce-scatter.19.cloned.1.call-start = ((), (), s32[]{:S(2)}) async-start(), calls=%async_computation.18 | async-start | bytes 9437184 | tf_op jit(solution)/shard_map/reduce_scatter | solution.py:311
  973.0 491.1 %reduce-scatter.17.cloned.1.call-start = ((), (), s32[]{:S(2)}) async-start(), calls=%async_computation.17 | async-start | bytes 9437184 | tf_op jit(solution)/shard_map/reduce_scatter | solution.py:311
  985.0 569.3 %reduce-scatter.15.cloned.1.call-start = ((), (), s32[]{:S(2)}) async-start(), calls=%async_computation.16 | async-start | bytes 9437184 | tf_op jit(solution)/shard_map/reduce_scatter | solution.py:311
  1012.7 52.4 %collective-permute-start.38 = (bf16[256,2048]{1,0:T(8,128)(2,1)}, bf16[256,2048]{1,0:T(8,128)(2,1)}, u32[]{:S(2)}, u32[]{:S(2)}) collective-permute-start(bf16[256,2048]{1,0:T(8,128)(2,1)} %get-tuple-element.477), channel_id=1, source_target_pairs={{0,24},{8,16},{16,8},{24,0},{1,25},{9,17},{17,9},{25,1},{2,26},{10... | collective-permute-start | bytes 3145736 | tf_op jit(solution)/shard_map/ppermute | solution.py:61
  1014.3 50.8 %collective-permute-start.37 = (bf16[256,2048]{1,0:T(8,128)(2,1)}, bf16[256,2048]{1,0:T(8,128)(2,1)}, u32[]{:S(2)}, u32[]{:S(2)}) collective-permute-start(bf16[256,2048]{1,0:T(8,128)(2,1)} %get-tuple-element.478), channel_id=1, source_target_pairs={{0,16},{8,24},{16,0},{24,8},{1,17},{9,25},{17,1},{25,9},{2,18},{10... | collective-permute-start | bytes 3145736 | tf_op jit(solution)/shard_map/ppermute | solution.py:61
  1015.1 50.0 %collective-permute-start.36 = (bf16[256,2048]{1,0:T(8,128)(2,1)}, bf16[256,2048]{1,0:T(8,128)(2,1)}, u32[]{:S(2)}, u32[]{:S(2)}) collective-permute-start(bf16[256,2048]{1,0:T(8,128)(2,1)} %get-tuple-element.476), channel_id=1, source_target_pairs={{0,8},{8,0},{16,24},{24,16},{1,9},{9,1},{17,25},{25,17},{2,10},{10... | collective-permute-start | bytes 3145736 | tf_op jit(solution)/shard_map/ppermute | solution.py:61
  1018.5 15.1 all-to-all-start.1
  1069.2 9.5 all-to-all-start
  1086.7 9.5 collective-permute-start.45
  1088.3 12.3 collective-permute-start.46
  1089.4 14.8 collective-permute-start.47
  1100.7 99.3 %collective-permute-start.39 = (bf16[256,1536]{1,0:T(8,128)(2,1)}, bf16[256,1536]{1,0:T(8,128)(2,1)}, u32[]{:S(2)}, u32[]{:S(2)}) collective-permute-start(bf16[256,1536]{1,0:T(8,128)(2,1)} %reduce-scatter.11.cloned.1.call-done), channel_id=1, source_target_pairs={{0,8},{8,0},{16,24},{24,16},{1,9},{9,1},{17,25},{25,17},{2,10},{10... | collective-permute-start | bytes 2359304 | tf_op jit(solution)/shard_map/ppermute | solution.py:61
  1101.8 99.7 %collective-permute-start.40 = (bf16[256,1536]{1,0:T(8,128)(2,1)}, bf16[256,1536]{1,0:T(8,128)(2,1)}, u32[]{:S(2)}, u32[]{:S(2)}) collective-permute-start(bf16[256,1536]{1,0:T(8,128)(2,1)} %reduce-scatter.11.cloned.1.call-done), channel_id=1, source_target_pairs={{0,16},{8,24},{16,0},{24,8},{1,17},{9,25},{17,1},{25,9},{2,18},{10... | collective-permute-start | bytes 2359304 | tf_op jit(solution)/shard_map/ppermute | solution.py:61
  1102.7 100.2 %collective-permute-start.41 = (bf16[256,1536]{1,0:T(8,128)(2,1)}, bf16[256,1536]{1,0:T(8,128)(2,1)}, u32[]{:S(2)}, u32[]{:S(2)}) collective-permute-start(bf16[256,1536]{1,0:T(8,128)(2,1)} %reduce-scatter.11.cloned.1.call-done), channel_id=1, source_target_pairs={{0,24},{8,16},{16,8},{24,0},{1,25},{9,17},{17,9},{25,1},{2,26},{10... | collective-permute-start | bytes 2359304 | tf_op jit(solution)/shard_map/ppermute | solution.py:61
  (175 other events, 3529.9 us)
Sparse Core Ops, SparseCore 0:
  10.2 33.5 all-gather.24
  45.9 63.9 all-gather.22
  111.5 80.2 all-gather.38
  193.2 80.5 all-gather.34
  275.2 80.5 all-gather.30
  357.2 45.3 all-gather.40
  404.2 45.6 all-gather.36
  451.5 45.6 all-gather.32
  498.8 80.8 all-gather.26
  581.2 45.3 all-gather.28
  881.5 33.7 reduce-scatter.12
  918.0 68.4 reduce-scatter.10
  988.8 51.5 reduce-scatter.28
  1042.5 49.2 reduce-scatter.26
  1093.9 48.3 reduce-scatter.24
  1144.5 48.3 reduce-scatter.22
  1195.6 87.9 reduce-scatter.20
  1285.8 87.9 reduce-scatter.18
  1376.1 87.9 reduce-scatter.16
  1466.3 87.9 reduce-scatter.14

commit v2 on v1

--- a/solution.py
+++ b/solution.py
@@ -134,34 +134,178 @@
     return jnp.einsum(form, left, right, preferred_element_type=jnp.float32)
 
 
-def expert_pass(rows, grad_result_rows, slot_weight, gate_up, down):
+def expert_forward(rows, grad_result_rows, slot_weight, gate_up, down):
     half_width = down.shape[0]
     gate_up_out = mixed_dot("rd,df->rf", rows, gate_up)
     gate_part = gate_up_out[:, :half_width]
     up_part = gate_up_out[:, half_width:]
     sigmoid_gate = jax.nn.sigmoid(gate_part)
     hidden = (gate_part * sigmoid_gate * up_part).astype(jnp.bfloat16)
-    result = mixed_dot("rf,fd->rd", hidden, down).astype(jnp.bfloat16)
     grad_result = (grad_result_rows.astype(jnp.float32) * slot_weight[:, None]).astype(jnp.bfloat16)
     grad_hidden = mixed_dot("rd,fd->rf", grad_result, down)
     grad_gate = grad_hidden * up_part * sigmoid_gate * (1.0 + gate_part * (1.0 - sigmoid_gate))
     grad_up = grad_hidden * gate_part * sigmoid_gate
     grad_mixed = jnp.concatenate([grad_gate, grad_up], -1).astype(jnp.bfloat16)
+    grad_rows = mixed_dot("rd,fd->rf", grad_mixed, gate_up).astype(jnp.bfloat16)
+    result = mixed_dot("rf,fd->rd", hidden, down).astype(jnp.bfloat16)
+    grad_slot = jnp.sum(
+        result.astype(jnp.float32) * grad_result_rows.astype(jnp.float32), axis=-1
+    )
+    weighted = (result.astype(jnp.float32) * slot_weight[:, None]).astype(jnp.bfloat16)
+    return (weighted, grad_slot, grad_rows, (rows, grad_mixed, hidden, grad_result))
+
+
+def expert_weights(kept):
+    rows, grad_mixed, hidden, grad_result = kept
     grad_gate_up = mixed_dot("rd,rf->df", rows, grad_mixed).astype(jnp.bfloat16)
     grad_down = mixed_dot("rf,rd->fd", hidden, grad_result).astype(jnp.bfloat16)
-    grad_rows = mixed_dot("rf,df->rd", grad_mixed, gate_up).astype(jnp.bfloat16)
-    grad_slot = jnp.sum(
-        result.astype(jnp.float32) * grad_result_rows.astype(jnp.float32), axis=-1
-    )
-    weighted = (result.astype(jnp.float32) * slot_weight[:, None]).astype(jnp.bfloat16)
-    return (weighted, grad_slot, grad_rows, grad_gate_up, grad_down)
-
-
-def sum_small(rows):
-    fsdp_count = lax.axis_size("fsdp")
-    pieces = rows.reshape(rows.shape[0], fsdp_count, -1)
-    pieces = lax.all_to_all(pieces, "fsdp", split_axis=1, concat_axis=1, tiled=True)
-    return jnp.sum(lax.all_gather(jnp.sum(pieces, axis=1), "seq", axis=0), axis=0)
+    return (grad_gate_up, grad_down)
+
+
+LINE = 4
+
+
+def along(values, hops):
+    pairs = [(2 * source + core, 2 * target + core) for source, target in hops for core in range(2)]
+    return lax.ppermute(values, "fsdp", pairs)
+
+
+def swap_cores(values):
+    count = lax.axis_size("fsdp")
+    return lax.ppermute(values, "fsdp", [(index, index ^ 1) for index in range(count)])
+
+
+def place_block(buffer, block, chip, core):
+    return lax.dynamic_update_slice(buffer, block[None, None], (chip, core, 0, 0))
+
+
+def place_side(buffer, side, core):
+    return lax.dynamic_update_slice(buffer, side[:, None], (0, core, 0, 0))
+
+
+def line_gather(gate_up, down):
+    index = lax.axis_index("fsdp")
+    chip, core = index // 2, index % 2
+    up_rows, width = gate_up.shape
+    own = jnp.concatenate([gate_up, down], axis=0)
+    right, left = yield (
+        along(own, [(0, 1), (1, 2), (2, 3)]),
+        along(own, [(3, 2), (2, 1), (1, 0)]),
+    )
+    right_two, left_two = yield (
+        along(right, [(1, 2), (2, 3)]),
+        along(left, [(2, 1), (1, 0)]),
+    )
+    right_three, left_three = yield (along(right_two, [(2, 3)]), along(left_two, [(1, 0)]))
+    near = jnp.where(chip < 3, left, right)
+    middle = jnp.where(chip < 2, left_two, right_two)
+    far = jnp.where(chip == 0, left_three, jnp.where(chip == 3, right_three, right))
+    near_chip = jnp.where(chip < 3, chip + 1, 2)
+    far_chip = jnp.where(chip == 0, 3, jnp.where(chip == 3, 0, chip - 1))
+    side = jnp.zeros((LINE,) + own.shape, own.dtype)
+    for block, place in ((own, chip), (near, near_chip), (middle, (chip + 2) % 4), (far, far_chip)):
+        side = lax.dynamic_update_slice(side, block[None], (place, 0, 0))
+    other = yield swap_cores(side)
+    sides = []
+    for start, stop in ((0, up_rows), (up_rows, own.shape[0])):
+        buffer = jnp.zeros((LINE, 2, stop - start, width), own.dtype)
+        buffer = place_side(buffer, side[:, start:stop], core)
+        buffer = place_side(buffer, other[:, start:stop], 1 - core)
+        sides.append(buffer.reshape(-1, width))
+    return tuple(sides)
+
+
+def line_scatter(gate_up, down):
+    f32 = jnp.float32
+    index = lax.axis_index("fsdp")
+    chip, core = index // 2, index % 2
+    width = gate_up.shape[1]
+    shaped = [grad.reshape(LINE, 2, -1, width) for grad in (gate_up, down)]
+    up_rows = shaped[0].shape[2]
+
+    def side(number):
+        return jnp.concatenate(
+            [lax.dynamic_index_in_dim(grad, number, 1, False) for grad in shaped], axis=1
+        )
+
+    got = yield swap_cores(side(1 - core))
+    part = (side(core).astype(f32) + got.astype(f32)).astype(jnp.bfloat16)
+
+    def take(place, landed=None):
+        block = lax.dynamic_index_in_dim(part, place, 0, False)
+        if landed is None:
+            return block
+        return (block.astype(f32) + landed.astype(f32)).astype(jnp.bfloat16)
+
+    first = yield along(take(jnp.where(chip == 0, 3, 0)), [(0, 1), (3, 2)])
+    outer, inner = yield (
+        along(take(jnp.where(chip == 0, 2, 1)), [(0, 1), (3, 2)]),
+        along(take(jnp.where(chip == 1, 3, 0), first), [(1, 2), (2, 1)]),
+    )
+    right, left = yield (
+        along(
+            take(jnp.minimum(chip + 1, 3), jnp.where(chip == 1, outer, inner)),
+            [(0, 1), (1, 2), (2, 3)],
+        ),
+        along(
+            take(jnp.maximum(chip - 1, 0), jnp.where(chip == 2, outer, inner)),
+            [(3, 2), (2, 1), (1, 0)],
+        ),
+    )
+    total = take(chip).astype(f32) + right.astype(f32) + left.astype(f32)
+    return (total[:up_rows], total[up_rows:])
+
+
+def whole_gather(gate_up, down):
+    landed = yield tuple(
+        lax.all_gather(part, "fsdp", axis=0, tiled=True) for part in (gate_up, down)
+    )
+    return tuple(landed)
+
+
+def whole_scatter(gate_up, down):
+    landed = yield tuple(
+        lax.psum_scatter(part, "fsdp", scatter_dimension=0, tiled=True) for part in (gate_up, down)
+    )
+    return tuple(part.astype(jnp.float32) for part in landed)
+
+
+class Stream:
+    def __init__(self, rounds):
+        self.rounds, self.result = rounds, None
+        self.flight = next(rounds)
+
+    def advance(self, landed):
+        try:
+            self.flight = self.rounds.send(landed)
+        except StopIteration as stop:
+            self.flight, self.result = (), stop.value
+
+
+class Slots:
+    def __init__(self):
+        self.streams, self.tick = [], jnp.zeros((), jnp.float32)
+
+    def start(self, rounds, *arrays):
+        arrays = self.gate(arrays)
+        self.streams.append(Stream(rounds(*arrays)))
+        return self.streams[-1]
+
+    def gate(self, arrays):
+        return lax.optimization_barrier((arrays, self.tick))[0]
+
+    def close(self, values):
+        flights = [stream.flight for stream in self.streams]
+        flights, values, self.tick = lax.optimization_barrier((flights, values, self.tick))
+        for stream, landed in zip(self.streams, flights):
+            stream.advance(landed)
+        self.streams = [stream for stream in self.streams if stream.result is None]
+        return values
+
+    def finish(self, stream, values):
+        while stream.result is None:
+            values = self.close(values)
+        return values
 
 
 def local(
@@ -182,6 +326,9 @@
     bf16, f32 = jnp.bfloat16, jnp.float32
     seq_count = lax.axis_size("seq")
     seq_rank = lax.axis_index("seq")
+    in_line = lax.axis_size("fsdp") == 2 * LINE
+    gather_rounds = line_gather if in_line else whole_gather
+    scatter_rounds = line_scatter if in_line else whole_scatter
     own_tokens = tokens[0]
     tok_count, model_width = own_tokens.shape
     local_count = gate_up_weight.shape[0]
@@ -196,36 +343,38 @@
     ).reshape(-1)
     valid_all = (places < length).reshape(seq_count, tok_count)
     keep_mask = valid_all[0].astype(f32)[:, None]
+    slots = Slots()
+    slot_weights = lambda index: (gate_up_weight[index], down_weight[index])
 
     own_qkv = lax.dynamic_index_in_dim(
         qkv_weight.reshape(-1, 3, seq_count, own_width), seq_rank, 2, False
     ).reshape(-1, 3 * own_width)
-    qkv_own = lax.all_gather(own_qkv, "fsdp", axis=0, tiled=True)
+    own_small = jnp.concatenate(
+        [jnp.stack([attn_gain, q_gain, k_gain, moe_gain], axis=1), router_weight], axis=1
+    )
+    small_count = 4 + experts_count
+    small_width = round_up(small_count, 128)
+    own_small = jnp.pad(own_small, ((0, 0), (0, small_width - small_count)))
+    front = jnp.concatenate([own_qkv, own_small], axis=1)
+    front_full = lax.all_gather(front, "fsdp", axis=0, tiled=True)
     token_blocks = gather_blocks(own_tokens)
-    small_rows = jnp.concatenate(
-        [jnp.stack([attn_gain, q_gain, k_gain, moe_gain]), router_weight.T], axis=0
-    )
-    small_full = lax.all_gather(small_rows, "fsdp", axis=1, tiled=True)
+    id_blocks = gather_blocks(experts[0])
+    out_cut = lax.dynamic_slice_in_dim(out_weight, seq_rank * own_width, own_width, 1)
+    out_cut = lax.optimization_barrier((out_cut, front))[0]
+    out_cut = lax.all_gather(out_cut, "fsdp", axis=0, tiled=True)
+    front_full, token_blocks = slots.close((front_full, token_blocks))
+
+    gathers = [slots.start(gather_rounds, *slot_weights(0))]
+    cot_blocks = gather_blocks(slots.gate(cotangent[0]))
+    qkv_own = front_full[:, : 3 * own_width]
+    small_full = front_full[:, 3 * own_width : 3 * own_width + small_count].T
     gain_one, gain_q, gain_k, gain_two = [small_full[i].astype(f32) for i in range(4)]
     router_rows = small_full[4:]
     gain_q = lax.dynamic_slice_in_dim(gain_q, seq_rank * own_width, own_width, 0)
     gain_k = lax.dynamic_slice_in_dim(gain_k, seq_rank * own_width, own_width, 0)
-    out_cut = lax.dynamic_slice_in_dim(out_weight, seq_rank * own_width, own_width, 1)
-    out_cut = lax.all_gather(out_cut, "fsdp", axis=0, tiled=True)
-    out_full = in_rank_order([from_peer(out_cut, step) for step in range(seq_count)])
-    weights = []
-    for index in range(local_count):
-        weights.append(
-            (
-                lax.all_gather(gate_up_weight[index], "fsdp", axis=0, tiled=True),
-                lax.all_gather(down_weight[index], "fsdp", axis=0, tiled=True),
-            )
-        )
-    id_blocks = gather_blocks(experts[0])
-    cot_blocks = gather_blocks(cotangent[0])
-
     inputs_all = token_blocks.reshape(key_span, model_width).astype(f32)
-    normed = (inputs_all * rms_scale(inputs_all) * gain_one).astype(bf16)
+    scale_all = rms_scale(inputs_all)
+    normed = (inputs_all * scale_all * gain_one).astype(bf16)
     projected = mixed_dot("td,de->te", normed, qkv_own)
     query_raw = projected[:, :own_width]
     key_raw = projected[:, own_width : 2 * own_width]
@@ -252,15 +401,20 @@
         key_rot.astype(bf16),
         value_raw.reshape(head_shape).astype(bf16),
     )
+    heads_in = slots.close(heads_in)
+
     row_count = min(512, key_span)
     block_starts = jnp.arange(key_span // row_count, dtype=jnp.int32) * row_count
     attended_blocks, sums_blocks = lax.map(
         partial(attend_block, heads_in, places, length, row_count), block_starts
     )
     log_sums = sums_blocks.reshape(key_span, own_heads)
+    out_parts = [from_peer(out_cut, step) for step in range(seq_count)]
+    attended_blocks, cot_blocks, out_parts = slots.close((attended_blocks, cot_blocks, out_parts))
+
+    out_full = in_rank_order(out_parts)
     attended_parts = return_blocks(attended_blocks.reshape(seq_count, tok_count, own_width))
     attended = jnp.transpose(in_rank_order(attended_parts), (1, 0, 2))
-
     inputs = own_tokens.astype(f32)
     branch = mixed_dot(
         "td,jdc->tjc", attended.reshape(tok_count, model_width), out_full
@@ -269,8 +423,11 @@
     scale_two = rms_scale(middle)
     unit_two = middle * scale_two
     normed_two = (unit_two * gain_two).astype(bf16)
-
-    row_blocks = gather_blocks(normed_two)
+    normed_two = slots.close(normed_two)
+
+    gathers.append(slots.start(gather_rounds, *slot_weights(1)))
+    row_blocks = slots.close(gather_blocks(normed_two))
+
     logits = mixed_dot("btd,ed->bte", row_blocks, router_rows)
     expert_range = jnp.arange(experts_count, dtype=jnp.int32)
     named = jnp.any(id_blocks[..., None] == expert_range, axis=2)
@@ -282,45 +439,71 @@
     local_routed = lax.dynamic_slice_in_dim(routed, seq_rank * local_count, local_count, 2)
     local_before = lax.dynamic_slice_in_dim(before, seq_rank * local_count, local_count, 2)
     local_gates = lax.dynamic_slice_in_dim(gates, seq_rank * local_count, local_count, 2)
-    slots = round_up(CAP, 16)
+    slot_count = round_up(CAP, 16)
     slot_place = jnp.where(local_routed == 1, local_before, -1)
     slot_place = jnp.transpose(slot_place, (2, 0, 1))
     local_gates = jnp.transpose(local_gates, (2, 0, 1))
-    slot_hit = slot_place[:, :, None, :] == jnp.arange(slots, dtype=jnp.int32)[:, None]
+    slot_hit = slot_place[:, :, None, :] == jnp.arange(slot_count, dtype=jnp.int32)[:, None]
     slot_pick = slot_hit.astype(bf16)
     slot_gates = jnp.sum(jnp.where(slot_hit, local_gates[:, :, None, :], 0.0), axis=-1)
 
-    weighted_rows, grad_row_sets, grad_slots, gate_up_sums, down_sums = [], [], [], [], []
-    for index in range(local_count):
-        pick = slot_pick[index]
-        rows = mixed_dot("bct,btd->bcd", pick, row_blocks).astype(bf16)
-        grad_source = mixed_dot("bct,btd->bcd", pick, cot_blocks).astype(bf16)
-        weighted, grad_slot, grad_rows, grad_gate_up, grad_down = expert_pass(
-            rows.reshape(seq_count * slots, model_width),
-            grad_source.reshape(seq_count * slots, model_width),
-            slot_gates[index].reshape(-1),
-            *weights[index],
+    def picked(index):
+        return tuple(
+            mixed_dot("bct,btd->bcd", slot_pick[index], blocks)
+            .astype(bf16)
+            .reshape(seq_count * slot_count, model_width)
+            for blocks in (row_blocks, cot_blocks)
         )
-        weighted_rows.append(weighted.reshape(seq_count, slots, model_width))
-        grad_row_sets.append(grad_rows.reshape(seq_count, slots, model_width))
+
+    def computed(index, pair):
+        weighted, grad_slot, grad_rows, kept = expert_forward(
+            *pair, slot_gates[index].reshape(-1), *gathers[index].result
+        )
+        weighted_rows.append(weighted.reshape(seq_count, slot_count, model_width))
+        grad_row_sets.append(grad_rows.reshape(seq_count, slot_count, model_width))
         grad_slots.append(
             jnp.sum(
-                jnp.where(slot_hit[index], grad_slot.reshape(seq_count, slots)[:, :, None], 0.0), 1
+                jnp.where(
+                    slot_hit[index], grad_slot.reshape(seq_count, slot_count)[:, :, None], 0.0
+                ),
+                1,
             )
         )
-        gate_up_sums.append(lax.psum_scatter(grad_gate_up, "fsdp", scatter_dimension=0, tiled=True))
-        down_sums.append(lax.psum_scatter(grad_down, "fsdp", scatter_dimension=0, tiled=True))
+        return kept
+
+    weighted_rows, grad_row_sets, grad_slots, scatters = [], [], [], []
+    pair = slots.close(picked(0))
+
+    for index in range(local_count):
+        pair = slots.finish(gathers[index], pair)
+        kept = computed(index, pair)
+        last = index == local_count - 1
+        if last:
+            break
+        grads = slots.close(expert_weights(kept))
+        pair = picked(index + 1)
+        if index + 2 < local_count:
+            gathers.append(slots.start(gather_rounds, *slot_weights(index + 2)))
+        scatters.append(slots.start(scatter_rounds, *grads))
+        pair = slots.close(pair)
     pick_all = jnp.concatenate([slot_pick[index] for index in range(local_count)], axis=1)
     grad_partial = mixed_dot("bct,bcd->btd", pick_all, jnp.concatenate(grad_row_sets, axis=1))
-    grad_back = return_blocks(grad_partial.astype(bf16))
-    grad_gates = in_rank_order(return_blocks(jnp.stack(grad_slots, axis=1)))
+    grad_partial, grad_slots, kept = slots.close(
+        (grad_partial.astype(bf16), jnp.stack(grad_slots, axis=1), kept)
+    )
+
+    grad_back = return_blocks(grad_partial)
+    grad_gates = return_blocks(grad_slots)
     moe_partial = mixed_dot("bct,bcd->btd", pick_all, jnp.concatenate(weighted_rows, axis=1))
-    moe_parts = return_blocks(moe_partial.astype(bf16))
-    moe_sum = sum(part.astype(f32) for part in moe_parts)
-    block_out = (middle + moe_sum).astype(bf16)
+    grads, grad_back, grad_gates, moe_partial = slots.close(
+        (expert_weights(kept), grad_back, grad_gates, moe_partial.astype(bf16))
+    )
+    scatters.append(slots.start(scatter_rounds, *grads))
 
     own_gates = gates[0]
-    grad_gates = jnp.transpose(grad_gates, (2, 0, 1)).reshape(tok_count, experts_count)
+    grad_gates = jnp.transpose(in_rank_order(grad_gates), (2, 0, 1)).reshape(
+        tok_count, experts_count
+    )
     grad_logits = own_gates * (
         grad_gates - jnp.sum(own_gates * grad_gates, axis=-1, keepdims=True)
     )
@@ -337,14 +520,6 @@
     grad_attended = mixed_dot(
         "tjc,jdc->td", grad_branch.reshape(tok_count, seq_count, own_width), out_full
     ).astype(bf16)
-    grad_cut = mixed_dot("td,tc->dc", attended.reshape(tok_count, model_width), grad_branch)
-    grad_cut = grad_cut.astype(bf16).reshape(model_width, seq_count, own_width)
-    grad_cut = [
-        from_peer(lax.dynamic_index_in_dim(grad_cut, seq_rank ^ step, 1, False), step)
-        for step in range(seq_count)
-    ]
-    grad_cut = sum(part.astype(f32) for part in grad_cut).astype(bf16)
-
     cut_heads = grad_attended.reshape(tok_count, seq_count, own_width)
     grad_heads = jnp.stack(
         [
@@ -352,12 +527,28 @@
             for step in range(seq_count)
         ]
     ).reshape(head_shape)
+    grad_heads, grad_branch, moe_partial = slots.close((grad_heads, grad_branch, moe_partial))
+
+    moe_parts = return_blocks(moe_partial)
+    grad_cut = mixed_dot("td,tc->dc", attended.reshape(tok_count, model_width), grad_branch)
+    grad_cut = grad_cut.astype(bf16).reshape(model_width, seq_count, own_width)
+    grad_cut = [
+        from_peer(lax.dynamic_index_in_dim(grad_cut, seq_rank ^ step, 1, False), step)
+        for step in range(seq_count)
+    ]
     zero_heads = jnp.zeros(head_shape, f32)
     (grad_keys, grad_values), grad_queries = lax.scan(
         partial(attend_back, heads_in, grad_heads, log_sums, places, length, row_count),
         (zero_heads, zero_heads),
         block_starts,
     )
+    grad_keys, grad_values, grad_queries, grad_cut, moe_parts = slots.close(
+        (grad_keys, grad_values, grad_queries, grad_cut, moe_parts)
+    )
+
+    moe_sum = sum(part.astype(f32) for part in moe_parts)
+    block_out = (middle + moe_sum).astype(bf16)
+    grad_cut = sum(part.astype(f32) for part in grad_cut).astype(bf16)
     low = lambda rows: rows.reshape(head_shape).astype(bf16).astype(f32)
     grad_qn = rotate_back(low(grad_queries), cosine_table, sine_table).reshape(key_span, own_width)
     grad_kn = rotate_back(low(grad_keys), cosine_table, sine_table).reshape(key_span, own_width)
@@ -375,49 +566,61 @@
         ],
         axis=1,
     ).astype(bf16)
+    grad_normed = mixed_dot("te,de->td", grad_projected, qkv_own)
+    grad_one = jnp.sum(grad_normed * (inputs_all * scale_all), axis=0)
     grad_qkv = mixed_dot("td,te->de", normed, grad_projected).astype(bf16)
-    grad_normed = mixed_dot("te,de->td", grad_projected, qkv_own).astype(bf16)
-    grad_normed = sum(
-        part.astype(f32)
-        for part in return_blocks(grad_normed.reshape(seq_count, tok_count, model_width))
-    )
+    placed = lambda row: lax.dynamic_update_slice(
+        jnp.zeros((model_width,), f32), row, (seq_rank * own_width,)
+    )
+    grad_small = jnp.concatenate(
+        [
+            jnp.stack(
+                [
+                    grad_one,
+                    placed(jnp.sum(grad_qn * unit_q, axis=0)),
+                    placed(jnp.sum(grad_kn * unit_k, axis=0)),
+                    grad_two,
+                ]
+            ),
+            grad_router,
+            jnp.zeros((small_width - small_count, model_width), f32),
+        ],
+        axis=0,
+    )
+    grad_front = jnp.concatenate([grad_qkv, grad_small.T.astype(bf16)], axis=1)
+    grad_front, grad_normed = slots.close((grad_front, grad_normed.astype(bf16)))
+
+    front_sum = lax.psum_scatter(grad_front, "fsdp", scatter_dimension=0, tiled=True)
+    out_sum = lax.psum_scatter(grad_cut, "fsdp", scatter_dimension=0, tiled=True)
+    grad_normed = return_blocks(grad_normed.reshape(seq_count, tok_count, model_width))
+    grad_normed = slots.finish(scatters[-1], grad_normed)
+    grad_normed = sum(part.astype(f32) for part in grad_normed)
     scale_one = rms_scale(inputs)
-    grad_inputs_norm, grad_one = norm_back(grad_normed, inputs * scale_one, scale_one, gain_one)
-    grad_tokens = (grad_middle + grad_inputs_norm).astype(bf16)
-
-    qkv_sum = lax.psum_scatter(grad_qkv, "fsdp", scatter_dimension=0, tiled=True)
-    qkv_sum = in_rank_order([from_peer(qkv_sum, step) for step in range(seq_count)])
+    scaled = grad_normed * gain_one
+    unit_one = inputs * scale_one
+    inner = jnp.mean(scaled * unit_one, axis=-1, keepdims=True)
+    grad_tokens = (grad_middle + scale_one * (scaled - unit_one * inner)).astype(bf16)
+    front_parts = [from_peer(front_sum, step) for step in range(seq_count)]
+    small_sum = sum(part[:, 3 * own_width :].astype(f32) for part in front_parts)
+    qkv_sum = in_rank_order([part[:, : 3 * own_width] for part in front_parts])
     qkv_sum = jnp.transpose(
         qkv_sum.reshape(seq_count, -1, 3, own_width), (1, 2, 0, 3)
     ).reshape(-1, 3 * model_width)
-    out_sum = lax.psum_scatter(grad_cut, "fsdp", scatter_dimension=0, tiled=True)
     out_sum = in_rank_order([from_peer(out_sum, step) for step in range(seq_count)])
     out_sum = jnp.transpose(out_sum, (1, 0, 2)).reshape(-1, model_width)
-    early = sum_small(jnp.concatenate([grad_router, grad_two[None]], axis=0))
-    placed = lambda row: lax.dynamic_update_slice(
-        jnp.zeros((model_width,), f32), row, (seq_rank * own_width,)
-    )
-    late = sum_small(
-        jnp.stack(
-            [
-                grad_one,
-                placed(jnp.sum(grad_qn * unit_q, axis=0)),
-                placed(jnp.sum(grad_kn * unit_k, axis=0)),
-            ]
-        )
-    )
+    sums = [stream.result for stream in scatters]
     return (
         block_out[None],
         grad_tokens[None],
-        late[0],
+        small_sum[:, 0],
         qkv_sum.astype(f32),
-        late[1],
-        late[2],
+        small_sum[:, 1],
+        small_sum[:, 2],
         out_sum.astype(f32),
-        early[experts_count],
-        early[:experts_count].T,
-        jnp.stack(gate_up_sums).astype(f32),
-        jnp.stack(down_sums).astype(f32),
+        small_sum[:, 3],
+        small_sum[:, 4:small_count],
+        jnp.stack([pair[0] for pair in sums]),
+        jnp.stack([pair[1] for pair in sums]),
     )
 
 

time: 1570 us -> 1640 us (1.045)
  waiting for transfers between devices: 866 us -> 674 us
  other arithmetic: 83.6 us -> 232 us
  local copies, waits for them, and re-layouts: 129 us -> 261 us
  starting transfers between devices: 69.6 us -> 143 us
  blocking collectives: 52.5 us -> 0 us
  matrix products: 340 us -> 300 us
    reduce_scatter x9 -> x1, waiting for transfers between devices: 421 us -> 0.02 us  [local(): lax.psum_scatter(grad_front, 'fsdp', scatter_dimension=0, tiled=True)]
    ppermute x0 -> x52, waiting for transfers between devices: none -> 309 us  [the longest x44 309 us: along(): return lax.ppermute(values, 'fsdp', pairs)]
    all_gather x9 -> x1, waiting for transfers between devices: 148 us -> 18.4 us  [local(): front_full = lax.all_gather(front, 'fsdp', axis=0, tiled=True)]
    ppermute x0 -> x52, starting transfers between devices: none -> 88.2 us  [the longest x44 87.3 us: along(): return lax.ppermute(values, 'fsdp', pairs)]
    ppermute x48, waiting for transfers between devices: 280 us -> 346 us  [from_peer(): lax.ppermute(values, 'seq', [(rank, rank ^ step) for rank in range(count)])]
    convert_element_type x4 -> x15, other arithmetic: 12.8 us -> 75.6 us  [the longest x4 43.5 us: line_scatter(): part = (side(core).astype(f32) + got.astype(f32)).astype(jnp.bfloat16)]
    all_gather x3 -> x0, blocking collectives: 52.5 us -> none  [the longest x2 38.2 us: sum_small(): lax.all_gather(jnp.sum(pieces, axis=1), 'seq', axis=0)]
    squeeze x1 -> x15, local copies, waits for them, and re-layouts: 1.04 us -> 53.4 us  [the longest x8 32.4 us: side(): lax.dynamic_index_in_dim(grad, number, 1, False)]
  transfers between devices with their start and end apart: 70 -> 104, of which waited for: 32 -> 42; matrix products, arithmetic and copies ran while one was open for 30% -> 36% of each run, Pallas kernels for 0% -> 0%
where the time goes in v2:
time: 1640 us
  waiting for transfers between devices  674 us (41%)
  matrix products  300 us (18%)
  local copies, waits for them, and re-layouts  261 us (16%)
  other arithmetic  232 us (14%)
  starting transfers between devices  143 us (9%)
  between operations  18.2 us (1%)
    ppermute x48, waiting for transfers between devices, from_peer(): lax.ppermute(values, 'seq', [(rank, rank ^ step) for rank in range(count)])  346 us
    ppermute x44, waiting for transfers between devices, along(): return lax.ppermute(values, 'fsdp', pairs)  309 us
    dot_general x40, matrix products, mixed_dot(): return jnp.einsum(form, left, right, preferred_element_type=jnp.float32)  251 us
    ppermute x44, starting transfers between devices, along(): return lax.ppermute(values, 'fsdp', pairs)  87.3 us
    ppermute x48, starting transfers between devices, from_peer(): lax.ppermute(values, 'seq', [(rank, rank ^ step) for rank in range(count)])  54.3 us
    unnamed x397, local copies, waits for them, and re-layouts  47.8 us
    dynamic_update_slice x16, local copies, waits for them, and re-layouts, place_side(): return lax.dynamic_update_slice(buffer, side[:, None], (0, core, 0, 0))  46.2 us
    convert_element_type x4, other arithmetic, line_scatter(): part = (side(core).astype(f32) + got.astype(f32)).astype(jnp.bfloat16)  43.5 us
  transfers between devices with their start and end apart: 104, of which 42 were waited for; matrix products, arithmetic and copies ran while one was open for 36% of the time, Pallas kernels for 0%

profile of v2, /device:TPU:0, one launch (start us, length us, event | category | flops | bytes accessed | tf_op | source)
XLA Modules:
  0.0 1637.1 jit_solution(7557757375802105691)
XLA Ops:
  7.2 7.5 reshape.513
  39.6 11.9 collective-permute-done
  51.4 23.1 %collective-permute-done.1 = bf16[256,2048]{1,0:T(8,128)(2,1)} collective-permute-done((bf16[256,2048]{1,0:T(8,128)(2,1)S(1)}, bf16[256,2048]{1,0:T(8,128)(2,1)}, u32[]{:S(2)}, u32[]{:S(2)}) %collective-permute-start.1) | collective-permute-done | bytes 1048608 | tf_op jit(solution)/shard_map/ppermute | solution.py:61
  78.2 18.4 %all-gather.3.cloned.1.call-done = bf16[2048,1664]{0,1:T(8,128)(2,1)} async-done(((bf16[256,1664]{0,1:T(8,128)(2,1)}), bf16[2048,1664]{0,1:T(8,128)(2,1)}) %all-gather.3.cloned.1.call-update) | async-done | bytes 6815760 | tf_op jit(solution)/shard_map/all_gather | solution.py:359
  104.2 6.7 fusion.55
  139.6 15.1 collective-permute-done.10
  156.1 22.1 %collective-permute-done.11 = bf16[256,2048]{1,0:T(8,128)(2,1)} collective-permute-done((bf16[256,2048]{1,0:T(8,128)(2,1)}, bf16[256,2048]{1,0:T(8,128)(2,1)}, u32[]{:S(2)}, u32[]{:S(2)}) %collective-permute-start.11) | collective-permute-done | bytes 1048608 | tf_op jit(solution)/shard_map/ppermute | solution.py:61
  187.8 23.3 %while.28 = (s32[]{:T(128)}, bf16[2,512,4,128]{3,1,2,0:T(8,128)(2,1)}, f32[2,512,4]{1,2,0:T(4,128)S(1)}, s32[2]{0:T(128)S(1)}, s32[1024]{0:T(1024)S(1)}, /*index...) while((s32[]{:T(128)}, ...), condition=%wide.region_6.7_spmd.clone, body=%wide.region_3.6_spmd.clone.sunk | while | flops 1100218368 | bytes 30503628 | solution.py:408
  215.6 6.6 collective-permute-done.13
  222.2 45.1 %collective-permute-done.14 = bf16[2048,512]{0,1:T(8,128)(2,1)} collective-permute-done((bf16[2048,512]{0,1:T(8,128)(2,1)}, bf16[2048,512]{0,1:T(8,128)(2,1)}, u32[]{:S(2)}, u32[]{:S(2)}) %collective-permute-start.14) | collective-permute-done | bytes 2097184 | tf_op jit(solution)/shard_map/ppermute | solution.py:61
  303.9 7.5 collective-permute-done.20
  338.2 12.0 collective-permute-done.24
  360.4 17.2 %collective-permute-done.25 = bf16[256,2048]{1,0:T(8,128)(2,1)S(1)} collective-permute-done((bf16[256,2048]{1,0:T(8,128)(2,1)S(1)}, bf16[256,2048]{1,0:T(8,128)(2,1)S(1)}, u32[]{:S(2)}, u32[]{:S(2)}) %collective-permute-start.25) | collective-permute-done | bytes 1048608 | tf_op jit(solution)/shard_map/ppermute | solution.py:61
  400.8 24.0 %collective-permute-done.28 = bf16[384,2048]{1,0:T(8,128)(2,1)S(1)} collective-permute-done((bf16[384,2048]{1,0:T(8,128)(2,1)}, bf16[384,2048]{1,0:T(8,128)(2,1)S(1)}, u32[]{:S(2)}, u32[]{:S(2)}) %collective-permute-start.28) | collective-permute-done | bytes 1572896 | tf_op jit(solution)/shard_map/ppermute | solution.py:170
  441.6 9.1 convolution_convert_fusion.5
  450.8 22.3 %collective-permute-done.33 = bf16[384,2048]{1,0:T(8,128)(2,1)S(1)} collective-permute-done((bf16[384,2048]{1,0:T(8,128)(2,1)S(1)}, bf16[384,2048]{1,0:T(8,128)(2,1)S(1)}, u32[]{:S(2)}, u32[]{:S(2)}) %collective-permute-start.33) | collective-permute-done | bytes 1572896 | tf_op jit(solution)/shard_map/ppermute | solution.py:170
  474.2 6.8 dynamic-slice_bitcast_fusion.7
  515.1 16.6 %collective-permute-done.35 = bf16[384,2048]{1,0:T(8,128)(2,1)S(1)} collective-permute-done((bf16[384,2048]{1,0:T(8,128)(2,1)S(1)}, bf16[384,2048]{1,0:T(8,128)(2,1)S(1)}, u32[]{:S(2)}, u32[]{:S(2)}) %collective-permute-start.35) | collective-permute-done | bytes 1572896 | tf_op jit(solution)/shard_map/ppermute | solution.py:170
  538.3 6.4 bitcast_dynamic-update-slice_fusion.3
  544.7 10.2 add_convert_fusion.3
  563.2 7.6 fusion.185
  578.4 9.4 convolution_convert_fusion.4
  600.2 6.8 dynamic-slice_bitcast_fusion.5
  633.1 17.6 %collective-permute-done.43 = bf16[384,2048]{1,0:T(8,128)(2,1)} collective-permute-done((bf16[384,2048]{1,0:T(8,128)(2,1)}, bf16[384,2048]{1,0:T(8,128)(2,1)}, u32[]{:S(2)}, u32[]{:S(2)}) %collective-permute-start.43) | collective-permute-done | bytes 1572896 | tf_op jit(solution)/shard_map/ppermute | solution.py:170
  662.2 21.7 %collective-permute-done.45 = bf16[384,2048]{1,0:T(8,128)(2,1)S(1)} collective-permute-done((bf16[384,2048]{1,0:T(8,128)(2,1)S(1)}, bf16[384,2048]{1,0:T(8,128)(2,1)S(1)}, u32[]{:S(2)}, u32[]{:S(2)}) %collective-permute-start.45) | collective-permute-done | bytes 1572896 | tf_op jit(solution)/shard_map/ppermute | solution.py:170
  683.9 20.1 %collective-permute-done.42 = bf16[384,2048]{1,0:T(8,128)(2,1)S(1)} collective-permute-done((bf16[384,2048]{1,0:T(8,128)(2,1)S(1)}, bf16[384,2048]{1,0:T(8,128)(2,1)S(1)}, u32[]{:S(2)}, u32[]{:S(2)}) %collective-permute-start.42) | collective-permute-done | bytes 1572896 | tf_op jit(solution)/shard_map/ppermute | solution.py:170
  712.7 11.1 add_convert_fusion.2
  729.3 8.9 convolution_convert_fusion.13
  752.5 11.3 collective-permute-done.53
  773.1 23.7 %collective-permute-done.49 = bf16[384,2048]{1,0:T(8,128)(2,1)} collective-permute-done((bf16[384,2048]{1,0:T(8,128)(2,1)}, bf16[384,2048]{1,0:T(8,128)(2,1)}, u32[]{:S(2)}, u32[]{:S(2)}) %collective-permute-start.49) | collective-permute-done | bytes 1572896 | tf_op jit(solution)/shard_map/ppermute | solution.py:170
  801.5 21.0 %collective-permute-done.52 = bf16[384,2048]{1,0:T(8,128)(2,1)} collective-permute-done((bf16[384,2048]{1,0:T(8,128)(2,1)S(1)}, bf16[384,2048]{1,0:T(8,128)(2,1)}, u32[]{:S(2)}, u32[]{:S(2)}) %collective-permute-start.52) | collective-permute-done | bytes 1572896 | tf_op jit(solution)/shard_map/ppermute | solution.py:170
  828.8 6.7 fusion.186
  853.3 9.2 convolution_convert_fusion.3
  862.5 23.5 %collective-permute-done.55 = bf16[384,2048]{1,0:T(8,128)(2,1)S(1)} collective-permute-done((bf16[384,2048]{1,0:T(8,128)(2,1)}, bf16[384,2048]{1,0:T(8,128)(2,1)S(1)}, u32[]{:S(2)}, u32[]{:S(2)}) %collective-permute-start.55) | collective-permute-done | bytes 1572896 | tf_op jit(solution)/shard_map/ppermute | solution.py:170
  887.1 6.8 dynamic-slice_bitcast_fusion.4
  903.4 6.3 fusion.62
  909.7 7.4 fusion.64
  917.3 21.2 %convolution_convert_fusion.12 = bf16[576,2048]{1,0:T(8,128)(2,1)} fusion(bf16[2048,2048]{1,0:T(8,128)(2,1)} %bitcast.104, bf16[576,1024]{1,0:T(8,128)(2,1)} %copy-done.184, bf16[576,1024]{1,0:T(8,128)(2,1)} %copy-done.183), kind=kOutput, calls=%fused_computation.190 | convolution fusion | flops 4837736448 | bytes 13107200 | tf_op jit(solution)/shard_map/rd,fd->rf/dot_general | solution.py:134
  938.5 10.1 convolution_convert_fusion.11
  966.3 21.6 %collective-permute-done.59 = bf16[384,2048]{1,0:T(8,128)(2,1)} collective-permute-done((bf16[384,2048]{1,0:T(8,128)(2,1)}, bf16[384,2048]{1,0:T(8,128)(2,1)}, u32[]{:S(2)}, u32[]{:S(2)}) %collective-permute-start.59) | collective-permute-done | bytes 1572896 | tf_op jit(solution)/shard_map/ppermute | solution.py:170
  1015.7 11.0 add_convert_fusion.1
  1033.3 10.1 convolution_convert_fusion.10
  1043.4 7.1 fusion.73
  1051.0 6.1 fusion.76
  1058.9 7.9 collective-permute-done.63
  1073.5 25.3 %collective-permute-done.62 = bf16[384,2048]{1,0:T(8,128)(2,1)S(1)} collective-permute-done((bf16[384,2048]{1,0:T(8,128)(2,1)S(1)}, bf16[384,2048]{1,0:T(8,128)(2,1)S(1)}, u32[]{:S(2)}, u32[]{:S(2)}) %collective-permute-start.62) | collective-permute-done | bytes 1572896 | tf_op jit(solution)/shard_map/ppermute | solution.py:170
  1099.6 12.4 collective-permute-done.68
  1112.3 9.2 convolution_convert_fusion.2
  1129.1 6.8 dynamic-slice_bitcast_fusion.2
  1146.9 13.4 collective-permute-start.71
  1180.6 6.2 collective-permute-done.74
  1215.5 11.1 add_convert_fusion
  1230.8 91.6 %collective-permute-done.81 = bf16[256,2048]{1,0:T(8,128)(2,1)} collective-permute-done((bf16[256,2048]{1,0:T(8,128)(2,1)}, bf16[256,2048]{1,0:T(8,128)(2,1)}, u32[]{:S(2)}, u32[]{:S(2)}) %collective-permute-start.81) | collective-permute-done | bytes 1048608 | tf_op jit(solution)/shard_map/ppermute | solution.py:61
  1328.1 50.8 %while.29 = (s32[]{:T(128)}, f32[1024,4,128]{0,2,1:T(8,128)S(1)}, f32[1024,4,128]{0,2,1:T(8,128)}, bf16[2,512,4,128]{3,1,2,0:T(8,128)(2,1)}, s32[2]{0:T(128)S(1)...) while((s32[]{:T(128)}, f32[1024,4,128]{0,2,1:T(8,128)S(1)}, ...), condition=%wide.region_26.27_spmd.clone, body=%wide.region_24.26_spmd.clone.sunk | while | flops 2719744000 | bytes 181490704 | solution.py:540
  1412.1 6.8 add_convert_fusion.4
  1431.7 11.6 fusion.173
  1444.1 11.1 convolution_convert_fusion
  1455.2 6.9 pad_maximum_fusion.1
  1489.8 17.8 %collective-permute-done.91 = bf16[256,2048]{1,0:T(8,128)(2,1)S(1)} collective-permute-done((bf16[256,2048]{1,0:T(8,128)(2,1)S(1)}, bf16[256,2048]{1,0:T(8,128)(2,1)S(1)}, u32[]{:S(2)}, u32[]{:S(2)}) %collective-permute-start.91) | collective-permute-done | bytes 1048608 | tf_op jit(solution)/shard_map/ppermute | solution.py:61
  1507.6 18.8 %collective-permute-done.92 = bf16[256,2048]{1,0:T(8,128)(2,1)S(1)} collective-permute-done((bf16[256,2048]{1,0:T(8,128)(2,1)S(1)}, bf16[256,2048]{1,0:T(8,128)(2,1)S(1)}, u32[]{:S(2)}, u32[]{:S(2)}) %collective-permute-start.92) | collective-permute-done | bytes 1048608 | tf_op jit(solution)/shard_map/ppermute | solution.py:61
  1526.4 20.2 %collective-permute-done.89 = bf16[384,2048]{1,0:T(8,128)(2,1)S(1)} collective-permute-done((bf16[384,2048]{1,0:T(8,128)(2,1)S(1)}, bf16[384,2048]{1,0:T(8,128)(2,1)S(1)}, u32[]{:S(2)}, u32[]{:S(2)}) %collective-permute-start.89) | collective-permute-done | bytes 1572896 | tf_op jit(solution)/shard_map/ppermute | solution.py:170
  1583.0 12.8 collective-permute-done.94
  1595.8 18.0 %collective-permute-done.95 = bf16[256,1664]{0,1:T(8,128)(2,1)} collective-permute-done((bf16[256,1664]{0,1:T(8,128)(2,1)}, bf16[256,1664]{0,1:T(8,128)(2,1)}, u32[]{:S(2)}, u32[]{:S(2)}) %collective-permute-start.95) | collective-permute-done | bytes 852000 | tf_op jit(solution)/shard_map/ppermute | solution.py:61
  1623.6 6.6 copy.311
  (946 shorter events, 701.1 us)
Async XLA Ops:
  7.2 89.4 %all-gather.3.cloned.1.call-start = ((), (), s32[]{:S(2)}) async-start(), calls=%async_computation.2 | async-start | bytes 7667712 | tf_op jit(solution)/shard_map/all_gather | solution.py:359
  24.2 115.4 %all-gather.5.cloned.1.call-start = ((), (), s32[]{:S(2)}) async-start(), calls=%async_computation.3 | async-start | bytes 2359296 | tf_op jit(solution)/shard_map/all_gather | solution.py:364
  27.3 47.2 %collective-permute-start.1 = (bf16[256,2048]{1,0:T(8,128)(2,1)S(1)}, bf16[256,2048]{1,0:T(8,128)(2,1)}, u32[]{:S(2)}, u32[]{:S(2)}) collective-permute-start(bf16[256,2048]{1,0:T(8,128)(2,1)S(1)} %bitcast.733), channel_id=1, source_target_pairs={{0,16},{8,24},{16,0},{24,8},{1,17},{9,25},{17,1},{25,9},{2,18},{10... | collective-permute-start | bytes 3145736 | tf_op jit(solution)/shard_map/ppermute | solution.py:61
  28.8 45.7 %collective-permute-start.2 = (bf16[256,2048]{1,0:T(8,128)(2,1)S(1)}, bf16[256,2048]{1,0:T(8,128)(2,1)}, u32[]{:S(2)}, u32[]{:S(2)}) collective-permute-start(bf16[256,2048]{1,0:T(8,128)(2,1)S(1)} %bitcast.734), channel_id=1, source_target_pairs={{0,24},{8,16},{16,8},{24,0},{1,25},{9,17},{17,9},{25,1},{2,26},{10... | collective-permute-start | bytes 3145736 | tf_op jit(solution)/shard_map/ppermute | solution.py:61
  29.8 1531.8 %reduce-scatter.5.cloned.1.call-start = ((), (), s32[]{:S(2)}) async-start(), calls=%async_computation.5 | async-start | bytes 2359296 | tf_op jit(solution)/shard_map/reduce_scatter | solution.py:594
  116.8 67.8 %collective-permute-start.3 = (bf16[384,2048]{1,0:T(8,128)(2,1)}, bf16[384,2048]{1,0:T(8,128)(2,1)}, u32[]{:S(2)}, u32[]{:S(2)}) collective-permute-start(bf16[384,2048]{1,0:T(8,128)(2,1)} %constant_dynamic-update-slice_fusion.10), channel_id=1, source_target_pairs={{0,2},{1,3},{2,4},{3,5},{4,6},{5,7},{8,10},{9,11},{10,12},{11,13},... | collective-permute-start | bytes 4718600 | tf_op jit(solution)/shard_map/ppermute | solution.py:170
  119.2 65.3 %collective-permute-start.4 = (bf16[384,2048]{1,0:T(8,128)(2,1)}, bf16[384,2048]{1,0:T(8,128)(2,1)}, u32[]{:S(2)}, u32[]{:S(2)}) collective-permute-start(bf16[384,2048]{1,0:T(8,128)(2,1)} %constant_dynamic-update-slice_fusion.10), channel_id=1, source_target_pairs={{6,4},{7,5},{4,2},{5,3},{2,0},{3,1},{14,12},{15,13},{12,10},{13,11... | collective-permute-start | bytes 4718600 | tf_op jit(solution)/shard_map/ppermute | solution.py:170
  130.4 47.9 %collective-permute-start.11 = (bf16[256,2048]{1,0:T(8,128)(2,1)}, bf16[256,2048]{1,0:T(8,128)(2,1)}, u32[]{:S(2)}, u32[]{:S(2)}) collective-permute-start(bf16[256,2048]{1,0:T(8,128)(2,1)} %bitcast.25), channel_id=1, source_target_pairs={{0,16},{8,24},{16,0},{24,8},{1,17},{9,25},{17,1},{25,9},{2,18},{10... | collective-permute-start | bytes 3145736 | tf_op jit(solution)/shard_map/ppermute | solution.py:61
  132.5 48.1 %collective-permute-start.12 = (bf16[256,2048]{1,0:T(8,128)(2,1)}, bf16[256,2048]{1,0:T(8,128)(2,1)}, u32[]{:S(2)}, u32[]{:S(2)}) collective-permute-start(bf16[256,2048]{1,0:T(8,128)(2,1)} %bitcast.25), channel_id=1, source_target_pairs={{0,24},{8,16},{16,8},{24,0},{1,25},{9,17},{17,9},{25,1},{2,26},{10... | collective-permute-start | bytes 3145736 | tf_op jit(solution)/shard_map/ppermute | solution.py:61
  154.7 67.5 %collective-permute-start.13 = (bf16[2048,512]{0,1:T(8,128)(2,1)}, bf16[2048,512]{0,1:T(8,128)(2,1)}, u32[]{:S(2)}, u32[]{:S(2)}) collective-permute-start(bf16[2048,512]{0,1:T(8,128)(2,1)} %all-gather.5.cloned.1.call-done), channel_id=1, source_target_pairs={{0,8},{8,0},{16,24},{24,16},{1,9},{9,1},{17,25},{25,17},{2,10},{10... | collective-permute-start | bytes 6291464 | tf_op jit(solution)/shard_map/ppermute | solution.py:61
  178.3 89.1 %collective-permute-start.14 = (bf16[2048,512]{0,1:T(8,128)(2,1)}, bf16[2048,512]{0,1:T(8,128)(2,1)}, u32[]{:S(2)}, u32[]{:S(2)}) collective-permute-start(bf16[2048,512]{0,1:T(8,128)(2,1)} %all-gather.5.cloned.1.call-done), channel_id=1, source_target_pairs={{0,16},{8,24},{16,0},{24,8},{1,17},{9,25},{17,1},{25,9},{2,18},{10... | collective-permute-start | bytes 6291464 | tf_op jit(solution)/shard_map/ppermute | solution.py:61
  180.6 86.7 %collective-permute-start.15 = (bf16[2048,512]{0,1:T(8,128)(2,1)}, bf16[2048,512]{0,1:T(8,128)(2,1)}, u32[]{:S(2)}, u32[]{:S(2)}) collective-permute-start(bf16[2048,512]{0,1:T(8,128)(2,1)} %all-gather.5.cloned.1.call-done), channel_id=1, source_target_pairs={{0,24},{8,16},{16,8},{24,0},{1,25},{9,17},{17,9},{25,1},{2,26},{10... | collective-permute-start | bytes 6291464 | tf_op jit(solution)/shard_map/ppermute | solution.py:61
  184.7 82.6 %collective-permute-start.8 = (bf16[384,2048]{1,0:T(8,128)(2,1)}, bf16[384,2048]{1,0:T(8,128)(2,1)}, u32[]{:S(2)}, u32[]{:S(2)}) collective-permute-start(bf16[384,2048]{1,0:T(8,128)(2,1)} %collective-permute-done.3), channel_id=1, source_target_pairs={{2,4},{3,5},{4,6},{5,7},{10,12},{11,13},{12,14},{13,15},{18,20},{1... | collective-permute-start | bytes 4718600 | tf_op jit(solution)/shard_map/ppermute | solution.py:170
  186.5 80.8 %collective-permute-start.9 = (bf16[384,2048]{1,0:T(8,128)(2,1)}, bf16[384,2048]{1,0:T(8,128)(2,1)}, u32[]{:S(2)}, u32[]{:S(2)}) collective-permute-start(bf16[384,2048]{1,0:T(8,128)(2,1)} %collective-permute-done.4), channel_id=1, source_target_pairs={{4,2},{5,3},{2,0},{3,1},{12,10},{13,11},{10,8},{11,9},{20,18},{21,... | collective-permute-start | bytes 4718600 | tf_op jit(solution)/shard_map/ppermute | solution.py:170
  315.5 68.0 %collective-permute-start.21 = (bf16[4,384,2048]{2,1,0:T(8,128)(2,1)}, bf16[4,384,2048]{2,1,0:T(8,128)(2,1)}, u32[]{:S(2)}, u32[]{:S(2)}) collective-permute-start(bf16[4,384,2048]{2,1,0:T(8,128)(2,1)} %bitcast_dynamic-update-slice_fusion.25), channel_id=1, source_target_pairs={{0,1},{1,0},{2,3},{3,2},{4,5},{5,4},{6,7},{7,6},{8,9},{9,8},{10,11... | collective-permute-start | bytes 18874376 | tf_op jit(solution)/shard_map/ppermute | solution.py:175
  331.6 46.0 %collective-permute-start.25 = (bf16[256,2048]{1,0:T(8,128)(2,1)S(1)}, bf16[256,2048]{1,0:T(8,128)(2,1)S(1)}, u32[]{:S(2)}, u32[]{:S(2)}) collective-permute-start(bf16[256,2048]{1,0:T(8,128)(2,1)S(1)} %multiply_convert_fusion.17), channel_id=1, source_target_pairs={{0,16},{8,24},{16,0},{24,8},{1,17},{9,25},{17,1},{25,9},{2,18},{10... | collective-permute-start | bytes 3145736 | tf_op jit(solution)/shard_map/ppermute | solution.py:61
  333.1 47.9 %collective-permute-start.22 = (bf16[384,2048]{1,0:T(8,128)(2,1)S(1)}, bf16[384,2048]{1,0:T(8,128)(2,1)S(1)}, u32[]{:S(2)}, u32[]{:S(2)}) collective-permute-start(bf16[384,2048]{1,0:T(8,128)(2,1)S(1)} %constant_dynamic-update-slice_fusion.12), channel_id=1, source_target_pairs={{0,2},{1,3},{2,4},{3,5},{4,6},{5,7},{8,10},{9,11},{10,12},{11,13},... | collective-permute-start | bytes 4718600 | tf_op jit(solution)/shard_map/ppermute | solution.py:170
  334.5 47.7 %collective-permute-start.23 = (bf16[384,2048]{1,0:T(8,128)(2,1)S(1)}, bf16[384,2048]{1,0:T(8,128)(2,1)S(1)}, u32[]{:S(2)}, u32[]{:S(2)}) collective-permute-start(bf16[384,2048]{1,0:T(8,128)(2,1)S(1)} %constant_dynamic-update-slice_fusion.12), channel_id=1, source_target_pairs={{6,4},{7,5},{4,2},{5,3},{2,0},{3,1},{14,12},{15,13},{12,10},{13,11... | collective-permute-start | bytes 4718600 | tf_op jit(solution)/shard_map/ppermute | solution.py:170
  388.7 36.1 %collective-permute-start.28 = (bf16[384,2048]{1,0:T(8,128)(2,1)}, bf16[384,2048]{1,0:T(8,128)(2,1)S(1)}, u32[]{:S(2)}, u32[]{:S(2)}) collective-permute-start(bf16[384,2048]{1,0:T(8,128)(2,1)} %copy-done.100), channel_id=1, source_target_pairs={{4,2},{5,3},{2,0},{3,1},{12,10},{13,11},{10,8},{11,9},{20,18},{21,... | collective-permute-start | bytes 4718600 | tf_op jit(solution)/shard_map/ppermute | solution.py:170
  484.9 51.0 %collective-permute-start.37 = (bf16[4,384,2048]{2,1,0:T(8,128)(2,1)}, bf16[4,384,2048]{2,1,0:T(8,128)(2,1)}, u32[]{:S(2)}, u32[]{:S(2)}) collective-permute-start(bf16[4,384,2048]{2,1,0:T(8,128)(2,1)} %pad_maximum_fusion.2), channel_id=1, source_target_pairs={{0,1},{1,0},{2,3},{3,2},{4,5},{5,4},{6,7},{7,6},{8,9},{9,8},{10,11... | collective-permute-start | bytes 18874376 | tf_op jit(solution)/shard_map/ppermute | solution.py:175
  488.9 47.0 %collective-permute-start.34 = (bf16[4,384,2048]{2,1,0:T(8,128)(2,1)}, bf16[4,384,2048]{2,1,0:T(8,128)(2,1)}, u32[]{:S(2)}, u32[]{:S(2)}) collective-permute-start(bf16[4,384,2048]{2,1,0:T(8,128)(2,1)} %bitcast_dynamic-update-slice_fusion.20), channel_id=1, source_target_pairs={{0,1},{1,0},{2,3},{3,2},{4,5},{5,4},{6,7},{7,6},{8,9},{9,8},{10,11... | collective-permute-start | bytes 18874376 | tf_op jit(solution)/shard_map/ppermute | solution.py:175
  497.7 38.2 %collective-permute-start.36 = (bf16[384,2048]{1,0:T(8,128)(2,1)S(1)}, bf16[384,2048]{1,0:T(8,128)(2,1)S(1)}, u32[]{:S(2)}, u32[]{:S(2)}) collective-permute-start(bf16[384,2048]{1,0:T(8,128)(2,1)S(1)} %constant_dynamic-update-slice_fusion.14), channel_id=1, source_target_pairs={{6,4},{7,5},{4,2},{5,3},{2,0},{3,1},{14,12},{15,13},{12,10},{13,11... | collective-permute-start | bytes 4718600 | tf_op jit(solution)/shard_map/ppermute | solution.py:170
  561.7 37.3 %collective-permute-start.39 = (bf16[384,2048]{1,0:T(8,128)(2,1)S(1)}, bf16[384,2048]{1,0:T(8,128)(2,1)S(1)}, u32[]{:S(2)}, u32[]{:S(2)}) collective-permute-start(bf16[384,2048]{1,0:T(8,128)(2,1)S(1)} %copy-done.87), channel_id=1, source_target_pairs={{4,2},{5,3},{2,0},{3,1},{12,10},{13,11},{10,8},{11,9},{20,18},{21,... | collective-permute-start | bytes 4718600 | tf_op jit(solution)/shard_map/ppermute | solution.py:170
  612.0 91.9 %collective-permute-start.47 = (bf16[4,384,2048]{2,1,0:T(8,128)(2,1)}, bf16[4,384,2048]{2,1,0:T(8,128)(2,1)}, u32[]{:S(2)}, u32[]{:S(2)}) collective-permute-start(bf16[4,384,2048]{2,1,0:T(8,128)(2,1)} %pad_maximum_fusion.3), channel_id=1, source_target_pairs={{0,1},{1,0},{2,3},{3,2},{4,5},{5,4},{6,7},{7,6},{8,9},{9,8},{10,11... | collective-permute-start | bytes 18874376 | tf_op jit(solution)/shard_map/ppermute | solution.py:175
  612.0 38.7 %collective-permute-start.43 = (bf16[384,2048]{1,0:T(8,128)(2,1)}, bf16[384,2048]{1,0:T(8,128)(2,1)}, u32[]{:S(2)}, u32[]{:S(2)}) collective-permute-start(bf16[384,2048]{1,0:T(8,128)(2,1)} %get-tuple-element.762), channel_id=1, source_target_pairs={{0,2},{1,3},{6,4},{7,5},{8,10},{9,11},{14,12},{15,13},{16,18},{17,... | collective-permute-start | bytes 4718600 | tf_op jit(solution)/shard_map/ppermute | solution.py:170
  630.2 53.7 %collective-permute-start.45 = (bf16[384,2048]{1,0:T(8,128)(2,1)S(1)}, bf16[384,2048]{1,0:T(8,128)(2,1)S(1)}, u32[]{:S(2)}, u32[]{:S(2)}) collective-permute-start(bf16[384,2048]{1,0:T(8,128)(2,1)S(1)} %constant_dynamic-update-slice_fusion.16), channel_id=1, source_target_pairs={{0,2},{1,3},{2,4},{3,5},{4,6},{5,7},{8,10},{9,11},{10,12},{11,13},... | collective-permute-start | bytes 4718600 | tf_op jit(solution)/shard_map/ppermute | solution.py:170
  631.8 52.1 %collective-permute-start.46 = (bf16[384,2048]{1,0:T(8,128)(2,1)S(1)}, bf16[384,2048]{1,0:T(8,128)(2,1)S(1)}, u32[]{:S(2)}, u32[]{:S(2)}) collective-permute-start(bf16[384,2048]{1,0:T(8,128)(2,1)S(1)} %constant_dynamic-update-slice_fusion.16), channel_id=1, source_target_pairs={{6,4},{7,5},{4,2},{5,3},{2,0},{3,1},{14,12},{15,13},{12,10},{13,11... | collective-permute-start | bytes 4718600 | tf_op jit(solution)/shard_map/ppermute | solution.py:170
  651.5 52.4 %collective-permute-start.42 = (bf16[384,2048]{1,0:T(8,128)(2,1)S(1)}, bf16[384,2048]{1,0:T(8,128)(2,1)S(1)}, u32[]{:S(2)}, u32[]{:S(2)}) collective-permute-start(bf16[384,2048]{1,0:T(8,128)(2,1)S(1)} %copy-done.96), channel_id=1, source_target_pairs={{2,0},{3,1},{10,8},{11,9},{18,16},{19,17},{26,24},{27,25}} | collective-permute-start | bytes 4718600 | tf_op jit(solution)/shard_map/ppermute | solution.py:170
  706.0 116.5 %collective-permute-start.48 = (bf16[4,384,2048]{2,1,0:T(8,128)(2,1)}, bf16[4,384,2048]{2,1,0:T(8,128)(2,1)}, u32[]{:S(2)}, u32[]{:S(2)}) collective-permute-start(bf16[4,384,2048]{2,1,0:T(8,128)(2,1)} %bitcast_dynamic-update-slice_fusion.17), channel_id=1, source_target_pairs={{0,1},{1,0},{2,3},{3,2},{4,5},{5,4},{6,7},{7,6},{8,9},{9,8},{10,11... | collective-permute-start | bytes 18874376 | tf_op jit(solution)/shard_map/ppermute | solution.py:175
  727.4 36.4 %collective-permute-start.53 = (bf16[384,2048]{1,0:T(8,128)(2,1)S(1)}, bf16[384,2048]{1,0:T(8,128)(2,1)S(1)}, u32[]{:S(2)}, u32[]{:S(2)}) collective-permute-start(bf16[384,2048]{1,0:T(8,128)(2,1)S(1)} %get-tuple-element.761), channel_id=1, source_target_pairs={{0,2},{1,3},{6,4},{7,5},{8,10},{9,11},{14,12},{15,13},{16,18},{17,... | collective-permute-start | bytes 4718600 | tf_op jit(solution)/shard_map/ppermute | solution.py:170
  748.0 48.8 %collective-permute-start.49 = (bf16[384,2048]{1,0:T(8,128)(2,1)}, bf16[384,2048]{1,0:T(8,128)(2,1)}, u32[]{:S(2)}, u32[]{:S(2)}) collective-permute-start(bf16[384,2048]{1,0:T(8,128)(2,1)} %get-tuple-element.731), channel_id=1, source_target_pairs={{0,2},{1,3},{2,4},{3,5},{4,6},{5,7},{8,10},{9,11},{10,12},{11,13},... | collective-permute-start | bytes 4718600 | tf_op jit(solution)/shard_map/ppermute | solution.py:170
  750.4 51.1 %collective-permute-start.50 = (bf16[384,2048]{1,0:T(8,128)(2,1)}, bf16[384,2048]{1,0:T(8,128)(2,1)}, u32[]{:S(2)}, u32[]{:S(2)}) collective-permute-start(bf16[384,2048]{1,0:T(8,128)(2,1)} %get-tuple-element.730), channel_id=1, source_target_pairs={{6,4},{7,5},{4,2},{5,3},{2,0},{3,1},{14,12},{15,13},{12,10},{13,11... | collective-permute-start | bytes 4718600 | tf_op jit(solution)/shard_map/ppermute | solution.py:170
  751.7 49.8 %collective-permute-start.51 = (bf16[384,2048]{1,0:T(8,128)(2,1)S(1)}, bf16[384,2048]{1,0:T(8,128)(2,1)S(1)}, u32[]{:S(2)}, u32[]{:S(2)}) collective-permute-start(bf16[384,2048]{1,0:T(8,128)(2,1)S(1)} %copy-done.42), channel_id=1, source_target_pairs={{2,4},{3,5},{4,6},{5,7},{10,12},{11,13},{12,14},{13,15},{18,20},{1... | collective-permute-start | bytes 4718600 | tf_op jit(solution)/shard_map/ppermute | solution.py:170
  763.8 58.7 %collective-permute-start.52 = (bf16[384,2048]{1,0:T(8,128)(2,1)S(1)}, bf16[384,2048]{1,0:T(8,128)(2,1)}, u32[]{:S(2)}, u32[]{:S(2)}) collective-permute-start(bf16[384,2048]{1,0:T(8,128)(2,1)S(1)} %copy-done.90), channel_id=1, source_target_pairs={{4,2},{5,3},{2,0},{3,1},{12,10},{13,11},{10,8},{11,9},{20,18},{21,... | collective-permute-start | bytes 4718600 | tf_op jit(solution)/shard_map/ppermute | solution.py:170
  796.8 65.7 %collective-permute-start.56 = (bf16[384,2048]{1,0:T(8,128)(2,1)}, bf16[384,2048]{1,0:T(8,128)(2,1)S(1)}, u32[]{:S(2)}, u32[]{:S(2)}) collective-permute-start(bf16[384,2048]{1,0:T(8,128)(2,1)} %get-tuple-element.760), channel_id=1, source_target_pairs={{0,2},{1,3},{6,4},{7,5},{8,10},{9,11},{14,12},{15,13},{16,18},{17,... | collective-permute-start | bytes 4718600 | tf_op jit(solution)/shard_map/ppermute | solution.py:170
  848.5 37.5 %collective-permute-start.55 = (bf16[384,2048]{1,0:T(8,128)(2,1)}, bf16[384,2048]{1,0:T(8,128)(2,1)S(1)}, u32[]{:S(2)}, u32[]{:S(2)}) collective-permute-start(bf16[384,2048]{1,0:T(8,128)(2,1)} %collective-permute-done.52), channel_id=1, source_target_pairs={{2,0},{3,1},{10,8},{11,9},{18,16},{19,17},{26,24},{27,25}} | collective-permute-start | bytes 4718600 | tf_op jit(solution)/shard_map/ppermute | solution.py:170
  898.9 94.2 %collective-permute-start.61 = (bf16[4,384,2048]{2,1,0:T(8,128)(2,1)}, bf16[4,384,2048]{2,1,0:T(8,128)(2,1)}, u32[]{:S(2)}, u32[]{:S(2)}) collective-permute-start(bf16[4,384,2048]{2,1,0:T(8,128)(2,1)} %pad_maximum_fusion.4), channel_id=1, source_target_pairs={{0,1},{1,0},{2,3},{3,2},{4,5},{5,4},{6,7},{7,6},{8,9},{9,8},{10,11... | collective-permute-start | bytes 18874376 | tf_op jit(solution)/shard_map/ppermute | solution.py:175
  903.0 90.1 %collective-permute-start.58 = (bf16[4,384,2048]{2,1,0:T(8,128)(2,1)}, bf16[4,384,2048]{2,1,0:T(8,128)(2,1)}, u32[]{:S(2)}, u32[]{:S(2)}) collective-permute-start(bf16[4,384,2048]{2,1,0:T(8,128)(2,1)} %bitcast_dynamic-update-slice_fusion.13), channel_id=1, source_target_pairs={{0,1},{1,0},{2,3},{3,2},{4,5},{5,4},{6,7},{7,6},{8,9},{9,8},{10,11... | collective-permute-start | bytes 18874376 | tf_op jit(solution)/shard_map/ppermute | solution.py:175
  954.4 38.7 %collective-permute-start.60 = (bf16[384,2048]{1,0:T(8,128)(2,1)}, bf16[384,2048]{1,0:T(8,128)(2,1)}, u32[]{:S(2)}, u32[]{:S(2)}) collective-permute-start(bf16[384,2048]{1,0:T(8,128)(2,1)} %get-tuple-element.728), channel_id=1, source_target_pairs={{6,4},{7,5},{4,2},{5,3},{2,0},{3,1},{14,12},{15,13},{12,10},{13,11... | collective-permute-start | bytes 4718600 | tf_op jit(solution)/shard_map/ppermute | solution.py:170
  1030.3 36.5 %collective-permute-start.63 = (bf16[384,2048]{1,0:T(8,128)(2,1)}, bf16[384,2048]{1,0:T(8,128)(2,1)S(1)}, u32[]{:S(2)}, u32[]{:S(2)}) collective-permute-start(bf16[384,2048]{1,0:T(8,128)(2,1)} %get-tuple-element.758), channel_id=1, source_target_pairs={{0,2},{1,3},{6,4},{7,5},{8,10},{9,11},{14,12},{15,13},{16,18},{17,... | collective-permute-start | bytes 4718600 | tf_op jit(solution)/shard_map/ppermute | solution.py:170
  1031.8 67.1 %collective-permute-start.62 = (bf16[384,2048]{1,0:T(8,128)(2,1)S(1)}, bf16[384,2048]{1,0:T(8,128)(2,1)S(1)}, u32[]{:S(2)}, u32[]{:S(2)}) collective-permute-start(bf16[384,2048]{1,0:T(8,128)(2,1)S(1)} %get-tuple-element.759), channel_id=1, source_target_pairs={{0,2},{1,3},{6,4},{7,5},{8,10},{9,11},{14,12},{15,13},{16,18},{17,... | collective-permute-start | bytes 4718600 | tf_op jit(solution)/shard_map/ppermute | solution.py:170
  1067.2 59.6 %collective-permute-start.65 = (bf16[256,2048]{1,0:T(8,128)(2,1)S(1)}, bf16[256,2048]{1,0:T(8,128)(2,1)S(1)}, u32[]{:S(2)}, u32[]{:S(2)}) collective-permute-start(bf16[256,2048]{1,0:T(8,128)(2,1)S(1)} %get-tuple-element.782), channel_id=1, source_target_pairs={{0,8},{8,0},{16,24},{24,16},{1,9},{9,1},{17,25},{25,17},{2,10},{10... | collective-permute-start | bytes 3145736 | tf_op jit(solution)/shard_map/ppermute | solution.py:61
  1067.8 59.1 %collective-permute-start.66 = (bf16[256,2048]{1,0:T(8,128)(2,1)S(1)}, bf16[256,2048]{1,0:T(8,128)(2,1)S(1)}, u32[]{:S(2)}, u32[]{:S(2)}) collective-permute-start(bf16[256,2048]{1,0:T(8,128)(2,1)S(1)} %get-tuple-element.781), channel_id=1, source_target_pairs={{0,16},{8,24},{16,0},{24,8},{1,17},{9,25},{17,1},{25,9},{2,18},{10... | collective-permute-start | bytes 3145736 | tf_op jit(solution)/shard_map/ppermute | solution.py:61
  1068.7 58.3 %collective-permute-start.67 = (bf16[256,2048]{1,0:T(8,128)(2,1)S(1)}, bf16[256,2048]{1,0:T(8,128)(2,1)S(1)}, u32[]{:S(2)}, u32[]{:S(2)}) collective-permute-start(bf16[256,2048]{1,0:T(8,128)(2,1)S(1)} %get-tuple-element.780), channel_id=1, source_target_pairs={{0,24},{8,16},{16,8},{24,0},{1,25},{9,17},{17,9},{25,1},{2,26},{10... | collective-permute-start | bytes 3145736 | tf_op jit(solution)/shard_map/ppermute | solution.py:61
  1070.8 41.2 %collective-permute-start.68 = (f32[4,256]{1,0:T(4,128)S(1)}, f32[4,256]{1,0:T(4,128)S(1)}, u32[]{:S(2)}, u32[]{:S(2)}) collective-permute-start(f32[4,256]{1,0:T(4,128)S(1)} %get-tuple-element.842), channel_id=1, source_target_pairs={{0,8},{8,0},{16,24},{24,16},{1,9},{9,1},{17,25},{25,17},{2,10},{10... | collective-permute-start | bytes 12296 | tf_op jit(solution)/shard_map/ppermute | solution.py:61
  1141.0 59.7 %collective-permute-start.73 = (bf16[4,384,2048]{2,1,0:T(8,128)(2,1)}, bf16[4,384,2048]{2,1,0:T(8,128)(2,1)}, u32[]{:S(2)}, u32[]{:S(2)}) collective-permute-start(bf16[4,384,2048]{2,1,0:T(8,128)(2,1)} %pad_maximum_fusion.5), channel_id=1, source_target_pairs={{0,1},{1,0},{2,3},{3,2},{4,5},{5,4},{6,7},{7,6},{8,9},{9,8},{10,11... | collective-permute-start | bytes 18874376 | tf_op jit(solution)/shard_map/ppermute | solution.py:175
  1146.9 53.8 %collective-permute-start.71 = (bf16[384,2048]{1,0:T(8,128)(2,1)}, bf16[384,2048]{1,0:T(8,128)(2,1)}, u32[]{:S(2)}, u32[]{:S(2)}) collective-permute-start(bf16[384,2048]{1,0:T(8,128)(2,1)} %get-tuple-element.727), channel_id=1, source_target_pairs={{0,2},{1,3},{2,4},{3,5},{4,6},{5,7},{8,10},{9,11},{10,12},{11,13},... | collective-permute-start | bytes 4718600 | tf_op jit(solution)/shard_map/ppermute | solution.py:170
  1160.3 40.4 %collective-permute-start.72 = (bf16[384,2048]{1,0:T(8,128)(2,1)}, bf16[384,2048]{1,0:T(8,128)(2,1)}, u32[]{:S(2)}, u32[]{:S(2)}) collective-permute-start(bf16[384,2048]{1,0:T(8,128)(2,1)} %get-tuple-element.726), channel_id=1, source_target_pairs={{6,4},{7,5},{4,2},{5,3},{2,0},{3,1},{14,12},{15,13},{12,10},{13,11... | collective-permute-start | bytes 4718600 | tf_op jit(solution)/shard_map/ppermute | solution.py:170
  1208.5 176.9 %collective-permute-start.78 = (bf16[2048,512]{0,1:T(8,128)(2,1)}, bf16[2048,512]{0,1:T(8,128)(2,1)}, u32[]{:S(2)}, u32[]{:S(2)}) collective-permute-start(bf16[2048,512]{0,1:T(8,128)(2,1)} %get-tuple-element.736), channel_id=1, source_target_pairs={{0,8},{8,0},{16,24},{24,16},{1,9},{9,1},{17,25},{25,17},{2,10},{10... | collective-permute-start | bytes 6291464 | tf_op jit(solution)/shard_map/ppermute | solution.py:61
  1209.0 176.4 %collective-permute-start.79 = (bf16[2048,512]{0,1:T(8,128)(2,1)}, bf16[2048,512]{0,1:T(8,128)(2,1)}, u32[]{:S(2)}, u32[]{:S(2)}) collective-permute-start(bf16[2048,512]{0,1:T(8,128)(2,1)} %get-tuple-element.735), channel_id=1, source_target_pairs={{0,16},{8,24},{16,0},{24,8},{1,17},{9,25},{17,1},{25,9},{2,18},{10... | collective-permute-start | bytes 6291464 | tf_op jit(solution)/shard_map/ppermute | solution.py:61
  1209.9 175.5 %collective-permute-start.80 = (bf16[2048,512]{0,1:T(8,128)(2,1)}, bf16[2048,512]{0,1:T(8,128)(2,1)}, u32[]{:S(2)}, u32[]{:S(2)}) collective-permute-start(bf16[2048,512]{0,1:T(8,128)(2,1)} %get-tuple-element.734), channel_id=1, source_target_pairs={{0,24},{8,16},{16,8},{24,0},{1,25},{9,17},{17,9},{25,1},{2,26},{10... | collective-permute-start | bytes 6291464 | tf_op jit(solution)/shard_map/ppermute | solution.py:61
  1214.2 108.2 %collective-permute-start.81 = (bf16[256,2048]{1,0:T(8,128)(2,1)}, bf16[256,2048]{1,0:T(8,128)(2,1)}, u32[]{:S(2)}, u32[]{:S(2)}) collective-permute-start(bf16[256,2048]{1,0:T(8,128)(2,1)} %get-tuple-element.776), channel_id=1, source_target_pairs={{0,8},{8,0},{16,24},{24,16},{1,9},{9,1},{17,25},{25,17},{2,10},{10... | collective-permute-start | bytes 3145736 | tf_op jit(solution)/shard_map/ppermute | solution.py:61
  1214.6 112.7 %collective-permute-start.82 = (bf16[256,2048]{1,0:T(8,128)(2,1)}, bf16[256,2048]{1,0:T(8,128)(2,1)}, u32[]{:S(2)}, u32[]{:S(2)}) collective-permute-start(bf16[256,2048]{1,0:T(8,128)(2,1)} %get-tuple-element.775), channel_id=1, source_target_pairs={{0,16},{8,24},{16,0},{24,8},{1,17},{9,25},{17,1},{25,9},{2,18},{10... | collective-permute-start | bytes 3145736 | tf_op jit(solution)/shard_map/ppermute | solution.py:61
  1322.4 62.9 %collective-permute-start.77 = (bf16[384,2048]{1,0:T(8,128)(2,1)}, bf16[384,2048]{1,0:T(8,128)(2,1)}, u32[]{:S(2)}, u32[]{:S(2)}) collective-permute-start(bf16[384,2048]{1,0:T(8,128)(2,1)} %get-tuple-element.757), channel_id=1, source_target_pairs={{0,2},{1,3},{6,4},{7,5},{8,10},{9,11},{14,12},{15,13},{16,18},{17,... | collective-permute-start | bytes 4718600 | tf_op jit(solution)/shard_map/ppermute | solution.py:170
  1327.3 55.6 %collective-permute-start.83 = (bf16[256,2048]{1,0:T(8,128)(2,1)}, bf16[256,2048]{1,0:T(8,128)(2,1)}, u32[]{:S(2)}, u32[]{:S(2)}) collective-permute-start(bf16[256,2048]{1,0:T(8,128)(2,1)} %get-tuple-element.774), channel_id=1, source_target_pairs={{0,24},{8,16},{16,8},{24,0},{1,25},{9,17},{17,9},{25,1},{2,26},{10... | collective-permute-start | bytes 3145736 | tf_op jit(solution)/shard_map/ppermute | solution.py:61
  1382.9 79.2 %collective-permute-start.84 = (bf16[384,2048]{1,0:T(8,128)(2,1)}, bf16[384,2048]{1,0:T(8,128)(2,1)}, u32[]{:S(2)}, u32[]{:S(2)}) collective-permute-start(bf16[384,2048]{1,0:T(8,128)(2,1)} %get-tuple-element.756), channel_id=1, source_target_pairs={{0,2},{1,3},{6,4},{7,5},{8,10},{9,11},{14,12},{15,13},{16,18},{17,... | collective-permute-start | bytes 4718600 | tf_op jit(solution)/shard_map/ppermute | solution.py:170
  1406.3 55.9 %collective-permute-start.85 = (bf16[384,2048]{1,0:T(8,128)(2,1)}, bf16[384,2048]{1,0:T(8,128)(2,1)}, u32[]{:S(2)}, u32[]{:S(2)}) collective-permute-start(bf16[384,2048]{1,0:T(8,128)(2,1)} %fusion.84), channel_id=1, source_target_pairs={{2,4},{3,5},{4,2},{5,3},{10,12},{11,13},{12,10},{13,11},{18,20},{1... | collective-permute-start | bytes 4718600 | tf_op jit(solution)/shard_map/ppermute | solution.py:170
  1418.9 151.4 %reduce-scatter.3.cloned.1.call-start = ((), (), s32[]{:S(2)}) async-start(), calls=%async_computation.4 | async-start | bytes 7667712 | tf_op jit(solution)/shard_map/reduce_scatter | solution.py:593
  1478.3 68.3 %collective-permute-start.89 = (bf16[384,2048]{1,0:T(8,128)(2,1)S(1)}, bf16[384,2048]{1,0:T(8,128)(2,1)S(1)}, u32[]{:S(2)}, u32[]{:S(2)}) collective-permute-start(bf16[384,2048]{1,0:T(8,128)(2,1)S(1)} %get-tuple-element.725), channel_id=1, source_target_pairs={{0,2},{1,3},{2,4},{3,5},{4,6},{5,7},{8,10},{9,11},{10,12},{11,13},... | collective-permute-start | bytes 4718600 | tf_op jit(solution)/shard_map/ppermute | solution.py:170
  1479.7 71.4 %collective-permute-start.90 = (bf16[384,2048]{1,0:T(8,128)(2,1)S(1)}, bf16[384,2048]{1,0:T(8,128)(2,1)S(1)}, u32[]{:S(2)}, u32[]{:S(2)}) collective-permute-start(bf16[384,2048]{1,0:T(8,128)(2,1)S(1)} %get-tuple-element.724), channel_id=1, source_target_pairs={{6,4},{7,5},{4,2},{5,3},{2,0},{3,1},{14,12},{15,13},{12,10},{13,11... | collective-permute-start | bytes 4718600 | tf_op jit(solution)/shard_map/ppermute | solution.py:170
  1482.7 43.7 %collective-permute-start.92 = (bf16[256,2048]{1,0:T(8,128)(2,1)S(1)}, bf16[256,2048]{1,0:T(8,128)(2,1)S(1)}, u32[]{:S(2)}, u32[]{:S(2)}) collective-permute-start(bf16[256,2048]{1,0:T(8,128)(2,1)S(1)} %get-tuple-element.771), channel_id=1, source_target_pairs={{0,16},{8,24},{16,0},{24,8},{1,17},{9,25},{17,1},{25,9},{2,18},{10... | collective-permute-start | bytes 3145736 | tf_op jit(solution)/shard_map/ppermute | solution.py:61
  1484.4 42.0 %collective-permute-start.93 = (bf16[256,2048]{1,0:T(8,128)(2,1)S(1)}, bf16[256,2048]{1,0:T(8,128)(2,1)S(1)}, u32[]{:S(2)}, u32[]{:S(2)}) collective-permute-start(bf16[256,2048]{1,0:T(8,128)(2,1)S(1)} %get-tuple-element.770), channel_id=1, source_target_pairs={{0,24},{8,16},{16,8},{24,0},{1,25},{9,17},{17,9},{25,1},{2,26},{10... | collective-permute-start | bytes 3145736 | tf_op jit(solution)/shard_map/ppermute | solution.py:61
  1572.4 41.4 %collective-permute-start.95 = (bf16[256,1664]{0,1:T(8,128)(2,1)}, bf16[256,1664]{0,1:T(8,128)(2,1)}, u32[]{:S(2)}, u32[]{:S(2)}) collective-permute-start(bf16[256,1664]{0,1:T(8,128)(2,1)} %reduce-scatter.3.cloned.1.call-done), channel_id=1, source_target_pairs={{0,16},{8,24},{16,0},{24,8},{1,17},{9,25},{17,1},{25,9},{2,18},{10... | collective-permute-start | bytes 2555912 | tf_op jit(solution)/shard_map/ppermute | solution.py:61
  1574.0 39.8 %collective-permute-start.96 = (bf16[256,1664]{0,1:T(8,128)(2,1)}, bf16[256,1664]{0,1:T(8,128)(2,1)}, u32[]{:S(2)}, u32[]{:S(2)}) collective-permute-start(bf16[256,1664]{0,1:T(8,128)(2,1)} %reduce-scatter.3.cloned.1.call-done), channel_id=1, source_target_pairs={{0,24},{8,16},{16,8},{24,0},{1,25},{9,17},{17,9},{25,1},{2,26},{10... | collective-permute-start | bytes 2555912 | tf_op jit(solution)/shard_map/ppermute | solution.py:61
  (249 other events, 4594.6 us)
Sparse Core Ops, SparseCore 0:
  24.4 72.2 all-gather.2
  98.2 30.8 all-gather.4
  1419.0 36.3 reduce-scatter.4
  1462.3 106.6 reduce-scatter.2

commit v3 on v2

--- a/solution.py
+++ b/solution.py
@@ -162,150 +162,22 @@
     return (grad_gate_up, grad_down)
 
 
-LINE = 4
-
-
-def along(values, hops):
-    pairs = [(2 * source + core, 2 * target + core) for source, target in hops for core in range(2)]
-    return lax.ppermute(values, "fsdp", pairs)
-
-
-def swap_cores(values):
+def after(values, *earlier):
+    return lax.optimization_barrier((values, earlier))[0]
+
+
+def split_rows(stacked, up_rows):
     count = lax.axis_size("fsdp")
-    return lax.ppermute(values, "fsdp", [(index, index ^ 1) for index in range(count)])
-
-
-def place_block(buffer, block, chip, core):
-    return lax.dynamic_update_slice(buffer, block[None, None], (chip, core, 0, 0))
-
-
-def place_side(buffer, side, core):
-    return lax.dynamic_update_slice(buffer, side[:, None], (0, core, 0, 0))
-
-
-def line_gather(gate_up, down):
-    index = lax.axis_index("fsdp")
-    chip, core = index // 2, index % 2
-    up_rows, width = gate_up.shape
-    own = jnp.concatenate([gate_up, down], axis=0)
-    right, left = yield (
-        along(own, [(0, 1), (1, 2), (2, 3)]),
-        along(own, [(3, 2), (2, 1), (1, 0)]),
-    )
-    right_two, left_two = yield (
-        along(right, [(1, 2), (2, 3)]),
-        along(left, [(2, 1), (1, 0)]),
-    )
-    right_three, left_three = yield (along(right_two, [(2, 3)]), along(left_two, [(1, 0)]))
-    near = jnp.where(chip < 3, left, right)
-    middle = jnp.where(chip < 2, left_two, right_two)
-    far = jnp.where(chip == 0, left_three, jnp.where(chip == 3, right_three, right))
-    near_chip = jnp.where(chip < 3, chip + 1, 2)
-    far_chip = jnp.where(chip == 0, 3, jnp.where(chip == 3, 0, chip - 1))
-    side = jnp.zeros((LINE,) + own.shape, own.dtype)
-    for block, place in ((own, chip), (near, near_chip), (middle, (chip + 2) % 4), (far, far_chip)):
-        side = lax.dynamic_update_slice(side, block[None], (place, 0, 0))
-    other = yield swap_cores(side)
-    sides = []
-    for start, stop in ((0, up_rows), (up_rows, own.shape[0])):
-        buffer = jnp.zeros((LINE, 2, stop - start, width), own.dtype)
-        buffer = place_side(buffer, side[:, start:stop], core)
-        buffer = place_side(buffer, other[:, start:stop], 1 - core)
-        sides.append(buffer.reshape(-1, width))
-    return tuple(sides)
-
-
-def line_scatter(gate_up, down):
-    f32 = jnp.float32
-    index = lax.axis_index("fsdp")
-    chip, core = index // 2, index % 2
-    width = gate_up.shape[1]
-    shaped = [grad.reshape(LINE, 2, -1, width) for grad in (gate_up, down)]
-    up_rows = shaped[0].shape[2]
-
-    def side(number):
-        return jnp.concatenate(
-            [lax.dynamic_index_in_dim(grad, number, 1, False) for grad in shaped], axis=1
-        )
-
-    got = yield swap_cores(side(1 - core))
-    part = (side(core).astype(f32) + got.astype(f32)).astype(jnp.bfloat16)
-
-    def take(place, landed=None):
-        block = lax.dynamic_index_in_dim(part, place, 0, False)
-        if landed is None:
-            return block
-        return (block.astype(f32) + landed.astype(f32)).astype(jnp.bfloat16)
-
-    first = yield along(take(jnp.where(chip == 0, 3, 0)), [(0, 1), (3, 2)])
-    outer, inner = yield (
-        along(take(jnp.where(chip == 0, 2, 1)), [(0, 1), (3, 2)]),
-        along(take(jnp.where(chip == 1, 3, 0), first), [(1, 2), (2, 1)]),
-    )
-    right, left = yield (
-        along(
-            take(jnp.minimum(chip + 1, 3), jnp.where(chip == 1, outer, inner)),
-            [(0, 1), (1, 2), (2, 3)],
-        ),
-        along(
-            take(jnp.maximum(chip - 1, 0), jnp.where(chip == 2, outer, inner)),
-            [(3, 2), (2, 1), (1, 0)],
-        ),
-    )
-    total = take(chip).astype(f32) + right.astype(f32) + left.astype(f32)
-    return (total[:up_rows], total[up_rows:])
-
-
-def whole_gather(gate_up, down):
-    landed = yield tuple(
-        lax.all_gather(part, "fsdp", axis=0, tiled=True) for part in (gate_up, down)
-    )
-    return tuple(landed)
-
-
-def whole_scatter(gate_up, down):
-    landed = yield tuple(
-        lax.psum_scatter(part, "fsdp", scatter_dimension=0, tiled=True) for part in (gate_up, down)
-    )
-    return tuple(part.astype(jnp.float32) for part in landed)
-
-
-class Stream:
-    def __init__(self, rounds):
-        self.rounds, self.result = rounds, None
-        self.flight = next(rounds)
-
-    def advance(self, landed):
-        try:
-            self.flight = self.rounds.send(landed)
-        except StopIteration as stop:
-            self.flight, self.result = (), stop.value
-
-
-class Slots:
-    def __init__(self):
-        self.streams, self.tick = [], jnp.zeros((), jnp.float32)
-
-    def start(self, rounds, *arrays):
-        arrays = self.gate(arrays)
-        self.streams.append(Stream(rounds(*arrays)))
-        return self.streams[-1]
-
-    def gate(self, arrays):
-        return lax.optimization_barrier((arrays, self.tick))[0]
-
-    def close(self, values):
-        flights = [stream.flight for stream in self.streams]
-        flights, values, self.tick = lax.optimization_barrier((flights, values, self.tick))
-        for stream, landed in zip(self.streams, flights):
-            stream.advance(landed)
-        self.streams = [stream for stream in self.streams if stream.result is None]
-        return values
-
-    def finish(self, stream, values):
-        while stream.result is None:
-            values = self.close(values)
-        return values
+    width = stacked.shape[-1]
+    stacked = stacked.reshape(count, -1, width)
+    return (stacked[:, :up_rows].reshape(-1, width), stacked[:, up_rows:].reshape(-1, width))
+
+
+def stack_rows(gate_up, down):
+    count = lax.axis_size("fsdp")
+    width = gate_up.shape[-1]
+    parts = [grad.reshape(count, -1, width) for grad in (gate_up, down)]
+    return jnp.concatenate(parts, axis=1).reshape(-1, width)
 
 
 def local(
@@ -326,9 +198,6 @@
     bf16, f32 = jnp.bfloat16, jnp.float32
     seq_count = lax.axis_size("seq")
     seq_rank = lax.axis_index("seq")
-    in_line = lax.axis_size("fsdp") == 2 * LINE
-    gather_rounds = line_gather if in_line else whole_gather
-    scatter_rounds = line_scatter if in_line else whole_scatter
     own_tokens = tokens[0]
     tok_count, model_width = own_tokens.shape
     local_count = gate_up_weight.shape[0]
@@ -343,8 +212,11 @@
     ).reshape(-1)
     valid_all = (places < length).reshape(seq_count, tok_count)
     keep_mask = valid_all[0].astype(f32)[:, None]
-    slots = Slots()
-    slot_weights = lambda index: (gate_up_weight[index], down_weight[index])
+    up_rows = gate_up_weight.shape[1]
+    shards = [
+        jnp.concatenate([gate_up_weight[index], down_weight[index]], axis=0)
+        for index in range(local_count)
+    ]
 
     own_qkv = lax.dynamic_index_in_dim(
         qkv_weight.reshape(-1, 3, seq_count, own_width), seq_rank, 2, False
@@ -358,14 +230,19 @@
     front = jnp.concatenate([own_qkv, own_small], axis=1)
     front_full = lax.all_gather(front, "fsdp", axis=0, tiled=True)
     token_blocks = gather_blocks(own_tokens)
-    id_blocks = gather_blocks(experts[0])
     out_cut = lax.dynamic_slice_in_dim(out_weight, seq_rank * own_width, own_width, 1)
-    out_cut = lax.optimization_barrier((out_cut, front))[0]
-    out_cut = lax.all_gather(out_cut, "fsdp", axis=0, tiled=True)
-    front_full, token_blocks = slots.close((front_full, token_blocks))
-
-    gathers = [slots.start(gather_rounds, *slot_weights(0))]
-    cot_blocks = gather_blocks(slots.gate(cotangent[0]))
+    out_cut = lax.all_gather(after(out_cut, front), "fsdp", axis=0, tiled=True)
+    gather_expert = lambda index, *earlier: lax.all_gather(
+        after(shards[index], *earlier), "fsdp", axis=0, tiled=True
+    )
+    weights = [gather_expert(0, front_full)]
+    id_rows = experts[0].astype(bf16).reshape(-1, model_width)
+    cot_parts = gather_blocks(
+        after(jnp.concatenate([cotangent[0], id_rows], axis=0), token_blocks)
+    )
+    cot_blocks = cot_parts[:, :tok_count]
+    id_blocks = cot_parts[:, tok_count:].reshape(seq_count, tok_count, -1).astype(jnp.int32)
+
     qkv_own = front_full[:, : 3 * own_width]
     small_full = front_full[:, 3 * own_width : 3 * own_width + small_count].T
     gain_one, gain_q, gain_k, gain_two = [small_full[i].astype(f32) for i in range(4)]
@@ -401,7 +278,6 @@
         key_rot.astype(bf16),
         value_raw.reshape(head_shape).astype(bf16),
     )
-    heads_in = slots.close(heads_in)
 
     row_count = min(512, key_span)
     block_starts = jnp.arange(key_span // row_count, dtype=jnp.int32) * row_count
@@ -409,8 +285,9 @@
         partial(attend_block, heads_in, places, length, row_count), block_starts
     )
     log_sums = sums_blocks.reshape(key_span, own_heads)
+    weights.append(gather_expert(1, heads_in))
+    out_cut = after(out_cut, heads_in)
     out_parts = [from_peer(out_cut, step) for step in range(seq_count)]
-    attended_blocks, cot_blocks, out_parts = slots.close((attended_blocks, cot_blocks, out_parts))
 
     out_full = in_rank_order(out_parts)
     attended_parts = return_blocks(attended_blocks.reshape(seq_count, tok_count, own_width))
@@ -423,11 +300,10 @@
     scale_two = rms_scale(middle)
     unit_two = middle * scale_two
     normed_two = (unit_two * gain_two).astype(bf16)
-    normed_two = slots.close(normed_two)
-
-    gathers.append(slots.start(gather_rounds, *slot_weights(1)))
-    row_blocks = slots.close(gather_blocks(normed_two))
-
+
+    row_blocks = gather_blocks(normed_two)
+    weights.append(gather_expert(2, normed_two))
+    weights += [gather_expert(index, row_blocks) for index in range(3, local_count)]
     logits = mixed_dot("btd,ed->bte", row_blocks, router_rows)
     expert_range = jnp.arange(experts_count, dtype=jnp.int32)
     named = jnp.any(id_blocks[..., None] == expert_range, axis=2)
@@ -457,7 +333,7 @@
 
     def computed(index, pair):
         weighted, grad_slot, grad_rows, kept = expert_forward(
-            *pair, slot_gates[index].reshape(-1), *gathers[index].result
+            *pair, slot_gates[index].reshape(-1), *split_rows(weights[index], up_rows)
         )
         weighted_rows.append(weighted.reshape(seq_count, slot_count, model_width))
         grad_row_sets.append(grad_rows.reshape(seq_count, slot_count, model_width))
@@ -471,34 +347,23 @@
         )
         return kept
 
-    weighted_rows, grad_row_sets, grad_slots, scatters = [], [], [], []
-    pair = slots.close(picked(0))
-
+    weighted_rows, grad_row_sets, grad_slots, sums = [], [], [], []
+    scatter = lambda grads: lax.psum_scatter(grads, "fsdp", scatter_dimension=0, tiled=True)
+    pair = picked(0)
     for index in range(local_count):
-        pair = slots.finish(gathers[index], pair)
         kept = computed(index, pair)
-        last = index == local_count - 1
-        if last:
-            break
-        grads = slots.close(expert_weights(kept))
-        pair = picked(index + 1)
-        if index + 2 < local_count:
-            gathers.append(slots.start(gather_rounds, *slot_weights(index + 2)))
-        scatters.append(slots.start(scatter_rounds, *grads))
-        pair = slots.close(pair)
+        if index + 1 < local_count:
+            grads = stack_rows(*expert_weights(kept))
+            sums.append(scatter(after(grads, *sums[: max(0, index - 1)])))
+            pair = after(picked(index + 1), grads)
     pick_all = jnp.concatenate([slot_pick[index] for index in range(local_count)], axis=1)
     grad_partial = mixed_dot("bct,bcd->btd", pick_all, jnp.concatenate(grad_row_sets, axis=1))
-    grad_partial, grad_slots, kept = slots.close(
-        (grad_partial.astype(bf16), jnp.stack(grad_slots, axis=1), kept)
-    )
-
-    grad_back = return_blocks(grad_partial)
-    grad_gates = return_blocks(grad_slots)
+
+    grad_gates = return_blocks(jnp.stack(grad_slots, axis=1))
+    grad_back = return_blocks(grad_partial.astype(bf16))
     moe_partial = mixed_dot("bct,bcd->btd", pick_all, jnp.concatenate(weighted_rows, axis=1))
-    grads, grad_back, grad_gates, moe_partial = slots.close(
-        (expert_weights(kept), grad_back, grad_gates, moe_partial.astype(bf16))
-    )
-    scatters.append(slots.start(scatter_rounds, *grads))
+    grads = stack_rows(*expert_weights(kept))
+    grad_back = after(grad_back, grads, moe_partial.astype(bf16))
 
     own_gates = gates[0]
     grad_gates = jnp.transpose(in_rank_order(grad_gates), (2, 0, 1)).reshape(
@@ -527,9 +392,8 @@
             for step in range(seq_count)
         ]
     ).reshape(head_shape)
-    grad_heads, grad_branch, moe_partial = slots.close((grad_heads, grad_branch, moe_partial))
-
-    moe_parts = return_blocks(moe_partial)
+
+    grad_branch = after(grad_branch, grad_heads)
     grad_cut = mixed_dot("td,tc->dc", attended.reshape(tok_count, model_width), grad_branch)
     grad_cut = grad_cut.astype(bf16).reshape(model_width, seq_count, own_width)
     grad_cut = [
@@ -542,12 +406,7 @@
         (zero_heads, zero_heads),
         block_starts,
     )
-    grad_keys, grad_values, grad_queries, grad_cut, moe_parts = slots.close(
-        (grad_keys, grad_values, grad_queries, grad_cut, moe_parts)
-    )
-
-    moe_sum = sum(part.astype(f32) for part in moe_parts)
-    block_out = (middle + moe_sum).astype(bf16)
+
     grad_cut = sum(part.astype(f32) for part in grad_cut).astype(bf16)
     low = lambda rows: rows.reshape(head_shape).astype(bf16).astype(f32)
     grad_qn = rotate_back(low(grad_queries), cosine_table, sine_table).reshape(key_span, own_width)
@@ -588,12 +447,13 @@
         axis=0,
     )
     grad_front = jnp.concatenate([grad_qkv, grad_small.T.astype(bf16)], axis=1)
-    grad_front, grad_normed = slots.close((grad_front, grad_normed.astype(bf16)))
-
-    front_sum = lax.psum_scatter(grad_front, "fsdp", scatter_dimension=0, tiled=True)
-    out_sum = lax.psum_scatter(grad_cut, "fsdp", scatter_dimension=0, tiled=True)
-    grad_normed = return_blocks(grad_normed.reshape(seq_count, tok_count, model_width))
-    grad_normed = slots.finish(scatters[-1], grad_normed)
+
+    front_sum = scatter(after(grad_front, *sums[:-1]))
+    out_sum = scatter(after(grad_cut, *sums, grad_front))
+    sums.append(scatter(after(grads, front_sum)))
+    grad_normed = return_blocks(grad_normed.astype(bf16).reshape(seq_count, tok_count, model_width))
+    moe_parts = return_blocks(after(moe_partial.astype(bf16), grad_normed))
+    block_out = (middle + sum(part.astype(f32) for part in moe_parts)).astype(bf16)
     grad_normed = sum(part.astype(f32) for part in grad_normed)
     scale_one = rms_scale(inputs)
     scaled = grad_normed * gain_one
@@ -608,7 +468,6 @@
     ).reshape(-1, 3 * model_width)
     out_sum = in_rank_order([from_peer(out_sum, step) for step in range(seq_count)])
     out_sum = jnp.transpose(out_sum, (1, 0, 2)).reshape(-1, model_width)
-    sums = [stream.result for stream in scatters]
     return (
         block_out[None],
         grad_tokens[None],
@@ -619,8 +478,8 @@
         out_sum.astype(f32),
         small_sum[:, 3],
         small_sum[:, 4:small_count],
-        jnp.stack([pair[0] for pair in sums]),
-        jnp.stack([pair[1] for pair in sums]),
+        jnp.stack([rows[:up_rows] for rows in sums]).astype(f32),
+        jnp.stack([rows[up_rows:] for rows in sums]).astype(f32),
     )
 
 

time: 1640 us -> 1260 us (0.77)
  other arithmetic: 232 us -> 122 us
  starting transfers between devices: 143 us -> 53.9 us
  local copies, waits for them, and re-layouts: 261 us -> 174 us
  waiting for transfers between devices: 674 us -> 593 us
  matrix products: 300 us -> 281 us
    ppermute x52 -> x0, waiting for transfers between devices: 309 us -> none  [the longest x44 309 us: along(): return lax.ppermute(values, 'fsdp', pairs)]
    reduce_scatter x2 -> x6, waiting for transfers between devices: 0.02 us -> 100 us  [local(): lax.psum_scatter(grads, 'fsdp', scatter_dimension=0, tiled=True)]
    ppermute x52 -> x0, starting transfers between devices: 88.2 us -> none  [the longest x44 87.3 us: along(): return lax.ppermute(values, 'fsdp', pairs)]
    ppermute x48 -> x45, waiting for transfers between devices: 346 us -> 428 us  [from_peer(): lax.ppermute(values, 'seq', [(rank, rank ^ step) for rank in range(count)])]
    convert_element_type x14 -> x4, other arithmetic: 74.6 us -> 8.2 us  [the longest x1 3.74 us: local(): jnp.stack([rows[:up_rows] for rows in sums]).astype(f32)]
    slice x3 -> x10, local copies, waits for them, and re-layouts: 0.34 us -> 53.3 us  [the longest x4 33.8 us: split_rows(): stacked[:, :up_rows].reshape(-1, width)]
    dynamic_update_slice x20 -> x2, local copies, waits for them, and re-layouts: 52.7 us -> 0.89 us  [local(): lax.map(partial(attend_block, heads_in, places, length, row_count), block...]
    squeeze x15 -> x3, local copies, waits for them, and re-layouts: 53.4 us -> 4.07 us  [the longest x1 1.84 us: local(): gate_up_weight[index]]
  transfers between devices with their start and end apart: 104 -> 57, of which waited for: 42 -> 30; matrix products, arithmetic and copies ran while one was open for 36% -> 42% of each run, Pallas kernels for 0% -> 0%
where the time goes in v3:
time: 1260 us; the launch traced here: 1250 us
  waiting for transfers between devices  593 us (47%)
  matrix products  281 us (22%)
  local copies, waits for them, and re-layouts  174 us (14%)
  other arithmetic  122 us (10%)
  starting transfers between devices  53.9 us (4%)
  between operations  17.4 us (1%)
    ppermute x45, waiting for transfers between devices, from_peer(): lax.ppermute(values, 'seq', [(rank, rank ^ step) for rank in range(count)])  428 us
    dot_general x40, matrix products, mixed_dot(): return jnp.einsum(form, left, right, preferred_element_type=jnp.float32)  236 us
    reduce_scatter x6, waiting for transfers between devices, local(): lax.psum_scatter(grads, 'fsdp', scatter_dimension=0, tiled=True)  100 us
    all_gather x1, waiting for transfers between devices, local(): front_full = lax.all_gather(front, 'fsdp', axis=0, tiled=True)  64.7 us
    ppermute x45, starting transfers between devices, from_peer(): lax.ppermute(values, 'seq', [(rank, rank ^ step) for rank in range(count)])  52.8 us
    concatenate x4, other arithmetic, stack_rows(): return jnp.concatenate(parts, axis=1).reshape(-1, width)  36.4 us
    unnamed x298, local copies, waits for them, and re-layouts  36.2 us
    slice x4, local copies, waits for them, and re-layouts, split_rows(): stacked[:, :up_rows].reshape(-1, width)  33.8 us
  transfers between devices with their start and end apart: 57, of which 30 were waited for; matrix products, arithmetic and copies ran while one was open for 42% of the time, Pallas kernels for 0%

profile of v3, /device:TPU:0, one launch (start us, length us, event | category | flops | bytes accessed | tf_op | source)
XLA Modules:
  0.0 1249.8 jit_solution(11664101353215913733)
XLA Ops:
  10.0 7.4 reshape.534
  31.0 64.7 %all-gather.7.cloned.1.call-done = bf16[2048,1664]{0,1:T(8,128)(2,1)} async-done(((bf16[256,1664]{0,1:T(8,128)(2,1)}), bf16[2048,1664]{0,1:T(8,128)(2,1)}) %all-gather.7.cloned.1.call-update) | async-done | bytes 6815760 | tf_op jit(solution)/shard_map/all_gather | solution.py:231
  105.9 15.3 %collective-permute-done.1 = bf16[256,2048]{1,0:T(8,128)(2,1)S(1)} collective-permute-done((bf16[256,2048]{1,0:T(8,128)(2,1)S(1)}, bf16[256,2048]{1,0:T(8,128)(2,1)S(1)}, u32[]{:S(2)}, u32[]{:S(2)}) %collective-permute-start.1) | collective-permute-done | bytes 1048608 | tf_op jit(solution)/shard_map/ppermute | solution.py:61
  123.4 21.5 %collective-permute-done.2 = bf16[256,2048]{1,0:T(8,128)(2,1)S(1)} collective-permute-done((bf16[256,2048]{1,0:T(8,128)(2,1)S(1)}, bf16[256,2048]{1,0:T(8,128)(2,1)S(1)}, u32[]{:S(2)}, u32[]{:S(2)}) %collective-permute-start.2) | collective-permute-done | bytes 1048608 | tf_op jit(solution)/shard_map/ppermute | solution.py:61
  149.1 6.7 fusion.54
  176.6 25.4 %while.28 = (s32[]{:T(128)}, bf16[2,512,4,128]{3,2,1,0:T(4,128)(2,1)}, f32[2,512,4]{1,2,0:T(4,128)S(1)}, s32[2]{0:T(128)S(1)}, s32[1024]{0:T(1024)S(1)}, /*index...) while((s32[]{:T(128)}, ...), condition=%wide.region_6.7_spmd.clone, body=%wide.region_3.6_spmd.clone.sunk | while | flops 1100218368 | bytes 39940364 | solution.py:284
  211.0 19.6 %collective-permute-done.8 = bf16[256,512]{1,0:T(8,128)(2,1)} collective-permute-done((bf16[256,512]{1,0:T(8,128)(2,1)}, bf16[256,512]{1,0:T(8,128)(2,1)}, u32[]{:S(2)}, u32[]{:S(2)}) %collective-permute-start.8) | collective-permute-done | bytes 262176 | tf_op jit(solution)/shard_map/ppermute | solution.py:61
  237.3 39.5 %collective-permute-done.7 = bf16[256,512]{1,0:T(8,128)(2,1)} collective-permute-done((bf16[256,512]{1,0:T(8,128)(2,1)}, bf16[256,512]{1,0:T(8,128)(2,1)}, u32[]{:S(2)}, u32[]{:S(2)}) %collective-permute-start.7) | collective-permute-done | bytes 262176 | tf_op jit(solution)/shard_map/ppermute | solution.py:61
  289.1 6.1 multiply_reduce_fusion.8
  302.1 20.6 %collective-permute-done.17 = bf16[256,2048]{1,0:T(8,128)(2,1)} collective-permute-done((bf16[256,2048]{1,0:T(8,128)(2,1)S(1)}, bf16[256,2048]{1,0:T(8,128)(2,1)}, u32[]{:S(2)}, u32[]{:S(2)}) %collective-permute-start.17) | collective-permute-done | bytes 1048608 | tf_op jit(solution)/shard_map/ppermute | solution.py:61
  322.7 18.1 %collective-permute-done.16 = bf16[256,2048]{1,0:T(8,128)(2,1)} collective-permute-done((bf16[256,2048]{1,0:T(8,128)(2,1)S(1)}, bf16[256,2048]{1,0:T(8,128)(2,1)}, u32[]{:S(2)}, u32[]{:S(2)}) %collective-permute-start.16) | collective-permute-done | bytes 1048608 | tf_op jit(solution)/shard_map/ppermute | solution.py:61
  349.4 24.1 %collective-permute-done.14 = bf16[257,2048]{1,0:T(8,128)(2,1)S(1)} collective-permute-done((bf16[257,2048]{1,0:T(8,128)(2,1)S(1)}, bf16[257,2048]{1,0:T(8,128)(2,1)S(1)}, u32[]{:S(2)}, u32[]{:S(2)}) %collective-permute-start.14) | collective-permute-done | bytes 1052704 | tf_op jit(solution)/shard_map/ppermute | solution.py:61
  373.5 22.2 %collective-permute-done.13 = bf16[257,2048]{1,0:T(8,128)(2,1)} collective-permute-done((bf16[257,2048]{1,0:T(8,128)(2,1)S(1)}, bf16[257,2048]{1,0:T(8,128)(2,1)}, u32[]{:S(2)}, u32[]{:S(2)}) %collective-permute-start.13) | collective-permute-done | bytes 1052704 | tf_op jit(solution)/shard_map/ppermute | solution.py:61
  409.0 5.4 multiply_convert_fusion.3
  414.4 4.7 slice.481
  419.1 8.5 slice.478
  427.5 7.6 fusion.168
  442.9 7.1 convolution_convert_fusion.5
  450.0 9.0 pad_maximum_fusion
  467.5 4.8 slice.488
  472.4 8.5 slice.485
  480.8 8.2 fusion.169
  496.7 7.1 convolution_convert_fusion.4
  503.9 9.1 pad_maximum_fusion.1
  530.1 5.8 fusion.57
  536.0 9.5 convolution_convert_fusion.13
  549.7 9.3 convolution_convert_fusion.12
  559.0 4.8 slice.494
  563.8 8.5 slice.491
  572.4 7.6 fusion.170
  580.0 4.9 multiply_convert_fusion.9
  589.4 5.7 convolution_convert_fusion.7
  595.1 7.2 convolution_convert_fusion.3
  602.3 9.1 pad_maximum_fusion.2
  611.4 9.8 convolution_convert_fusion.11
  621.2 4.9 slice.500
  626.1 8.4 slice.497
  634.4 7.6 fusion.171
  642.0 5.0 multiply_convert_fusion.6
  654.4 9.3 convolution_convert_fusion.10
  663.8 59.2 %reduce-scatter.7.cloned.1.call-done = bf16[384,2048]{1,0:T(8,128)(2,1)} async-done(((bf16[3072,2048]{1,0:T(8,128)(2,1)}), bf16[384,2048]{1,0:T(8,128)(2,1)}) %reduce-scatter.7.cloned.1.call-update) | async-done | bytes 1572880 | tf_op jit(solution)/shard_map/reduce_scatter | solution.py:351
  723.1 6.4 fusion.70
  738.8 7.6 fusion.73
  746.4 7.2 convolution_convert_fusion.2
  753.6 9.2 pad_maximum_fusion.3
  764.4 13.7 %collective-permute-done.19 = f32[4,256]{1,0:T(4,128)S(1)} collective-permute-done((f32[4,256]{1,0:T(4,128)S(1)}, f32[4,256]{1,0:T(4,128)S(1)}, u32[]{:S(2)}, u32[]{:S(2)}) %collective-permute-start.19) | collective-permute-done | bytes 4128 | tf_op jit(solution)/shard_map/ppermute | solution.py:61
  785.2 5.8 fusion.77
  806.7 4.7 collective-permute-done.24
  815.9 42.3 %while.29 = (s32[]{:T(128)}, f32[1024,4,128]{0,2,1:T(8,128)S(1)}, f32[1024,4,128]{0,2,1:T(8,128)}, bf16[2,512,4,128]{3,1,0,2:T(8,128)(2,1)}, s32[2]{0:T(128)S(1)...) while((s32[]{:T(128)}, f32[1024,4,128]{0,2,1:T(8,128)S(1)}, ...), condition=%wide.region_26.27_spmd.clone, body=%wide.region_24.26_spmd.clone.sunk | while | flops 2719744000 | bytes 97603952 | solution.py:404
  843.9 5.1 bitcast_add_fusion.5
  885.1 11.7 multiply_reduce_fusion.1
  897.8 10.9 convolution_convert_fusion.1
  908.7 7.0 pad_maximum_fusion.4
  924.3 45.0 %collective-permute-done.39 = bf16[2048,512]{0,1:T(8,128)(2,1)S(1)} collective-permute-done((bf16[2048,512]{0,1:T(8,128)(2,1)S(1)}, bf16[2048,512]{0,1:T(8,128)(2,1)S(1)}, u32[]{:S(2)}, u32[]{:S(2)}) %collective-permute-start.39) | collective-permute-done | bytes 2097184 | tf_op jit(solution)/shard_map/ppermute | solution.py:61
  969.3 43.9 %collective-permute-done.41 = bf16[2048,512]{0,1:T(8,128)(2,1)S(1)} collective-permute-done((bf16[2048,512]{0,1:T(8,128)(2,1)S(1)}, bf16[2048,512]{0,1:T(8,128)(2,1)S(1)}, u32[]{:S(2)}, u32[]{:S(2)}) %collective-permute-start.41) | collective-permute-done | bytes 2097184 | tf_op jit(solution)/shard_map/ppermute | solution.py:61
  1017.7 41.0 %reduce-scatter.11.cloned.1.call-done = bf16[256,1664]{0,1:T(8,128)(2,1)} async-done(((bf16[2048,1664]{0,1:T(8,128)(2,1)}), bf16[256,1664]{0,1:T(8,128)(2,1)}) %reduce-scatter.11.cloned.1.call-update) | async-done | bytes 851984 | tf_op jit(solution)/shard_map/reduce_scatter | solution.py:351
  1065.1 23.1 %collective-permute-done.32 = bf16[256,2048]{1,0:T(8,128)(2,1)S(1)} collective-permute-done((bf16[256,2048]{1,0:T(8,128)(2,1)S(1)}, bf16[256,2048]{1,0:T(8,128)(2,1)S(1)}, u32[]{:S(2)}, u32[]{:S(2)}) %collective-permute-start.32) | collective-permute-done | bytes 1048608 | tf_op jit(solution)/shard_map/ppermute | solution.py:61
  1088.2 19.4 %collective-permute-done.31 = bf16[256,2048]{1,0:T(8,128)(2,1)S(1)} collective-permute-done((bf16[256,2048]{1,0:T(8,128)(2,1)S(1)}, bf16[256,2048]{1,0:T(8,128)(2,1)S(1)}, u32[]{:S(2)}, u32[]{:S(2)}) %collective-permute-start.31) | collective-permute-done | bytes 1048608 | tf_op jit(solution)/shard_map/ppermute | solution.py:61
  1115.2 19.0 %collective-permute-done.33 = bf16[256,2048]{1,0:T(8,128)(2,1)S(1)} collective-permute-done((bf16[256,2048]{1,0:T(8,128)(2,1)S(1)}, bf16[256,2048]{1,0:T(8,128)(2,1)S(1)}, u32[]{:S(2)}, u32[]{:S(2)}) %collective-permute-start.33) | collective-permute-done | bytes 1048608 | tf_op jit(solution)/shard_map/ppermute | solution.py:61
  1134.2 22.6 %collective-permute-done.35 = bf16[256,2048]{1,0:T(8,128)(2,1)S(1)} collective-permute-done((bf16[256,2048]{1,0:T(8,128)(2,1)S(1)}, bf16[256,2048]{1,0:T(8,128)(2,1)S(1)}, u32[]{:S(2)}, u32[]{:S(2)}) %collective-permute-start.35) | collective-permute-done | bytes 1048608 | tf_op jit(solution)/shard_map/ppermute | solution.py:61
  1167.6 18.1 %collective-permute-done.38 = bf16[256,1664]{0,1:T(8,128)(2,1)S(1)} collective-permute-done((bf16[256,1664]{0,1:T(8,128)(2,1)S(1)}, bf16[256,1664]{0,1:T(8,128)(2,1)S(1)}, u32[]{:S(2)}, u32[]{:S(2)}) %collective-permute-start.38) | collective-permute-done | bytes 852000 | tf_op jit(solution)/shard_map/ppermute | solution.py:61
  1185.7 15.2 %collective-permute-done.37 = bf16[256,1664]{0,1:T(8,128)(2,1)S(1)} collective-permute-done((bf16[256,1664]{0,1:T(8,128)(2,1)S(1)}, bf16[256,1664]{0,1:T(8,128)(2,1)S(1)}, u32[]{:S(2)}, u32[]{:S(2)}) %collective-permute-start.37) | collective-permute-done | bytes 852000 | tf_op jit(solution)/shard_map/ppermute | solution.py:61
  1205.9 6.7 copy.226
  1223.7 7.0 collective-permute-done.43
  (681 shorter events, 350.9 us)
Async XLA Ops:
  7.2 88.6 %all-gather.7.cloned.1.call-start = ((), (), s32[]{:S(2)}) async-start(), calls=%async_computation.6 | async-start | bytes 7667712 | tf_op jit(solution)/shard_map/all_gather | solution.py:231
  23.4 151.1 %all-gather.9.cloned.1.call-start = ((), (), s32[]{:S(2)}) async-start(), calls=%async_computation.7 | async-start | bytes 2359296 | tf_op jit(solution)/shard_map/all_gather | solution.py:234
  24.4 390.0 %all-gather.11.cloned.1.call-start = ((), (), s32[]{:S(2)}) async-start(), calls=%async_computation.8 | async-start | bytes 14155776 | tf_op jit(solution)/shard_map/all_gather | solution.py:235
  29.7 69.8 %copy-start.120 = (s32[4]{0:T(128)S(1)}, s32[4]{0:T(128)}, u32[]{:S(2)}) copy-start(s32[4]{0:T(128)} %constant.168) | copy-start | bytes 52
  29.7 69.9 %copy-start.119 = (s32[4]{0:T(128)S(1)}, s32[4]{0:T(128)}, u32[]{:S(2)}) copy-start(s32[4]{0:T(128)} %constant.169) | copy-start | bytes 52
  29.7 69.9 %copy-start.118 = (s32[4]{0:T(128)S(1)}, s32[4]{0:T(128)}, u32[]{:S(2)}) copy-start(s32[4]{0:T(128)} %constant.170) | copy-start | bytes 52
  95.8 371.8 %all-gather.13.cloned.1.call-start = ((), (), s32[]{:S(2)}) async-start(), calls=%async_computation.9 | async-start | bytes 14155776 | tf_op jit(solution)/shard_map/all_gather | solution.py:235
  95.8 25.4 %collective-permute-start.1 = (bf16[256,2048]{1,0:T(8,128)(2,1)S(1)}, bf16[256,2048]{1,0:T(8,128)(2,1)S(1)}, u32[]{:S(2)}, u32[]{:S(2)}) collective-permute-start(bf16[256,2048]{1,0:T(8,128)(2,1)S(1)} %bitcast.534), channel_id=1, source_target_pairs={{0,16},{8,24},{16,0},{24,8},{1,17},{9,25},{17,1},{25,9},{2,18},{10... | collective-permute-start | bytes 3145736 | tf_op jit(solution)/shard_map/ppermute | solution.py:61
  97.4 26.0 %collective-permute-start = (bf16[256,2048]{1,0:T(8,128)(2,1)S(1)}, bf16[256,2048]{1,0:T(8,128)(2,1)S(1)}, u32[]{:S(2)}, u32[]{:S(2)}) collective-permute-start(bf16[256,2048]{1,0:T(8,128)(2,1)S(1)} %bitcast.535), channel_id=1, source_target_pairs={{0,8},{8,0},{16,24},{24,16},{1,9},{9,1},{17,25},{25,17},{2,10},{10... | collective-permute-start | bytes 3145736 | tf_op jit(solution)/shard_map/ppermute | solution.py:61
  98.9 46.0 %collective-permute-start.2 = (bf16[256,2048]{1,0:T(8,128)(2,1)S(1)}, bf16[256,2048]{1,0:T(8,128)(2,1)S(1)}, u32[]{:S(2)}, u32[]{:S(2)}) collective-permute-start(bf16[256,2048]{1,0:T(8,128)(2,1)S(1)} %bitcast.536), channel_id=1, source_target_pairs={{0,24},{8,16},{16,8},{24,0},{1,25},{9,17},{17,9},{25,1},{2,26},{10... | collective-permute-start | bytes 3145736 | tf_op jit(solution)/shard_map/ppermute | solution.py:61
  146.7 254.9 %copy-start.76 = (bf16[20,2048]{1,0:T(8,128)(2,1)}, bf16[20,2048]{1,0:T(8,128)(2,1)S(1)}, u32[]{:S(2)}) copy-start(bf16[20,2048]{1,0:T(8,128)(2,1)S(1)} %slice_bitcast_fusion.46) | copy-start | bytes 245764
  146.7 155.1 %copy-start.90 = (f32[1,2048]{1,0:T(1,128)}, f32[1,2048]{1,0:T(1,128)S(1)}, u32[]{:S(2)}) copy-start(f32[1,2048]{1,0:T(1,128)S(1)} %get-tuple-element.544) | copy-start | bytes 24580
  158.9 4.6 collective-permute-start.5
  161.3 3.7 collective-permute-start.4
  161.9 3.7 collective-permute-start.3
  172.1 386.9 %all-gather.15.cloned.1.call-start = ((), (), s32[]{:S(2)}) async-start(), calls=%async_computation.10 | async-start | bytes 14155776 | tf_op jit(solution)/shard_map/all_gather | solution.py:235
  174.6 108.1 %collective-permute-start.10 = (bf16[2048,512]{0,1:T(8,128)(2,1)}, bf16[2048,512]{0,1:T(8,128)(2,1)}, u32[]{:S(2)}, u32[]{:S(2)}) collective-permute-start(bf16[2048,512]{0,1:T(8,128)(2,1)} %all-gather.9.cloned.1.call-done), channel_id=1, source_target_pairs={{0,16},{8,24},{16,0},{24,8},{1,17},{9,25},{17,1},{25,9},{2,18},{10... | collective-permute-start | bytes 6291464 | tf_op jit(solution)/shard_map/ppermute | solution.py:61
  176.1 103.0 %collective-permute-start.9 = (bf16[2048,512]{0,1:T(8,128)(2,1)}, bf16[2048,512]{0,1:T(8,128)(2,1)}, u32[]{:S(2)}, u32[]{:S(2)}) collective-permute-start(bf16[2048,512]{0,1:T(8,128)(2,1)} %all-gather.9.cloned.1.call-done), channel_id=1, source_target_pairs={{0,8},{8,0},{16,24},{24,16},{1,9},{9,1},{17,25},{25,17},{2,10},{10... | collective-permute-start | bytes 6291464 | tf_op jit(solution)/shard_map/ppermute | solution.py:61
  202.1 147.3 %copy-start.96 = (s32[4]{0:T(128)}, s32[4]{0:T(128)S(1)}, u32[]{:S(2)}) copy-start(s32[4]{0:T(128)S(1)} %get-tuple-element.916) | copy-start | bytes 52
  207.4 23.2 %collective-permute-start.8 = (bf16[256,512]{1,0:T(8,128)(2,1)}, bf16[256,512]{1,0:T(8,128)(2,1)}, u32[]{:S(2)}, u32[]{:S(2)}) collective-permute-start(bf16[256,512]{1,0:T(8,128)(2,1)} %get-tuple-element.532), channel_id=1, source_target_pairs={{0,24},{8,16},{16,8},{24,0},{1,25},{9,17},{17,9},{25,1},{2,26},{10... | collective-permute-start | bytes 786440 | tf_op jit(solution)/shard_map/ppermute | solution.py:61
  209.0 80.1 %copy-start.116 = (f32[256]{0:T(256)}, f32[256]{0:T(256)S(1)}, u32[]{:S(2)}) copy-start(f32[256]{0:T(256)S(1)} %slice_convert_fusion.3) | copy-start | bytes 3076
  209.0 76.8 %collective-permute-start.11 = (bf16[2048,512]{0,1:T(8,128)(2,1)}, bf16[2048,512]{0,1:T(8,128)(2,1)}, u32[]{:S(2)}, u32[]{:S(2)}) collective-permute-start(bf16[2048,512]{0,1:T(8,128)(2,1)} %all-gather.9.cloned.1.call-done), channel_id=1, source_target_pairs={{0,24},{8,16},{16,8},{24,0},{1,25},{9,17},{17,9},{25,1},{2,26},{10... | collective-permute-start | bytes 6291464 | tf_op jit(solution)/shard_map/ppermute | solution.py:61
  210.4 66.3 %collective-permute-start.7 = (bf16[256,512]{1,0:T(8,128)(2,1)}, bf16[256,512]{1,0:T(8,128)(2,1)}, u32[]{:S(2)}, u32[]{:S(2)}) collective-permute-start(bf16[256,512]{1,0:T(8,128)(2,1)} %get-tuple-element.533), channel_id=1, source_target_pairs={{0,16},{8,24},{16,0},{24,8},{1,17},{9,25},{17,1},{25,9},{2,18},{10... | collective-permute-start | bytes 786440 | tf_op jit(solution)/shard_map/ppermute | solution.py:61
  230.6 47.2 %collective-permute-start.6 = (bf16[256,512]{1,0:T(8,128)(2,1)}, bf16[256,512]{1,0:T(8,128)(2,1)}, u32[]{:S(2)}, u32[]{:S(2)}) collective-permute-start(bf16[256,512]{1,0:T(8,128)(2,1)} %get-tuple-element.534), channel_id=1, source_target_pairs={{0,8},{8,0},{16,24},{24,16},{1,9},{9,1},{17,25},{25,17},{2,10},{10... | collective-permute-start | bytes 786440 | tf_op jit(solution)/shard_map/ppermute | solution.py:61
  295.5 325.6 %all-gather.17.cloned.1.call-start = ((), (), s32[]{:S(2)}) async-start(), calls=%async_computation.11 | async-start | bytes 14155776 | tf_op jit(solution)/shard_map/all_gather | solution.py:235
  295.6 27.1 %collective-permute-start.17 = (bf16[256,2048]{1,0:T(8,128)(2,1)S(1)}, bf16[256,2048]{1,0:T(8,128)(2,1)}, u32[]{:S(2)}, u32[]{:S(2)}) collective-permute-start(bf16[256,2048]{1,0:T(8,128)(2,1)S(1)} %multiply_convert_fusion.20), channel_id=1, source_target_pairs={{0,24},{8,16},{16,8},{24,0},{1,25},{9,17},{17,9},{25,1},{2,26},{10... | collective-permute-start | bytes 3145736 | tf_op jit(solution)/shard_map/ppermute | solution.py:61
  297.5 43.2 %collective-permute-start.16 = (bf16[256,2048]{1,0:T(8,128)(2,1)S(1)}, bf16[256,2048]{1,0:T(8,128)(2,1)}, u32[]{:S(2)}, u32[]{:S(2)}) collective-permute-start(bf16[256,2048]{1,0:T(8,128)(2,1)S(1)} %multiply_convert_fusion.20), channel_id=1, source_target_pairs={{0,16},{8,24},{16,0},{24,8},{1,17},{9,25},{17,1},{25,9},{2,18},{10... | collective-permute-start | bytes 3145736 | tf_op jit(solution)/shard_map/ppermute | solution.py:61
  298.2 42.6 %collective-permute-start.15 = (bf16[256,2048]{1,0:T(8,128)(2,1)S(1)}, bf16[256,2048]{1,0:T(8,128)(2,1)}, u32[]{:S(2)}, u32[]{:S(2)}) collective-permute-start(bf16[256,2048]{1,0:T(8,128)(2,1)S(1)} %multiply_convert_fusion.20), channel_id=1, source_target_pairs={{0,8},{8,0},{16,24},{24,16},{1,9},{9,1},{17,25},{25,17},{2,10},{10... | collective-permute-start | bytes 3145736 | tf_op jit(solution)/shard_map/ppermute | solution.py:61
  344.4 378.6 %reduce-scatter.7.cloned.1.call-start = ((), (), s32[]{:S(2)}) async-start(), calls=%async_computation.12 | async-start | bytes 14155776 | tf_op jit(solution)/shard_map/reduce_scatter | solution.py:351
  345.8 27.7 %collective-permute-start.14 = (bf16[257,2048]{1,0:T(8,128)(2,1)S(1)}, bf16[257,2048]{1,0:T(8,128)(2,1)S(1)}, u32[]{:S(2)}, u32[]{:S(2)}) collective-permute-start(bf16[257,2048]{1,0:T(8,128)(2,1)S(1)} %pad_maximum_fusion.30), channel_id=1, source_target_pairs={{0,24},{8,16},{16,8},{24,0},{1,25},{9,17},{17,9},{25,1},{2,26},{10... | collective-permute-start | bytes 3158024 | tf_op jit(solution)/shard_map/ppermute | solution.py:61
  347.8 48.0 %collective-permute-start.13 = (bf16[257,2048]{1,0:T(8,128)(2,1)S(1)}, bf16[257,2048]{1,0:T(8,128)(2,1)}, u32[]{:S(2)}, u32[]{:S(2)}) collective-permute-start(bf16[257,2048]{1,0:T(8,128)(2,1)S(1)} %pad_maximum_fusion.30), channel_id=1, source_target_pairs={{0,16},{8,24},{16,0},{24,8},{1,17},{9,25},{17,1},{25,9},{2,18},{10... | collective-permute-start | bytes 3158024 | tf_op jit(solution)/shard_map/ppermute | solution.py:61
  348.7 47.1 %collective-permute-start.12 = (bf16[257,2048]{1,0:T(8,128)(2,1)S(1)}, bf16[257,2048]{1,0:T(8,128)(2,1)}, u32[]{:S(2)}, u32[]{:S(2)}) collective-permute-start(bf16[257,2048]{1,0:T(8,128)(2,1)S(1)} %pad_maximum_fusion.30), channel_id=1, source_target_pairs={{0,8},{8,0},{16,24},{24,16},{1,9},{9,1},{17,25},{25,17},{2,10},{10... | collective-permute-start | bytes 3158024 | tf_op jit(solution)/shard_map/ppermute | solution.py:61
  459.1 456.6 %reduce-scatter.9.cloned.1.call-start = ((), (), s32[]{:S(2)}) async-start(), calls=%async_computation.13 | async-start | bytes 14155776 | tf_op jit(solution)/shard_map/reduce_scatter | solution.py:351
  513.0 504.7 %reduce-scatter.13.cloned.1.call-start = ((), (), s32[]{:S(2)}) async-start(), calls=%async_computation.15 | async-start | bytes 14155776 | tf_op jit(solution)/shard_map/reduce_scatter | solution.py:351
  651.7 126.3 %collective-permute-start.20 = (f32[4,256]{1,0:T(4,128)S(1)}, f32[4,256]{1,0:T(4,128)S(1)}, u32[]{:S(2)}, u32[]{:S(2)}) collective-permute-start(f32[4,256]{1,0:T(4,128)S(1)} %get-tuple-element.550), channel_id=1, source_target_pairs={{0,24},{8,16},{16,8},{24,0},{1,25},{9,17},{17,9},{25,1},{2,26},{10... | collective-permute-start | bytes 12296 | tf_op jit(solution)/shard_map/ppermute | solution.py:61
  653.0 109.8 %collective-permute-start.18 = (f32[4,256]{1,0:T(4,128)S(1)}, f32[4,256]{1,0:T(4,128)S(1)}, u32[]{:S(2)}, u32[]{:S(2)}) collective-permute-start(f32[4,256]{1,0:T(4,128)S(1)} %get-tuple-element.552), channel_id=1, source_target_pairs={{0,8},{8,0},{16,24},{24,16},{1,9},{9,1},{17,25},{25,17},{2,10},{10... | collective-permute-start | bytes 12296 | tf_op jit(solution)/shard_map/ppermute | solution.py:61
  723.0 335.7 %reduce-scatter.11.cloned.1.call-start = ((), (), s32[]{:S(2)}) async-start(), calls=%async_computation.14 | async-start | bytes 7667712 | tf_op jit(solution)/shard_map/reduce_scatter | solution.py:351
  731.3 46.8 %collective-permute-start.23 = (bf16[256,2048]{1,0:T(8,128)(2,1)}, bf16[256,2048]{1,0:T(8,128)(2,1)}, u32[]{:S(2)}, u32[]{:S(2)}) collective-permute-start(bf16[256,2048]{1,0:T(8,128)(2,1)} %get-tuple-element.496), channel_id=1, source_target_pairs={{0,24},{8,16},{16,8},{24,0},{1,25},{9,17},{17,9},{25,1},{2,26},{10... | collective-permute-start | bytes 3145736 | tf_op jit(solution)/shard_map/ppermute | solution.py:61
  733.7 44.4 %collective-permute-start.22 = (bf16[256,2048]{1,0:T(8,128)(2,1)}, bf16[256,2048]{1,0:T(8,128)(2,1)}, u32[]{:S(2)}, u32[]{:S(2)}) collective-permute-start(bf16[256,2048]{1,0:T(8,128)(2,1)} %get-tuple-element.497), channel_id=1, source_target_pairs={{0,16},{8,24},{16,0},{24,8},{1,17},{9,25},{17,1},{25,9},{2,18},{10... | collective-permute-start | bytes 3145736 | tf_op jit(solution)/shard_map/ppermute | solution.py:61
  734.2 43.9 %collective-permute-start.21 = (bf16[256,2048]{1,0:T(8,128)(2,1)}, bf16[256,2048]{1,0:T(8,128)(2,1)}, u32[]{:S(2)}, u32[]{:S(2)}) collective-permute-start(bf16[256,2048]{1,0:T(8,128)(2,1)} %get-tuple-element.498), channel_id=1, source_target_pairs={{0,8},{8,0},{16,24},{24,16},{1,9},{9,1},{17,25},{25,17},{2,10},{10... | collective-permute-start | bytes 3145736 | tf_op jit(solution)/shard_map/ppermute | solution.py:61
  762.8 15.2 %collective-permute-start.19 = (f32[4,256]{1,0:T(4,128)S(1)}, f32[4,256]{1,0:T(4,128)S(1)}, u32[]{:S(2)}, u32[]{:S(2)}) collective-permute-start(f32[4,256]{1,0:T(4,128)S(1)} %get-tuple-element.551), channel_id=1, source_target_pairs={{0,16},{8,24},{16,0},{24,8},{1,17},{9,25},{17,1},{25,9},{2,18},{10... | collective-permute-start | bytes 12296 | tf_op jit(solution)/shard_map/ppermute | solution.py:61
  796.3 10.4 collective-permute-start.26
  798.1 13.3 %collective-permute-start.24 = (bf16[256,512]{1,0:T(8,128)(2,1)}, bf16[256,512]{1,0:T(8,128)(2,1)}, u32[]{:S(2)}, u32[]{:S(2)}) collective-permute-start(bf16[256,512]{1,0:T(8,128)(2,1)} %bitcast.480), channel_id=1, source_target_pairs={{0,8},{8,0},{16,24},{24,16},{1,9},{9,1},{17,25},{25,17},{2,10},{10... | collective-permute-start | bytes 786440 | tf_op jit(solution)/shard_map/ppermute | solution.py:61
  799.3 12.2 collective-permute-start.25
  869.0 8.7 collective-permute-start.29
  870.5 7.9 collective-permute-start.28
  871.9 7.2 collective-permute-start.27
  915.7 298.5 %reduce-scatter.15.cloned.1.call-start = ((), (), s32[]{:S(2)}) async-start(), calls=%async_computation.16 | async-start | bytes 2359296 | tf_op jit(solution)/shard_map/reduce_scatter | solution.py:351
  920.7 48.6 %collective-permute-start.39 = (bf16[2048,512]{0,1:T(8,128)(2,1)S(1)}, bf16[2048,512]{0,1:T(8,128)(2,1)S(1)}, u32[]{:S(2)}, u32[]{:S(2)}) collective-permute-start(bf16[2048,512]{0,1:T(8,128)(2,1)S(1)} %get-tuple-element.469), channel_id=1, source_target_pairs={{0,8},{8,0},{16,24},{24,16},{1,9},{9,1},{17,25},{25,17},{2,10},{10... | collective-permute-start | bytes 6291464 | tf_op jit(solution)/shard_map/ppermute | solution.py:61
  922.2 90.9 %collective-permute-start.41 = (bf16[2048,512]{0,1:T(8,128)(2,1)S(1)}, bf16[2048,512]{0,1:T(8,128)(2,1)S(1)}, u32[]{:S(2)}, u32[]{:S(2)}) collective-permute-start(bf16[2048,512]{0,1:T(8,128)(2,1)S(1)} %get-tuple-element.470), channel_id=1, source_target_pairs={{0,24},{8,16},{16,8},{24,0},{1,25},{9,17},{17,9},{25,1},{2,26},{10... | collective-permute-start | bytes 6291464 | tf_op jit(solution)/shard_map/ppermute | solution.py:61
  923.6 90.9 %collective-permute-start.40 = (bf16[2048,512]{0,1:T(8,128)(2,1)S(1)}, bf16[2048,512]{0,1:T(8,128)(2,1)S(1)}, u32[]{:S(2)}, u32[]{:S(2)}) collective-permute-start(bf16[2048,512]{0,1:T(8,128)(2,1)S(1)} %get-tuple-element.471), channel_id=1, source_target_pairs={{0,16},{8,24},{16,0},{24,8},{1,17},{9,25},{17,1},{25,9},{2,18},{10... | collective-permute-start | bytes 6291464 | tf_op jit(solution)/shard_map/ppermute | solution.py:61
  1017.7 215.0 %reduce-scatter.17.cloned.1.call-start = ((), (), s32[]{:S(2)}) async-start(), calls=%async_computation.17 | async-start | bytes 14155776 | tf_op jit(solution)/shard_map/reduce_scatter | solution.py:351
  1061.2 27.0 %collective-permute-start.32 = (bf16[256,2048]{1,0:T(8,128)(2,1)S(1)}, bf16[256,2048]{1,0:T(8,128)(2,1)S(1)}, u32[]{:S(2)}, u32[]{:S(2)}) collective-permute-start(bf16[256,2048]{1,0:T(8,128)(2,1)S(1)} %get-tuple-element.493), channel_id=1, source_target_pairs={{0,24},{8,16},{16,8},{24,0},{1,25},{9,17},{17,9},{25,1},{2,26},{10... | collective-permute-start | bytes 3145736 | tf_op jit(solution)/shard_map/ppermute | solution.py:61
  1063.6 44.0 %collective-permute-start.31 = (bf16[256,2048]{1,0:T(8,128)(2,1)S(1)}, bf16[256,2048]{1,0:T(8,128)(2,1)S(1)}, u32[]{:S(2)}, u32[]{:S(2)}) collective-permute-start(bf16[256,2048]{1,0:T(8,128)(2,1)S(1)} %get-tuple-element.494), channel_id=1, source_target_pairs={{0,16},{8,24},{16,0},{24,8},{1,17},{9,25},{17,1},{25,9},{2,18},{10... | collective-permute-start | bytes 3145736 | tf_op jit(solution)/shard_map/ppermute | solution.py:61
  1064.2 43.5 %collective-permute-start.30 = (bf16[256,2048]{1,0:T(8,128)(2,1)S(1)}, bf16[256,2048]{1,0:T(8,128)(2,1)S(1)}, u32[]{:S(2)}, u32[]{:S(2)}) collective-permute-start(bf16[256,2048]{1,0:T(8,128)(2,1)S(1)} %get-tuple-element.495), channel_id=1, source_target_pairs={{0,8},{8,0},{16,24},{24,16},{1,9},{9,1},{17,25},{25,17},{2,10},{10... | collective-permute-start | bytes 3145736 | tf_op jit(solution)/shard_map/ppermute | solution.py:61
  1108.1 26.1 %collective-permute-start.33 = (bf16[256,2048]{1,0:T(8,128)(2,1)S(1)}, bf16[256,2048]{1,0:T(8,128)(2,1)S(1)}, u32[]{:S(2)}, u32[]{:S(2)}) collective-permute-start(bf16[256,2048]{1,0:T(8,128)(2,1)S(1)} %get-tuple-element.490), channel_id=1, source_target_pairs={{0,8},{8,0},{16,24},{24,16},{1,9},{9,1},{17,25},{25,17},{2,10},{10... | collective-permute-start | bytes 3145736 | tf_op jit(solution)/shard_map/ppermute | solution.py:61
  1109.7 47.1 %collective-permute-start.35 = (bf16[256,2048]{1,0:T(8,128)(2,1)S(1)}, bf16[256,2048]{1,0:T(8,128)(2,1)S(1)}, u32[]{:S(2)}, u32[]{:S(2)}) collective-permute-start(bf16[256,2048]{1,0:T(8,128)(2,1)S(1)} %get-tuple-element.491), channel_id=1, source_target_pairs={{0,24},{8,16},{16,8},{24,0},{1,25},{9,17},{17,9},{25,1},{2,26},{10... | collective-permute-start | bytes 3145736 | tf_op jit(solution)/shard_map/ppermute | solution.py:61
  1111.1 47.1 %collective-permute-start.34 = (bf16[256,2048]{1,0:T(8,128)(2,1)S(1)}, bf16[256,2048]{1,0:T(8,128)(2,1)S(1)}, u32[]{:S(2)}, u32[]{:S(2)}) collective-permute-start(bf16[256,2048]{1,0:T(8,128)(2,1)S(1)} %get-tuple-element.492), channel_id=1, source_target_pairs={{0,16},{8,24},{16,0},{24,8},{1,17},{9,25},{17,1},{25,9},{2,18},{10... | collective-permute-start | bytes 3145736 | tf_op jit(solution)/shard_map/ppermute | solution.py:61
  1163.0 22.7 %collective-permute-start.38 = (bf16[256,1664]{0,1:T(8,128)(2,1)S(1)}, bf16[256,1664]{0,1:T(8,128)(2,1)S(1)}, u32[]{:S(2)}, u32[]{:S(2)}) collective-permute-start(bf16[256,1664]{0,1:T(8,128)(2,1)S(1)} %copy-done.75), channel_id=1, source_target_pairs={{0,24},{8,16},{16,8},{24,0},{1,25},{9,17},{17,9},{25,1},{2,26},{10... | collective-permute-start | bytes 2555912 | tf_op jit(solution)/shard_map/ppermute | solution.py:61
  1164.5 36.5 %collective-permute-start.37 = (bf16[256,1664]{0,1:T(8,128)(2,1)S(1)}, bf16[256,1664]{0,1:T(8,128)(2,1)S(1)}, u32[]{:S(2)}, u32[]{:S(2)}) collective-permute-start(bf16[256,1664]{0,1:T(8,128)(2,1)S(1)} %copy-done.75), channel_id=1, source_target_pairs={{0,16},{8,24},{16,0},{24,8},{1,17},{9,25},{17,1},{25,9},{2,18},{10... | collective-permute-start | bytes 2555912 | tf_op jit(solution)/shard_map/ppermute | solution.py:61
  1164.8 36.1 %collective-permute-start.36 = (bf16[256,1664]{0,1:T(8,128)(2,1)S(1)}, bf16[256,1664]{0,1:T(8,128)(2,1)S(1)}, u32[]{:S(2)}, u32[]{:S(2)}) collective-permute-start(bf16[256,1664]{0,1:T(8,128)(2,1)S(1)} %copy-done.75), channel_id=1, source_target_pairs={{0,8},{8,0},{16,24},{24,16},{1,9},{9,1},{17,25},{25,17},{2,10},{10... | collective-permute-start | bytes 2555912 | tf_op jit(solution)/shard_map/ppermute | solution.py:61
  1214.2 9.4 collective-permute-start.42
  1215.6 15.1 %collective-permute-start.44 = (bf16[256,512]{0,1:T(8,128)(2,1)}, bf16[256,512]{0,1:T(8,128)(2,1)S(1)}, u32[]{:S(2)}, u32[]{:S(2)}) collective-permute-start(bf16[256,512]{0,1:T(8,128)(2,1)} %reduce-scatter.15.cloned.1.call-done), channel_id=1, source_target_pairs={{0,24},{8,16},{16,8},{24,0},{1,25},{9,17},{17,9},{25,1},{2,26},{10... | collective-permute-start | bytes 786440 | tf_op jit(solution)/shard_map/ppermute | solution.py:61
  1217.1 13.5 %collective-permute-start.43 = (bf16[256,512]{0,1:T(8,128)(2,1)}, bf16[256,512]{0,1:T(8,128)(2,1)S(1)}, u32[]{:S(2)}, u32[]{:S(2)}) collective-permute-start(bf16[256,512]{0,1:T(8,128)(2,1)} %reduce-scatter.15.cloned.1.call-done), channel_id=1, source_target_pairs={{0,16},{8,24},{16,0},{24,8},{1,17},{9,25},{17,1},{25,9},{2,18},{10... | collective-permute-start | bytes 786440 | tf_op jit(solution)/shard_map/ppermute | solution.py:61
  (149 other events, 1768.7 us)
Sparse Core Ops, SparseCore 0:
  23.5 72.1 all-gather.6
  97.9 28.7 all-gather.8
  128.4 115.6 all-gather.10
  245.6 114.8 all-gather.12
  362.0 114.8 all-gather.14
  478.4 114.8 all-gather.16
  595.6 127.3 reduce-scatter.6
  725.3 127.5 reduce-scatter.8
  855.2 127.5 reduce-scatter.12
  985.6 73.1 reduce-scatter.10
  1061.0 34.5 reduce-scatter.14
  1097.8 127.7 reduce-scatter.16

commit v4 on v3

--- a/solution.py
+++ b/solution.py
@@ -173,11 +173,28 @@
     return (stacked[:, :up_rows].reshape(-1, width), stacked[:, up_rows:].reshape(-1, width))
 
 
-def stack_rows(gate_up, down):
+def chip_sums(gate_up, down):
     count = lax.axis_size("fsdp")
+    core = lax.axis_index("fsdp") % 2
     width = gate_up.shape[-1]
-    parts = [grad.reshape(count, -1, width) for grad in (gate_up, down)]
-    return jnp.concatenate(parts, axis=1).reshape(-1, width)
+    parts = [grad.reshape(count // 2, 2, -1, width) for grad in (gate_up, down)]
+
+    def side(number):
+        return jnp.concatenate(
+            [lax.dynamic_index_in_dim(part, number, 1, False) for part in parts], axis=1
+        )
+
+    swapped = lax.ppermute(side(1 - core), "fsdp", [(index, index ^ 1) for index in range(count)])
+    total = side(core).astype(jnp.float32) + swapped.astype(jnp.float32)
+    return total.astype(gate_up.dtype).reshape(-1, width)
+
+
+def scatter_chips(rows):
+    count = lax.axis_size("fsdp")
+    groups = [list(range(core, count, 2)) for core in range(2)]
+    return lax.psum_scatter(
+        rows, "fsdp", scatter_dimension=0, tiled=True, axis_index_groups=groups
+    )
 
 
 def local(
@@ -353,17 +370,18 @@
     for index in range(local_count):
         kept = computed(index, pair)
         if index + 1 < local_count:
-            grads = stack_rows(*expert_weights(kept))
-            sums.append(scatter(after(grads, *sums[: max(0, index - 1)])))
+            grads = chip_sums(*expert_weights(kept))
             pair = after(picked(index + 1), grads)
+            if index + 2 < local_count:
+                sums.append(scatter_chips(grads))
     pick_all = jnp.concatenate([slot_pick[index] for index in range(local_count)], axis=1)
     grad_partial = mixed_dot("bct,bcd->btd", pick_all, jnp.concatenate(grad_row_sets, axis=1))
 
     grad_gates = return_blocks(jnp.stack(grad_slots, axis=1))
     grad_back = return_blocks(grad_partial.astype(bf16))
     moe_partial = mixed_dot("bct,bcd->btd", pick_all, jnp.concatenate(weighted_rows, axis=1))
-    grads = stack_rows(*expert_weights(kept))
-    grad_back = after(grad_back, grads, moe_partial.astype(bf16))
+    last_grads = expert_weights(kept)
+    grad_back = after(grad_back, last_grads, moe_partial.astype(bf16))
 
     own_gates = gates[0]
     grad_gates = jnp.transpose(in_rank_order(grad_gates), (2, 0, 1)).reshape(
@@ -393,13 +411,8 @@
         ]
     ).reshape(head_shape)
 
-    grad_branch = after(grad_branch, grad_heads)
-    grad_cut = mixed_dot("td,tc->dc", attended.reshape(tok_count, model_width), grad_branch)
-    grad_cut = grad_cut.astype(bf16).reshape(model_width, seq_count, own_width)
-    grad_cut = [
-        from_peer(lax.dynamic_index_in_dim(grad_cut, seq_rank ^ step, 1, False), step)
-        for step in range(seq_count)
-    ]
+    sums.append(scatter_chips(after(grads, grad_heads, *sums[:1])))
+    moe_parts = return_blocks(after(moe_partial.astype(bf16), grad_heads))
     zero_heads = jnp.zeros(head_shape, f32)
     (grad_keys, grad_values), grad_queries = lax.scan(
         partial(attend_back, heads_in, grad_heads, log_sums, places, length, row_count),
@@ -407,7 +420,7 @@
         block_starts,
     )
 
-    grad_cut = sum(part.astype(f32) for part in grad_cut).astype(bf16)
+    grad_queries = after(grad_queries, moe_parts)
     low = lambda rows: rows.reshape(head_shape).astype(bf16).astype(f32)
     grad_qn = rotate_back(low(grad_queries), cosine_table, sine_table).reshape(key_span, own_width)
     grad_kn = rotate_back(low(grad_keys), cosine_table, sine_table).reshape(key_span, own_width)
@@ -416,6 +429,16 @@
     inners = over_heads(
         jnp.stack([jnp.sum(scaled_q * unit_q, -1), jnp.sum(scaled_k * unit_k, -1)])
     )
+    grad_branch = after(grad_branch, inners)
+    grad_cut = mixed_dot("td,tc->dc", attended.reshape(tok_count, model_width), grad_branch)
+    grad_cut = grad_cut.astype(bf16).reshape(model_width, seq_count, own_width)
+    grad_cut = [
+        lax.dynamic_index_in_dim(grad_cut, seq_rank ^ step, 1, False) for step in range(seq_count)
+    ]
+    near_cuts = [from_peer(grad_cut[step], step) for step in range(min(3, seq_count))]
+    far_cuts = [
+        from_peer(after(grad_cut[step], near_cuts), step) for step in range(3, seq_count)
+    ]
     inners = (inners / model_width)[:, :, None]
     grad_projected = jnp.concatenate(
         [
@@ -447,12 +470,14 @@
         axis=0,
     )
     grad_front = jnp.concatenate([grad_qkv, grad_small.T.astype(bf16)], axis=1)
+    grad_front = after(grad_front, near_cuts)
 
     front_sum = scatter(after(grad_front, *sums[:-1]))
+    grad_cut = sum(part.astype(f32) for part in near_cuts + far_cuts).astype(bf16)
     out_sum = scatter(after(grad_cut, *sums, grad_front))
-    sums.append(scatter(after(grads, front_sum)))
+    last_grads = chip_sums(*after(last_grads, grad_front))
     grad_normed = return_blocks(grad_normed.astype(bf16).reshape(seq_count, tok_count, model_width))
-    moe_parts = return_blocks(after(moe_partial.astype(bf16), grad_normed))
+    front_parts = [from_peer(front_sum, step) for step in range(seq_count)]
     block_out = (middle + sum(part.astype(f32) for part in moe_parts)).astype(bf16)
     grad_normed = sum(part.astype(f32) for part in grad_normed)
     scale_one = rms_scale(inputs)
@@ -460,7 +485,6 @@
     unit_one = inputs * scale_one
     inner = jnp.mean(scaled * unit_one, axis=-1, keepdims=True)
     grad_tokens = (grad_middle + scale_one * (scaled - unit_one * inner)).astype(bf16)
-    front_parts = [from_peer(front_sum, step) for step in range(seq_count)]
     small_sum = sum(part[:, 3 * own_width :].astype(f32) for part in front_parts)
     qkv_sum = in_rank_order([part[:, : 3 * own_width] for part in front_parts])
     qkv_sum = jnp.transpose(
@@ -468,18 +492,32 @@
     ).reshape(-1, 3 * model_width)
     out_sum = in_rank_order([from_peer(out_sum, step) for step in range(seq_count)])
     out_sum = jnp.transpose(out_sum, (1, 0, 2)).reshape(-1, model_width)
+    last_sum = scatter_chips(after(last_grads, front_sum))
+    qkv_sum, out_sum = qkv_sum.astype(f32), out_sum.astype(f32)
+    up_sums = jnp.zeros((local_count, up_rows, model_width), f32)
+    down_sums = jnp.zeros((local_count,) + down_weight.shape[1:], f32)
+    for index in range(local_count):
+        if index + 1 == local_count:
+            last_sum, up_sums, down_sums, block_out, grad_tokens, qkv_sum, out_sum = (
+                lax.optimization_barrier(
+                    (last_sum, up_sums, down_sums, block_out, grad_tokens, qkv_sum, out_sum)
+                )
+            )
+        rows = (sums[index] if index + 1 < local_count else last_sum).astype(f32)
+        up_sums = lax.dynamic_update_slice(up_sums, rows[None, :up_rows], (index, 0, 0))
+        down_sums = lax.dynamic_update_slice(down_sums, rows[None, up_rows:], (index, 0, 0))
     return (
         block_out[None],
         grad_tokens[None],
         small_sum[:, 0],
-        qkv_sum.astype(f32),
+        qkv_sum,
         small_sum[:, 1],
         small_sum[:, 2],
-        out_sum.astype(f32),
+        out_sum,
         small_sum[:, 3],
         small_sum[:, 4:small_count],
-        jnp.stack([rows[:up_rows] for rows in sums]).astype(f32),
-        jnp.stack([rows[up_rows:] for rows in sums]).astype(f32),
+        up_sums,
+        down_sums,
     )
 
 

time: 1260 us -> 1180 us (0.937)
  waiting for transfers between devices: 593 us -> 417 us
  local copies, waits for them, and re-layouts: 174 us -> 225 us
  matrix products: 281 us -> 308 us
  other arithmetic: 122 us -> 144 us
    reduce_scatter x6 -> x2, waiting for transfers between devices: 100 us -> 0.01 us  [local(): lax.psum_scatter(grads, 'fsdp', scatter_dimension=0, tiled=True)]
    ppermute x45, waiting for transfers between devices: 428 us -> 340 us  [from_peer(): lax.ppermute(values, 'seq', [(rank, rank ^ step) for rank in range(count)])]
    convert_element_type x5 -> x14, other arithmetic: 11.2 us -> 58.2 us  [the longest x4 42.6 us: chip_sums(): return total.astype(gate_up.dtype).reshape(-1, width)]
    squeeze x2 -> x9, local copies, waits for them, and re-layouts: 2.18 us -> 35.6 us  [the longest x8 33.3 us: side(): lax.dynamic_index_in_dim(part, number, 1, False)]
    concatenate x4, other arithmetic: 36.4 us -> 14 us  [side(): jnp.concatenate([lax.dynamic_index_in_dim(part, number, 1, False) for par...]
    dot_general x40, matrix products: 236 us -> 255 us  [mixed_dot(): return jnp.einsum(form, left, right, preferred_element_type=jnp.float32)]
    dynamic_update_slice x0 -> x8, local copies, waits for them, and re-layouts: none -> 15.9 us  [the longest x4 8.89 us: local(): lax.dynamic_update_slice(up_sums, rows[None, :up_rows], (index, 0, 0))]
    reduce_scatter x0 -> x4, waiting for transfers between devices: none -> 12.8 us  [scatter_chips(): lax.psum_scatter(rows, 'fsdp', scatter_dimension=0, tiled=True, axis_inde...]
  transfers between devices with their start and end apart: 57 -> 61, of which waited for: 30 -> 29; matrix products, arithmetic and copies ran while one was open for 42% -> 53% of each run, Pallas kernels for 0% -> 0%
where the time goes in v4:
time: 1180 us
  waiting for transfers between devices  417 us (35%)
  matrix products  308 us (26%)
  local copies, waits for them, and re-layouts  225 us (19%)
  other arithmetic  144 us (12%)
  starting transfers between devices  54.6 us (5%)
  between operations  17.6 us (1%)
    ppermute x45, waiting for transfers between devices, from_peer(): lax.ppermute(values, 'seq', [(rank, rank ^ step) for rank in range(count)])  340 us
    dot_general x40, matrix products, mixed_dot(): return jnp.einsum(form, left, right, preferred_element_type=jnp.float32)  255 us
    all_gather x1, waiting for transfers between devices, local(): front_full = lax.all_gather(front, 'fsdp', axis=0, tiled=True)  64.8 us
    ppermute x45, starting transfers between devices, from_peer(): lax.ppermute(values, 'seq', [(rank, rank ^ step) for rank in range(count)])  53 us
    unnamed x297, local copies, waits for them, and re-layouts  43.4 us
    convert_element_type x4, other arithmetic, chip_sums(): return total.astype(gate_up.dtype).reshape(-1, width)  42.6 us
    slice x4, local copies, waits for them, and re-layouts, split_rows(): stacked[:, :up_rows].reshape(-1, width)  33.6 us
    squeeze x8, local copies, waits for them, and re-layouts, side(): lax.dynamic_index_in_dim(part, number, 1, False)  33.3 us
  transfers between devices with their start and end apart: 61, of which 29 were waited for; matrix products, arithmetic and copies ran while one was open for 53% of the time, Pallas kernels for 0%

profile of v4, /device:TPU:0, one launch (start us, length us, event | category | flops | bytes accessed | tf_op | source)
XLA Modules:
  0.0 1176.2 jit_solution(976468205330124969)
XLA Ops:
  7.2 7.5 reshape.532
  28.5 64.8 %all-gather.7.cloned.1.call-done = bf16[2048,1664]{0,1:T(8,128)(2,1)} async-done(((bf16[256,1664]{0,1:T(8,128)(2,1)}), bf16[2048,1664]{0,1:T(8,128)(2,1)}) %all-gather.7.cloned.1.call-update) | async-done | bytes 6815760 | tf_op jit(solution)/shard_map/all_gather | solution.py:248
  103.5 16.0 %collective-permute-done = bf16[256,2048]{1,0:T(8,128)(2,1)S(1)} collective-permute-done((bf16[256,2048]{1,0:T(8,128)(2,1)S(1)}, bf16[256,2048]{1,0:T(8,128)(2,1)S(1)}, u32[]{:S(2)}, u32[]{:S(2)}) %collective-permute-start) | collective-permute-done | bytes 1048608 | tf_op jit(solution)/shard_map/ppermute | solution.py:61
  119.5 22.9 %collective-permute-done.1 = bf16[256,2048]{1,0:T(8,128)(2,1)S(1)} collective-permute-done((bf16[256,2048]{1,0:T(8,128)(2,1)S(1)}, bf16[256,2048]{1,0:T(8,128)(2,1)S(1)}, u32[]{:S(2)}, u32[]{:S(2)}) %collective-permute-start.1) | collective-permute-done | bytes 1048608 | tf_op jit(solution)/shard_map/ppermute | solution.py:61
  146.7 6.7 fusion.54
  174.1 25.1 %while.28 = (s32[]{:T(128)}, bf16[2,512,4,128]{3,2,1,0:T(4,128)(2,1)}, f32[2,512,4]{1,2,0:T(4,128)S(1)}, s32[2]{0:T(128)S(1)}, s32[1024]{0:T(1024)S(1)}, /*index...) while((s32[]{:T(128)}, ...), condition=%wide.region_9.10_spmd.clone, body=%wide.region_6.9_spmd.clone.sunk | while | flops 1100218368 | bytes 31552204 | solution.py:301
  208.3 18.4 %collective-permute-done.9 = bf16[256,512]{1,0:T(8,128)(2,1)} collective-permute-done((bf16[256,512]{1,0:T(8,128)(2,1)}, bf16[256,512]{1,0:T(8,128)(2,1)}, u32[]{:S(2)}, u32[]{:S(2)}) %collective-permute-start.9) | collective-permute-done | bytes 262176 | tf_op jit(solution)/shard_map/ppermute | solution.py:61
  234.1 41.1 %collective-permute-done.10 = bf16[256,512]{1,0:T(8,128)(2,1)} collective-permute-done((bf16[256,512]{1,0:T(8,128)(2,1)}, bf16[256,512]{1,0:T(8,128)(2,1)}, u32[]{:S(2)}, u32[]{:S(2)}) %collective-permute-start.10) | collective-permute-done | bytes 262176 | tf_op jit(solution)/shard_map/ppermute | solution.py:61
  287.6 6.2 multiply_reduce_fusion.8
  304.0 21.0 %collective-permute-done.3 = bf16[257,2048]{1,0:T(8,128)(2,1)} collective-permute-done((bf16[257,2048]{1,0:T(8,128)(2,1)}, bf16[257,2048]{1,0:T(8,128)(2,1)}, u32[]{:S(2)}, u32[]{:S(2)}) %collective-permute-start.3) | collective-permute-done | bytes 1052704 | tf_op jit(solution)/shard_map/ppermute | solution.py:61
  325.0 18.4 %collective-permute-done.4 = bf16[257,2048]{1,0:T(8,128)(2,1)} collective-permute-done((bf16[257,2048]{1,0:T(8,128)(2,1)}, bf16[257,2048]{1,0:T(8,128)(2,1)}, u32[]{:S(2)}, u32[]{:S(2)}) %collective-permute-start.4) | collective-permute-done | bytes 1052704 | tf_op jit(solution)/shard_map/ppermute | solution.py:61
  353.2 20.7 %collective-permute-done.15 = bf16[256,2048]{1,0:T(8,128)(2,1)S(1)} collective-permute-done((bf16[256,2048]{1,0:T(8,128)(2,1)}, bf16[256,2048]{1,0:T(8,128)(2,1)S(1)}, u32[]{:S(2)}, u32[]{:S(2)}) %collective-permute-start.15) | collective-permute-done | bytes 1048608 | tf_op jit(solution)/shard_map/ppermute | solution.py:61
  374.0 15.8 %collective-permute-done.16 = bf16[256,2048]{1,0:T(8,128)(2,1)S(1)} collective-permute-done((bf16[256,2048]{1,0:T(8,128)(2,1)}, bf16[256,2048]{1,0:T(8,128)(2,1)S(1)}, u32[]{:S(2)}, u32[]{:S(2)}) %collective-permute-start.16) | collective-permute-done | bytes 1048608 | tf_op jit(solution)/shard_map/ppermute | solution.py:61
  400.7 6.8 multiply_convert_fusion.3
  407.7 8.5 slice.480
  422.5 5.1 fusion.167
  438.2 9.6 convolution_convert_fusion.5
  447.8 6.9 dynamic-slice_bitcast_fusion.8
  467.2 8.3 slice.485
  475.6 4.8 slice.484
  480.4 11.8 %add_convert_fusion.3 = bf16[4,384,2048]{2,1,0:T(8,128)(2,1)} fusion(bf16[4,384,2048]{2,1,0:T(8,128)(2,1)} %collective-permute-done.18, bf16[4,128,2048]{2,1,0:T(8,128)(2,1)S(1)} %get-tuple-element.545, bf16[4,256,2048]{2,1,0:T(8,128)(2,1)} %get-tuple-element.507), kind=kLoop, calls=%fused_computation.59 | loop fusion | flops 22020096 | bytes 18874368 | tf_op jit(solution)/shard_map/convert_element_type | solution.py:189
  492.2 8.5 fusion.168
  509.9 9.1 convolution_convert_fusion.4
  519.0 6.8 dynamic-slice_bitcast_fusion.6
  550.3 8.4 slice.490
  558.8 4.7 slice.489
  563.5 10.3 add_convert_fusion.2
  573.8 8.4 fusion.169
  591.3 9.3 convolution_convert_fusion.3
  600.6 6.7 dynamic-slice_bitcast_fusion.4
  610.8 8.0 fusion.59
  618.9 9.2 convolution_convert_fusion.13
  628.1 8.3 slice.495
  636.5 5.1 slice.494
  646.6 9.5 convolution_convert_fusion.12
  660.4 9.5 convolution_convert_fusion.11
  670.0 10.3 add_convert_fusion.1
  680.2 8.3 fusion.170
  688.6 5.0 multiply_convert_fusion.7
  699.0 10.0 convolution_convert_fusion.10
  709.0 5.4 fusion.70
  719.6 6.9 fusion.67
  726.5 10.9 convolution_convert_fusion.2
  737.4 5.3 convolution_convert_fusion.6
  745.7 19.8 %collective-permute-done.22 = f32[4,256]{1,0:T(4,128)S(1)} collective-permute-done((f32[4,256]{1,0:T(4,128)S(1)}, f32[4,256]{1,0:T(4,128)S(1)}, u32[]{:S(2)}, u32[]{:S(2)}) %collective-permute-start.22) | collective-permute-done | bytes 4128 | tf_op jit(solution)/shard_map/ppermute | solution.py:61
  772.7 5.7 fusion.74
  791.6 4.9 collective-permute-done.28
  806.2 51.5 %while.29 = (s32[]{:T(128)}, f32[1024,4,128]{0,2,1:T(8,128)S(1)}, f32[1024,4,128]{0,2,1:T(8,128)}, bf16[2,512,4,128]{3,1,2,0:T(8,128)(2,1)}, s32[2]{0:T(128)S(1)...) while((s32[]{:T(128)}, f32[1024,4,128]{0,2,1:T(8,128)S(1)}, ...), condition=%wide.region_26.27_spmd.clone, body=%wide.region_24.26_spmd.clone.sunk | while | flops 2719744000 | bytes 181490704 | solution.py:417
  852.7 5.0 bitcast_add_fusion.5
  892.9 12.0 %fusion.156 = (bf16[1024,2048]{1,0:T(8,128)(2,1)}, bf16[2048]{0:T(1024)(128)(2,1)S(1)}) fusion(f32[1024]{0:T(1024)S(1)} %bitcast.688, bf16[4,256,2048]{2,1,0:T(8,128)(2,1)S(1)} %copy-done.20, bf16[2048,1664]{0,1:T(8,128)(2,1)} %all-gather.7.cloned.1.call-done, bf16[1024,512]{1,0:T(8,128)(2,1)S(1)} %copy-done.67, ...), kind=kOutput, calls=%fused_computation.435 | convolution fusion | flops 6462371840 | bytes 17833984 | tf_op jit(solution)/shard_map/te,de->td/dot_general | solution.py:134
  905.8 10.8 convolution_convert_fusion.1
  916.6 6.9 pad_maximum_fusion
  923.5 7.3 collective-permute-done.36
  936.2 7.5 dynamic-slice_bitcast_fusion.2
  955.0 48.0 %collective-permute-done.45 = bf16[2048,512]{0,1:T(8,128)(2,1)S(1)} collective-permute-done((bf16[2048,512]{0,1:T(8,128)(2,1)}, bf16[2048,512]{0,1:T(8,128)(2,1)S(1)}, u32[]{:S(2)}, u32[]{:S(2)}) %collective-permute-start.45) | collective-permute-done | bytes 2097184 | tf_op jit(solution)/shard_map/ppermute | solution.py:61
  1003.0 5.3 add_convert_fusion.4
  1009.9 10.3 add_convert_fusion
  1038.8 13.8 %collective-permute-done.39 = bf16[256,2048]{1,0:T(8,128)(2,1)S(1)} collective-permute-done((bf16[256,2048]{1,0:T(8,128)(2,1)S(1)}, bf16[256,2048]{1,0:T(8,128)(2,1)S(1)}, u32[]{:S(2)}, u32[]{:S(2)}) %collective-permute-start.39) | collective-permute-done | bytes 1048608 | tf_op jit(solution)/shard_map/ppermute | solution.py:61
  1052.6 21.3 %collective-permute-done.40 = bf16[256,2048]{1,0:T(8,128)(2,1)S(1)} collective-permute-done((bf16[256,2048]{1,0:T(8,128)(2,1)S(1)}, bf16[256,2048]{1,0:T(8,128)(2,1)S(1)}, u32[]{:S(2)}, u32[]{:S(2)}) %collective-permute-start.40) | collective-permute-done | bytes 1048608 | tf_op jit(solution)/shard_map/ppermute | solution.py:61
  1094.9 6.3 collective-permute-done.47
  1104.4 13.2 %collective-permute-done.42 = bf16[256,1664]{0,1:T(8,128)(2,1)S(1)} collective-permute-done((bf16[256,1664]{0,1:T(8,128)(2,1)}, bf16[256,1664]{0,1:T(8,128)(2,1)S(1)}, u32[]{:S(2)}, u32[]{:S(2)}) %collective-permute-start.42) | collective-permute-done | bytes 852000 | tf_op jit(solution)/shard_map/ppermute | solution.py:61
  1117.6 19.5 %collective-permute-done.43 = bf16[256,1664]{0,1:T(8,128)(2,1)S(1)} collective-permute-done((bf16[256,1664]{0,1:T(8,128)(2,1)}, bf16[256,1664]{0,1:T(8,128)(2,1)S(1)}, u32[]{:S(2)}, u32[]{:S(2)}) %collective-permute-start.43) | collective-permute-done | bytes 852000 | tf_op jit(solution)/shard_map/ppermute | solution.py:61
  1143.4 12.8 %reduce-scatter.13.cloned.1.call-done = bf16[384,2048]{1,0:T(8,128)(2,1)} async-done(((bf16[1536,2048]{1,0:T(8,128)(2,1)}), bf16[384,2048]{1,0:T(8,128)(2,1)}) %reduce-scatter.13.cloned.1.call-update) | async-done | bytes 1572880 | tf_op jit(solution)/shard_map/reduce_scatter | solution.py:195
  1160.5 6.6 copy.255
  (719 shorter events, 407.3 us)
Async XLA Ops:
  7.2 86.1 %all-gather.7.cloned.1.call-start = ((), (), s32[]{:S(2)}) async-start(), calls=%async_computation.6 | async-start | bytes 7667712 | tf_op jit(solution)/shard_map/all_gather | solution.py:248
  20.9 151.2 %all-gather.9.cloned.1.call-start = ((), (), s32[]{:S(2)}) async-start(), calls=%async_computation.7 | async-start | bytes 2359296 | tf_op jit(solution)/shard_map/all_gather | solution.py:251
  21.9 385.8 %all-gather.11.cloned.1.call-start = ((), (), s32[]{:S(2)}) async-start(), calls=%async_computation.8 | async-start | bytes 14155776 | tf_op jit(solution)/shard_map/all_gather | solution.py:252
  93.3 373.9 %all-gather.13.cloned.1.call-start = ((), (), s32[]{:S(2)}) async-start(), calls=%async_computation.9 | async-start | bytes 14155776 | tf_op jit(solution)/shard_map/all_gather | solution.py:252
  93.4 26.1 %collective-permute-start = (bf16[256,2048]{1,0:T(8,128)(2,1)S(1)}, bf16[256,2048]{1,0:T(8,128)(2,1)S(1)}, u32[]{:S(2)}, u32[]{:S(2)}) collective-permute-start(bf16[256,2048]{1,0:T(8,128)(2,1)S(1)} %bitcast.577), channel_id=1, source_target_pairs={{0,8},{8,0},{16,24},{24,16},{1,9},{9,1},{17,25},{25,17},{2,10},{10... | collective-permute-start | bytes 3145736 | tf_op jit(solution)/shard_map/ppermute | solution.py:61
  94.9 47.5 %collective-permute-start.1 = (bf16[256,2048]{1,0:T(8,128)(2,1)S(1)}, bf16[256,2048]{1,0:T(8,128)(2,1)S(1)}, u32[]{:S(2)}, u32[]{:S(2)}) collective-permute-start(bf16[256,2048]{1,0:T(8,128)(2,1)S(1)} %bitcast.578), channel_id=1, source_target_pairs={{0,16},{8,24},{16,0},{24,8},{1,17},{9,25},{17,1},{25,9},{2,18},{10... | collective-permute-start | bytes 3145736 | tf_op jit(solution)/shard_map/ppermute | solution.py:61
  96.4 46.0 %collective-permute-start.2 = (bf16[256,2048]{1,0:T(8,128)(2,1)S(1)}, bf16[256,2048]{1,0:T(8,128)(2,1)S(1)}, u32[]{:S(2)}, u32[]{:S(2)}) collective-permute-start(bf16[256,2048]{1,0:T(8,128)(2,1)S(1)} %bitcast.579), channel_id=1, source_target_pairs={{0,24},{8,16},{16,8},{24,0},{1,25},{9,17},{17,9},{25,1},{2,26},{10... | collective-permute-start | bytes 3145736 | tf_op jit(solution)/shard_map/ppermute | solution.py:61
  144.2 249.3 %copy-start.69 = (bf16[20,2048]{1,0:T(8,128)(2,1)}, bf16[20,2048]{1,0:T(8,128)(2,1)S(1)}, u32[]{:S(2)}) copy-start(bf16[20,2048]{1,0:T(8,128)(2,1)S(1)} %slice_bitcast_fusion.47) | copy-start | bytes 245764
  144.2 208.7 %copy-start.81 = (f32[1,2048]{1,0:T(1,128)}, f32[1,2048]{1,0:T(1,128)S(1)}, u32[]{:S(2)}) copy-start(f32[1,2048]{1,0:T(1,128)S(1)} %get-tuple-element.587) | copy-start | bytes 24580
  156.4 3.7 collective-permute-start.6
  157.7 3.7 collective-permute-start.7
  158.6 4.5 collective-permute-start.8
  169.6 380.7 %all-gather.15.cloned.1.call-start = ((), (), s32[]{:S(2)}) async-start(), calls=%async_computation.10 | async-start | bytes 14155776 | tf_op jit(solution)/shard_map/all_gather | solution.py:252
  172.1 105.4 %collective-permute-start.12 = (bf16[2048,512]{0,1:T(8,128)(2,1)}, bf16[2048,512]{0,1:T(8,128)(2,1)}, u32[]{:S(2)}, u32[]{:S(2)}) collective-permute-start(bf16[2048,512]{0,1:T(8,128)(2,1)} %all-gather.9.cloned.1.call-done), channel_id=1, source_target_pairs={{0,8},{8,0},{16,24},{24,16},{1,9},{9,1},{17,25},{25,17},{2,10},{10... | collective-permute-start | bytes 6291464 | tf_op jit(solution)/shard_map/ppermute | solution.py:61
  173.6 107.4 %collective-permute-start.13 = (bf16[2048,512]{0,1:T(8,128)(2,1)}, bf16[2048,512]{0,1:T(8,128)(2,1)}, u32[]{:S(2)}, u32[]{:S(2)}) collective-permute-start(bf16[2048,512]{0,1:T(8,128)(2,1)} %all-gather.9.cloned.1.call-done), channel_id=1, source_target_pairs={{0,16},{8,24},{16,0},{24,8},{1,17},{9,25},{17,1},{25,9},{2,18},{10... | collective-permute-start | bytes 6291464 | tf_op jit(solution)/shard_map/ppermute | solution.py:61
  204.7 21.9 %collective-permute-start.9 = (bf16[256,512]{1,0:T(8,128)(2,1)}, bf16[256,512]{1,0:T(8,128)(2,1)}, u32[]{:S(2)}, u32[]{:S(2)}) collective-permute-start(bf16[256,512]{1,0:T(8,128)(2,1)} %get-tuple-element.577), channel_id=1, source_target_pairs={{0,8},{8,0},{16,24},{24,16},{1,9},{9,1},{17,25},{25,17},{2,10},{10... | collective-permute-start | bytes 786440 | tf_op jit(solution)/shard_map/ppermute | solution.py:61
  205.9 78.3 %collective-permute-start.14 = (bf16[2048,512]{0,1:T(8,128)(2,1)}, bf16[2048,512]{0,1:T(8,128)(2,1)}, u32[]{:S(2)}, u32[]{:S(2)}) collective-permute-start(bf16[2048,512]{0,1:T(8,128)(2,1)} %all-gather.9.cloned.1.call-done), channel_id=1, source_target_pairs={{0,24},{8,16},{16,8},{24,0},{1,25},{9,17},{17,9},{25,1},{2,26},{10... | collective-permute-start | bytes 6291464 | tf_op jit(solution)/shard_map/ppermute | solution.py:61
  207.8 67.4 %collective-permute-start.10 = (bf16[256,512]{1,0:T(8,128)(2,1)}, bf16[256,512]{1,0:T(8,128)(2,1)}, u32[]{:S(2)}, u32[]{:S(2)}) collective-permute-start(bf16[256,512]{1,0:T(8,128)(2,1)} %get-tuple-element.576), channel_id=1, source_target_pairs={{0,16},{8,24},{16,0},{24,8},{1,17},{9,25},{17,1},{25,9},{2,18},{10... | collective-permute-start | bytes 786440 | tf_op jit(solution)/shard_map/ppermute | solution.py:61
  226.6 49.7 %collective-permute-start.11 = (bf16[256,512]{1,0:T(8,128)(2,1)}, bf16[256,512]{1,0:T(8,128)(2,1)}, u32[]{:S(2)}, u32[]{:S(2)}) collective-permute-start(bf16[256,512]{1,0:T(8,128)(2,1)} %get-tuple-element.575), channel_id=1, source_target_pairs={{0,24},{8,16},{16,8},{24,0},{1,25},{9,17},{17,9},{25,1},{2,26},{10... | collective-permute-start | bytes 786440 | tf_op jit(solution)/shard_map/ppermute | solution.py:61
  295.3 332.8 %all-gather.17.cloned.1.call-start = ((), (), s32[]{:S(2)}) async-start(), calls=%async_computation.11 | async-start | bytes 14155776 | tf_op jit(solution)/shard_map/all_gather | solution.py:252
  298.0 27.1 %collective-permute-start.3 = (bf16[257,2048]{1,0:T(8,128)(2,1)}, bf16[257,2048]{1,0:T(8,128)(2,1)}, u32[]{:S(2)}, u32[]{:S(2)}) collective-permute-start(bf16[257,2048]{1,0:T(8,128)(2,1)} %pad_maximum_fusion.30), channel_id=1, source_target_pairs={{0,8},{8,0},{16,24},{24,16},{1,9},{9,1},{17,25},{25,17},{2,10},{10... | collective-permute-start | bytes 3158024 | tf_op jit(solution)/shard_map/ppermute | solution.py:61
  298.4 45.0 %collective-permute-start.4 = (bf16[257,2048]{1,0:T(8,128)(2,1)}, bf16[257,2048]{1,0:T(8,128)(2,1)}, u32[]{:S(2)}, u32[]{:S(2)}) collective-permute-start(bf16[257,2048]{1,0:T(8,128)(2,1)} %pad_maximum_fusion.30), channel_id=1, source_target_pairs={{0,16},{8,24},{16,0},{24,8},{1,17},{9,25},{17,1},{25,9},{2,18},{10... | collective-permute-start | bytes 3158024 | tf_op jit(solution)/shard_map/ppermute | solution.py:61
  299.9 43.6 %collective-permute-start.5 = (bf16[257,2048]{1,0:T(8,128)(2,1)}, bf16[257,2048]{1,0:T(8,128)(2,1)}, u32[]{:S(2)}, u32[]{:S(2)}) collective-permute-start(bf16[257,2048]{1,0:T(8,128)(2,1)} %pad_maximum_fusion.30), channel_id=1, source_target_pairs={{0,24},{8,16},{16,8},{24,0},{1,25},{9,17},{17,9},{25,1},{2,26},{10... | collective-permute-start | bytes 3158024 | tf_op jit(solution)/shard_map/ppermute | solution.py:61
  347.7 26.3 %collective-permute-start.15 = (bf16[256,2048]{1,0:T(8,128)(2,1)}, bf16[256,2048]{1,0:T(8,128)(2,1)S(1)}, u32[]{:S(2)}, u32[]{:S(2)}) collective-permute-start(bf16[256,2048]{1,0:T(8,128)(2,1)} %multiply_convert_fusion.20), channel_id=1, source_target_pairs={{0,8},{8,0},{16,24},{24,16},{1,9},{9,1},{17,25},{25,17},{2,10},{10... | collective-permute-start | bytes 3145736 | tf_op jit(solution)/shard_map/ppermute | solution.py:61
  349.2 40.6 %collective-permute-start.16 = (bf16[256,2048]{1,0:T(8,128)(2,1)}, bf16[256,2048]{1,0:T(8,128)(2,1)S(1)}, u32[]{:S(2)}, u32[]{:S(2)}) collective-permute-start(bf16[256,2048]{1,0:T(8,128)(2,1)} %multiply_convert_fusion.20), channel_id=1, source_target_pairs={{0,16},{8,24},{16,0},{24,8},{1,17},{9,25},{17,1},{25,9},{2,18},{10... | collective-permute-start | bytes 3145736 | tf_op jit(solution)/shard_map/ppermute | solution.py:61
  349.6 41.6 %collective-permute-start.17 = (bf16[256,2048]{1,0:T(8,128)(2,1)}, bf16[256,2048]{1,0:T(8,128)(2,1)S(1)}, u32[]{:S(2)}, u32[]{:S(2)}) collective-permute-start(bf16[256,2048]{1,0:T(8,128)(2,1)} %multiply_convert_fusion.20), channel_id=1, source_target_pairs={{0,24},{8,16},{16,8},{24,0},{1,25},{9,17},{17,9},{25,1},{2,26},{10... | collective-permute-start | bytes 3145736 | tf_op jit(solution)/shard_map/ppermute | solution.py:61
  353.0 193.0 %copy-start.35 = (pred[4,4,144,256]{3,2,1,0:T(8,128)(4,1)}, pred[4,4,144,256]{3,2,1,0:T(8,128)(4,1)S(1)}, u32[]{:S(2)}) copy-start(pred[4,4,144,256]{3,2,1,0:T(8,128)(4,1)S(1)} %get-tuple-element.598) | copy-start | bytes 1769476
  407.6 398.5 %reduce-scatter.7.cloned.1.call-start = ((), (), s32[]{:S(2)}) async-start(), calls=%async_computation.12 | async-start | bytes 7864320 | tf_op jit(solution)/shard_map/reduce_scatter | solution.py:195
  458.3 22.0 %collective-permute-start.18 = (bf16[4,384,2048]{2,1,0:T(8,128)(2,1)}, bf16[4,384,2048]{2,1,0:T(8,128)(2,1)}, u32[]{:S(2)}, u32[]{:S(2)}) collective-permute-start(bf16[4,384,2048]{2,1,0:T(8,128)(2,1)} %pad_maximum_fusion.1), channel_id=1, source_target_pairs={{0,1},{1,0},{2,3},{3,2},{4,5},{5,4},{6,7},{7,6},{8,9},{9,8},{10,11... | collective-permute-start | bytes 18874376 | tf_op jit(solution)/shard_map/ppermute | solution.py:187
  529.3 34.2 %collective-permute-start.19 = (bf16[4,384,2048]{2,1,0:T(8,128)(2,1)}, bf16[4,384,2048]{2,1,0:T(8,128)(2,1)}, u32[]{:S(2)}, u32[]{:S(2)}) collective-permute-start(bf16[4,384,2048]{2,1,0:T(8,128)(2,1)} %pad_maximum_fusion.2), channel_id=1, source_target_pairs={{0,1},{1,0},{2,3},{3,2},{4,5},{5,4},{6,7},{7,6},{8,9},{9,8},{10,11... | collective-permute-start | bytes 18874376 | tf_op jit(solution)/shard_map/ppermute | solution.py:187
  540.9 391.2 %reduce-scatter.9.cloned.1.call-start = ((), (), s32[]{:S(2)}) async-start(), calls=%async_computation.13 | async-start | bytes 7864320 | tf_op jit(solution)/shard_map/reduce_scatter | solution.py:195
  610.8 59.2 %collective-permute-start.20 = (bf16[4,384,2048]{2,1,0:T(8,128)(2,1)}, bf16[4,384,2048]{2,1,0:T(8,128)(2,1)}, u32[]{:S(2)}, u32[]{:S(2)}) collective-permute-start(bf16[4,384,2048]{2,1,0:T(8,128)(2,1)} %pad_maximum_fusion.3), channel_id=1, source_target_pairs={{0,1},{1,0},{2,3},{3,2},{4,5},{5,4},{6,7},{7,6},{8,9},{9,8},{10,11... | collective-permute-start | bytes 18874376 | tf_op jit(solution)/shard_map/ppermute | solution.py:187
  660.4 347.9 %reduce-scatter.15.cloned.1.call-start = ((), (), s32[]{:S(2)}) async-start(), calls=%async_computation.16 | async-start | bytes 7864320 | tf_op jit(solution)/shard_map/reduce_scatter | solution.py:195
  698.2 46.2 %collective-permute-start.21 = (f32[4,256]{1,0:T(4,128)S(1)}, f32[4,256]{1,0:T(4,128)S(1)}, u32[]{:S(2)}, u32[]{:S(2)}) collective-permute-start(f32[4,256]{1,0:T(4,128)S(1)} %get-tuple-element.595), channel_id=1, source_target_pairs={{0,8},{8,0},{16,24},{24,16},{1,9},{9,1},{17,25},{25,17},{2,10},{10... | collective-permute-start | bytes 12296 | tf_op jit(solution)/shard_map/ppermute | solution.py:61
  716.1 49.5 %collective-permute-start.24 = (bf16[256,2048]{1,0:T(8,128)(2,1)}, bf16[256,2048]{1,0:T(8,128)(2,1)}, u32[]{:S(2)}, u32[]{:S(2)}) collective-permute-start(bf16[256,2048]{1,0:T(8,128)(2,1)} %get-tuple-element.535), channel_id=1, source_target_pairs={{0,8},{8,0},{16,24},{24,16},{1,9},{9,1},{17,25},{25,17},{2,10},{10... | collective-permute-start | bytes 3145736 | tf_op jit(solution)/shard_map/ppermute | solution.py:61
  717.5 48.1 %collective-permute-start.25 = (bf16[256,2048]{1,0:T(8,128)(2,1)}, bf16[256,2048]{1,0:T(8,128)(2,1)}, u32[]{:S(2)}, u32[]{:S(2)}) collective-permute-start(bf16[256,2048]{1,0:T(8,128)(2,1)} %get-tuple-element.534), channel_id=1, source_target_pairs={{0,16},{8,24},{16,0},{24,8},{1,17},{9,25},{17,1},{25,9},{2,18},{10... | collective-permute-start | bytes 3145736 | tf_op jit(solution)/shard_map/ppermute | solution.py:61
  718.2 47.4 %collective-permute-start.26 = (bf16[256,2048]{1,0:T(8,128)(2,1)}, bf16[256,2048]{1,0:T(8,128)(2,1)}, u32[]{:S(2)}, u32[]{:S(2)}) collective-permute-start(bf16[256,2048]{1,0:T(8,128)(2,1)} %get-tuple-element.533), channel_id=1, source_target_pairs={{0,24},{8,16},{16,8},{24,0},{1,25},{9,17},{17,9},{25,1},{2,26},{10... | collective-permute-start | bytes 3145736 | tf_op jit(solution)/shard_map/ppermute | solution.py:61
  742.8 22.8 %collective-permute-start.22 = (f32[4,256]{1,0:T(4,128)S(1)}, f32[4,256]{1,0:T(4,128)S(1)}, u32[]{:S(2)}, u32[]{:S(2)}) collective-permute-start(f32[4,256]{1,0:T(4,128)S(1)} %get-tuple-element.594), channel_id=1, source_target_pairs={{0,16},{8,24},{16,0},{24,8},{1,17},{9,25},{17,1},{25,9},{2,18},{10... | collective-permute-start | bytes 12296 | tf_op jit(solution)/shard_map/ppermute | solution.py:61
  744.4 21.1 %collective-permute-start.23 = (f32[4,256]{1,0:T(4,128)S(1)}, f32[4,256]{1,0:T(4,128)S(1)}, u32[]{:S(2)}, u32[]{:S(2)}) collective-permute-start(f32[4,256]{1,0:T(4,128)S(1)} %get-tuple-element.593), channel_id=1, source_target_pairs={{0,24},{8,16},{16,8},{24,0},{1,25},{9,17},{17,9},{25,1},{2,26},{10... | collective-permute-start | bytes 12296 | tf_op jit(solution)/shard_map/ppermute | solution.py:61
  782.2 9.4 collective-permute-start.27
  782.8 13.7 %collective-permute-start.28 = (bf16[256,512]{1,0:T(8,128)(2,1)S(1)}, bf16[256,512]{1,0:T(8,128)(2,1)}, u32[]{:S(2)}, u32[]{:S(2)}) collective-permute-start(bf16[256,512]{1,0:T(8,128)(2,1)S(1)} %bitcast.647), channel_id=1, source_target_pairs={{0,16},{8,24},{16,0},{24,8},{1,17},{9,25},{17,1},{25,9},{2,18},{10... | collective-permute-start | bytes 786440 | tf_op jit(solution)/shard_map/ppermute | solution.py:61
  784.4 12.1 %collective-permute-start.29 = (bf16[256,512]{1,0:T(8,128)(2,1)S(1)}, bf16[256,512]{1,0:T(8,128)(2,1)}, u32[]{:S(2)}, u32[]{:S(2)}) collective-permute-start(bf16[256,512]{1,0:T(8,128)(2,1)S(1)} %bitcast.648), channel_id=1, source_target_pairs={{0,24},{8,16},{16,8},{24,0},{1,25},{9,17},{17,9},{25,1},{2,26},{10... | collective-permute-start | bytes 786440 | tf_op jit(solution)/shard_map/ppermute | solution.py:61
  802.5 59.1 %collective-permute-start.30 = (bf16[256,2048]{1,0:T(8,128)(2,1)}, bf16[256,2048]{1,0:T(8,128)(2,1)}, u32[]{:S(2)}, u32[]{:S(2)}) collective-permute-start(bf16[256,2048]{1,0:T(8,128)(2,1)} %get-tuple-element.532), channel_id=1, source_target_pairs={{0,8},{8,0},{16,24},{24,16},{1,9},{9,1},{17,25},{25,17},{2,10},{10... | collective-permute-start | bytes 3145736 | tf_op jit(solution)/shard_map/ppermute | solution.py:61
  804.0 57.6 %collective-permute-start.31 = (bf16[256,2048]{1,0:T(8,128)(2,1)}, bf16[256,2048]{1,0:T(8,128)(2,1)}, u32[]{:S(2)}, u32[]{:S(2)}) collective-permute-start(bf16[256,2048]{1,0:T(8,128)(2,1)} %get-tuple-element.531), channel_id=1, source_target_pairs={{0,16},{8,24},{16,0},{24,8},{1,17},{9,25},{17,1},{25,9},{2,18},{10... | collective-permute-start | bytes 3145736 | tf_op jit(solution)/shard_map/ppermute | solution.py:61
  804.6 57.0 %collective-permute-start.32 = (bf16[256,2048]{1,0:T(8,128)(2,1)}, bf16[256,2048]{1,0:T(8,128)(2,1)}, u32[]{:S(2)}, u32[]{:S(2)}) collective-permute-start(bf16[256,2048]{1,0:T(8,128)(2,1)} %get-tuple-element.530), channel_id=1, source_target_pairs={{0,24},{8,16},{16,8},{24,0},{1,25},{9,17},{17,9},{25,1},{2,26},{10... | collective-permute-start | bytes 3145736 | tf_op jit(solution)/shard_map/ppermute | solution.py:61
  806.1 214.1 %reduce-scatter.11.cloned.1.call-start = ((), (), s32[]{:S(2)}) async-start(), calls=%async_computation.14 | async-start | bytes 7667712 | tf_op jit(solution)/shard_map/reduce_scatter | solution.py:368
  871.4 3.7 collective-permute-start.33
  872.9 3.7 collective-permute-start.34
  873.7 4.5 collective-permute-start.35
  887.2 43.7 %collective-permute-start.36 = (bf16[2048,512]{0,1:T(8,128)(2,1)}, bf16[2048,512]{0,1:T(8,128)(2,1)}, u32[]{:S(2)}, u32[]{:S(2)}) collective-permute-start(bf16[2048,512]{0,1:T(8,128)(2,1)} %get-tuple-element.497), channel_id=1, source_target_pairs={{0,8},{8,0},{16,24},{24,16},{1,9},{9,1},{17,25},{25,17},{2,10},{10... | collective-permute-start | bytes 6291464 | tf_op jit(solution)/shard_map/ppermute | solution.py:61
  888.5 43.5 %collective-permute-start.37 = (bf16[2048,512]{0,1:T(8,128)(2,1)}, bf16[2048,512]{0,1:T(8,128)(2,1)}, u32[]{:S(2)}, u32[]{:S(2)}) collective-permute-start(bf16[2048,512]{0,1:T(8,128)(2,1)} %get-tuple-element.496), channel_id=1, source_target_pairs={{0,16},{8,24},{16,0},{24,8},{1,17},{9,25},{17,1},{25,9},{2,18},{10... | collective-permute-start | bytes 6291464 | tf_op jit(solution)/shard_map/ppermute | solution.py:61
  932.1 152.4 %reduce-scatter.17.cloned.1.call-start = ((), (), s32[]{:S(2)}) async-start(), calls=%async_computation.17 | async-start | bytes 2359296 | tf_op jit(solution)/shard_map/reduce_scatter | solution.py:368
  947.2 61.4 %collective-permute-start.38 = (bf16[4,384,2048]{2,1,0:T(8,128)(2,1)}, bf16[4,384,2048]{2,1,0:T(8,128)(2,1)}, u32[]{:S(2)}, u32[]{:S(2)}) collective-permute-start(bf16[4,384,2048]{2,1,0:T(8,128)(2,1)} %pad_maximum_fusion.4), channel_id=1, source_target_pairs={{0,1},{1,0},{2,3},{3,2},{4,5},{5,4},{6,7},{7,6},{8,9},{9,8},{10,11... | collective-permute-start | bytes 18874376 | tf_op jit(solution)/shard_map/ppermute | solution.py:187
  953.8 49.2 %collective-permute-start.45 = (bf16[2048,512]{0,1:T(8,128)(2,1)}, bf16[2048,512]{0,1:T(8,128)(2,1)S(1)}, u32[]{:S(2)}, u32[]{:S(2)}) collective-permute-start(bf16[2048,512]{0,1:T(8,128)(2,1)} %copy.252), channel_id=1, source_target_pairs={{0,24},{8,16},{16,8},{24,0},{1,25},{9,17},{17,9},{25,1},{2,26},{10... | collective-permute-start | bytes 6291464 | tf_op jit(solution)/shard_map/ppermute | solution.py:61
  1008.3 147.9 %reduce-scatter.13.cloned.1.call-start = ((), (), s32[]{:S(2)}) async-start(), calls=%async_computation.15 | async-start | bytes 7864320 | tf_op jit(solution)/shard_map/reduce_scatter | solution.py:195
  1026.5 26.1 %collective-permute-start.39 = (bf16[256,2048]{1,0:T(8,128)(2,1)S(1)}, bf16[256,2048]{1,0:T(8,128)(2,1)S(1)}, u32[]{:S(2)}, u32[]{:S(2)}) collective-permute-start(bf16[256,2048]{1,0:T(8,128)(2,1)S(1)} %get-tuple-element.525), channel_id=1, source_target_pairs={{0,8},{8,0},{16,24},{24,16},{1,9},{9,1},{17,25},{25,17},{2,10},{10... | collective-permute-start | bytes 3145736 | tf_op jit(solution)/shard_map/ppermute | solution.py:61
  1026.6 47.3 %collective-permute-start.40 = (bf16[256,2048]{1,0:T(8,128)(2,1)S(1)}, bf16[256,2048]{1,0:T(8,128)(2,1)S(1)}, u32[]{:S(2)}, u32[]{:S(2)}) collective-permute-start(bf16[256,2048]{1,0:T(8,128)(2,1)S(1)} %get-tuple-element.527), channel_id=1, source_target_pairs={{0,16},{8,24},{16,0},{24,8},{1,17},{9,25},{17,1},{25,9},{2,18},{10... | collective-permute-start | bytes 3145736 | tf_op jit(solution)/shard_map/ppermute | solution.py:61
  1028.4 45.6 %collective-permute-start.41 = (bf16[256,2048]{1,0:T(8,128)(2,1)S(1)}, bf16[256,2048]{1,0:T(8,128)(2,1)S(1)}, u32[]{:S(2)}, u32[]{:S(2)}) collective-permute-start(bf16[256,2048]{1,0:T(8,128)(2,1)S(1)} %get-tuple-element.526), channel_id=1, source_target_pairs={{0,24},{8,16},{16,8},{24,0},{1,25},{9,17},{17,9},{25,1},{2,26},{10... | collective-permute-start | bytes 3145736 | tf_op jit(solution)/shard_map/ppermute | solution.py:61
  1084.5 7.9 collective-permute-start.46
  1088.5 12.7 %collective-permute-start.47 = (bf16[256,512]{0,1:T(8,128)(2,1)}, bf16[256,512]{0,1:T(8,128)(2,1)S(1)}, u32[]{:S(2)}, u32[]{:S(2)}) collective-permute-start(bf16[256,512]{0,1:T(8,128)(2,1)} %reduce-scatter.17.cloned.1.call-done), channel_id=1, source_target_pairs={{0,16},{8,24},{16,0},{24,8},{1,17},{9,25},{17,1},{25,9},{2,18},{10... | collective-permute-start | bytes 786440 | tf_op jit(solution)/shard_map/ppermute | solution.py:61
  1088.7 12.5 %collective-permute-start.48 = (bf16[256,512]{0,1:T(8,128)(2,1)}, bf16[256,512]{0,1:T(8,128)(2,1)S(1)}, u32[]{:S(2)}, u32[]{:S(2)}) collective-permute-start(bf16[256,512]{0,1:T(8,128)(2,1)} %reduce-scatter.17.cloned.1.call-done), channel_id=1, source_target_pairs={{0,24},{8,16},{16,8},{24,0},{1,25},{9,17},{17,9},{25,1},{2,26},{10... | collective-permute-start | bytes 786440 | tf_op jit(solution)/shard_map/ppermute | solution.py:61
  1092.4 25.2 %collective-permute-start.42 = (bf16[256,1664]{0,1:T(8,128)(2,1)}, bf16[256,1664]{0,1:T(8,128)(2,1)S(1)}, u32[]{:S(2)}, u32[]{:S(2)}) collective-permute-start(bf16[256,1664]{0,1:T(8,128)(2,1)} %reduce-scatter.11.cloned.1.call-done), channel_id=1, source_target_pairs={{0,8},{8,0},{16,24},{24,16},{1,9},{9,1},{17,25},{25,17},{2,10},{10... | collective-permute-start | bytes 2555912 | tf_op jit(solution)/shard_map/ppermute | solution.py:61
  1101.4 35.7 %collective-permute-start.43 = (bf16[256,1664]{0,1:T(8,128)(2,1)}, bf16[256,1664]{0,1:T(8,128)(2,1)S(1)}, u32[]{:S(2)}, u32[]{:S(2)}) collective-permute-start(bf16[256,1664]{0,1:T(8,128)(2,1)} %reduce-scatter.11.cloned.1.call-done), channel_id=1, source_target_pairs={{0,16},{8,24},{16,0},{24,8},{1,17},{9,25},{17,1},{25,9},{2,18},{10... | collective-permute-start | bytes 2555912 | tf_op jit(solution)/shard_map/ppermute | solution.py:61
  1101.9 35.2 %collective-permute-start.44 = (bf16[256,1664]{0,1:T(8,128)(2,1)}, bf16[256,1664]{0,1:T(8,128)(2,1)S(1)}, u32[]{:S(2)}, u32[]{:S(2)}) collective-permute-start(bf16[256,1664]{0,1:T(8,128)(2,1)} %reduce-scatter.11.cloned.1.call-done), channel_id=1, source_target_pairs={{0,24},{8,16},{16,8},{24,0},{1,25},{9,17},{17,9},{25,1},{2,26},{10... | collective-permute-start | bytes 2555912 | tf_op jit(solution)/shard_map/ppermute | solution.py:61
  (158 other events, 2041.0 us)
Sparse Core Ops, SparseCore 0:
  21.0 72.1 all-gather.6
  95.4 28.7 all-gather.8
  125.9 115.6 all-gather.10
  243.1 114.8 all-gather.12
  359.5 114.8 all-gather.14
  475.9 114.8 all-gather.16
  593.2 108.9 reduce-scatter.6
  704.4 111.2 reduce-scatter.8
  818.1 111.2 reduce-scatter.14
  932.2 75.0 reduce-scatter.10
  1009.6 34.4 reduce-scatter.16
  1046.9 109.2 reduce-scatter.12

commit v5 on v4

--- a/solution.py
+++ b/solution.py
@@ -235,16 +235,19 @@
         for index in range(local_count)
     ]
 
-    own_qkv = lax.dynamic_index_in_dim(
-        qkv_weight.reshape(-1, 3, seq_count, own_width), seq_rank, 2, False
-    ).reshape(-1, 3 * own_width)
+    own_qkv = [
+        lax.dynamic_slice_in_dim(
+            qkv_weight, kind * model_width + seq_rank * own_width, own_width, 1
+        )
+        for kind in range(3)
+    ]
     own_small = jnp.concatenate(
         [jnp.stack([attn_gain, q_gain, k_gain, moe_gain], axis=1), router_weight], axis=1
     )
     small_count = 4 + experts_count
-    small_width = round_up(small_count, 128)
+    small_width = round_up(small_count, 32)
     own_small = jnp.pad(own_small, ((0, 0), (0, small_width - small_count)))
-    front = jnp.concatenate([own_qkv, own_small], axis=1)
+    front = jnp.concatenate(own_qkv + [own_small], axis=1)
     front_full = lax.all_gather(front, "fsdp", axis=0, tiled=True)
     token_blocks = gather_blocks(own_tokens)
     out_cut = lax.dynamic_slice_in_dim(out_weight, seq_rank * own_width, own_width, 1)
@@ -498,9 +501,9 @@
     down_sums = jnp.zeros((local_count,) + down_weight.shape[1:], f32)
     for index in range(local_count):
         if index + 1 == local_count:
-            last_sum, up_sums, down_sums, block_out, grad_tokens, qkv_sum, out_sum = (
+            last_sum, up_sums, down_sums, block_out, grad_tokens, small_sum, out_sum = (
                 lax.optimization_barrier(
-                    (last_sum, up_sums, down_sums, block_out, grad_tokens, qkv_sum, out_sum)
+                    (last_sum, up_sums, down_sums, block_out, grad_tokens, small_sum, out_sum)
                 )
             )
         rows = (sums[index] if index + 1 < local_count else last_sum).astype(f32)

time: 1180 us -> 1170 us (level)
  waiting for transfers between devices: 417 us -> 405 us
    unnamed x297 -> x303, local copies, waits for them, and re-layouts: 43.4 us -> 46 us
  transfers between devices with their start and end apart: 61 -> 61, of which waited for: 29 -> 29; matrix products, arithmetic and copies ran while one was open for 53% -> 54% of each run, Pallas kernels for 0% -> 0%
where the time goes in v5:
time: 1170 us; the launch traced here: 1160 us
  waiting for transfers between devices  405 us (35%)
  matrix products  308 us (26%)
  local copies, waits for them, and re-layouts  218 us (19%)
  other arithmetic  146 us (12%)
  starting transfers between devices  55.5 us (5%)
  between operations  17.5 us (1%)
    ppermute x45, waiting for transfers between devices, from_peer(): lax.ppermute(values, 'seq', [(rank, rank ^ step) for rank in range(count)])  338 us
    dot_general x40, matrix products, mixed_dot(): return jnp.einsum(form, left, right, preferred_element_type=jnp.float32)  256 us
    all_gather x1, waiting for transfers between devices, local(): front_full = lax.all_gather(front, 'fsdp', axis=0, tiled=True)  62.2 us
    ppermute x45, starting transfers between devices, from_peer(): lax.ppermute(values, 'seq', [(rank, rank ^ step) for rank in range(count)])  54.1 us
    unnamed x303, local copies, waits for them, and re-layouts  46 us
    convert_element_type x4, other arithmetic, chip_sums(): return total.astype(gate_up.dtype).reshape(-1, width)  43 us
    slice x4, local copies, waits for them, and re-layouts, split_rows(): stacked[:, :up_rows].reshape(-1, width)  33.5 us
    squeeze x8, local copies, waits for them, and re-layouts, side(): lax.dynamic_index_in_dim(part, number, 1, False)  33.2 us
  transfers between devices with their start and end apart: 61, of which 29 were waited for; matrix products, arithmetic and copies ran while one was open for 54% of the time, Pallas kernels for 0%

profile of v5, /device:TPU:0, one launch (start us, length us, event | category | flops | bytes accessed | tf_op | source)
XLA Modules:
  0.0 1159.7 jit_solution(9686681597876228221)
XLA Ops:
  22.4 62.2 %all-gather.7.cloned.1.call-done = bf16[2048,1568]{0,1:T(8,128)(2,1)} async-done(((bf16[256,1568]{0,1:T(8,128)(2,1)}), bf16[2048,1568]{0,1:T(8,128)(2,1)}) %all-gather.7.cloned.1.call-update) | async-done | bytes 6422544 | tf_op jit(solution)/shard_map/all_gather | solution.py:251
  94.8 16.0 %collective-permute-done = bf16[256,2048]{1,0:T(8,128)(2,1)S(1)} collective-permute-done((bf16[256,2048]{1,0:T(8,128)(2,1)S(1)}, bf16[256,2048]{1,0:T(8,128)(2,1)S(1)}, u32[]{:S(2)}, u32[]{:S(2)}) %collective-permute-start) | collective-permute-done | bytes 1048608 | tf_op jit(solution)/shard_map/ppermute | solution.py:61
  110.8 22.9 %collective-permute-done.1 = bf16[256,2048]{1,0:T(8,128)(2,1)S(1)} collective-permute-done((bf16[256,2048]{1,0:T(8,128)(2,1)S(1)}, bf16[256,2048]{1,0:T(8,128)(2,1)S(1)}, u32[]{:S(2)}, u32[]{:S(2)}) %collective-permute-start.1) | collective-permute-done | bytes 1048608 | tf_op jit(solution)/shard_map/ppermute | solution.py:61
  138.2 6.7 fusion.54
  165.7 24.9 %while.28 = (s32[]{:T(128)}, bf16[2,512,4,128]{3,2,1,0:T(4,128)(2,1)}, f32[2,512,4]{1,2,0:T(4,128)S(1)}, s32[2]{0:T(128)S(1)}, s32[1024]{0:T(1024)S(1)}, /*index...) while((s32[]{:T(128)}, ...), condition=%wide.region_9.10_spmd.clone, body=%wide.region_6.9_spmd.clone.sunk | while | flops 1100218368 | bytes 31552204 | solution.py:304
  199.6 18.6 %collective-permute-done.9 = bf16[256,512]{1,0:T(8,128)(2,1)} collective-permute-done((bf16[256,512]{1,0:T(8,128)(2,1)}, bf16[256,512]{1,0:T(8,128)(2,1)}, u32[]{:S(2)}, u32[]{:S(2)}) %collective-permute-start.9) | collective-permute-done | bytes 262176 | tf_op jit(solution)/shard_map/ppermute | solution.py:61
  225.7 41.1 %collective-permute-done.10 = bf16[256,512]{1,0:T(8,128)(2,1)} collective-permute-done((bf16[256,512]{1,0:T(8,128)(2,1)}, bf16[256,512]{1,0:T(8,128)(2,1)}, u32[]{:S(2)}, u32[]{:S(2)}) %collective-permute-start.10) | collective-permute-done | bytes 262176 | tf_op jit(solution)/shard_map/ppermute | solution.py:61
  279.2 6.2 multiply_reduce_fusion.8
  295.5 21.1 %collective-permute-done.3 = bf16[257,2048]{1,0:T(8,128)(2,1)} collective-permute-done((bf16[257,2048]{1,0:T(8,128)(2,1)}, bf16[257,2048]{1,0:T(8,128)(2,1)}, u32[]{:S(2)}, u32[]{:S(2)}) %collective-permute-start.3) | collective-permute-done | bytes 1052704 | tf_op jit(solution)/shard_map/ppermute | solution.py:61
  316.5 18.4 %collective-permute-done.4 = bf16[257,2048]{1,0:T(8,128)(2,1)} collective-permute-done((bf16[257,2048]{1,0:T(8,128)(2,1)}, bf16[257,2048]{1,0:T(8,128)(2,1)}, u32[]{:S(2)}, u32[]{:S(2)}) %collective-permute-start.4) | collective-permute-done | bytes 1052704 | tf_op jit(solution)/shard_map/ppermute | solution.py:61
  344.8 20.8 %collective-permute-done.15 = bf16[256,2048]{1,0:T(8,128)(2,1)S(1)} collective-permute-done((bf16[256,2048]{1,0:T(8,128)(2,1)}, bf16[256,2048]{1,0:T(8,128)(2,1)S(1)}, u32[]{:S(2)}, u32[]{:S(2)}) %collective-permute-start.15) | collective-permute-done | bytes 1048608 | tf_op jit(solution)/shard_map/ppermute | solution.py:61
  365.6 15.7 %collective-permute-done.16 = bf16[256,2048]{1,0:T(8,128)(2,1)S(1)} collective-permute-done((bf16[256,2048]{1,0:T(8,128)(2,1)}, bf16[256,2048]{1,0:T(8,128)(2,1)S(1)}, u32[]{:S(2)}, u32[]{:S(2)}) %collective-permute-start.16) | collective-permute-done | bytes 1048608 | tf_op jit(solution)/shard_map/ppermute | solution.py:61
  392.3 6.8 multiply_convert_fusion.3
  399.2 8.5 slice.480
  414.0 5.1 fusion.167
  419.2 4.6 multiply_convert_fusion.16
  430.0 9.3 convolution_convert_fusion.5
  439.4 6.9 dynamic-slice_bitcast_fusion.8
  458.7 8.3 slice.485
  467.1 4.8 slice.484
  471.8 11.9 %add_convert_fusion.3 = bf16[4,384,2048]{2,1,0:T(8,128)(2,1)} fusion(bf16[4,384,2048]{2,1,0:T(8,128)(2,1)} %collective-permute-done.18, bf16[4,128,2048]{2,1,0:T(8,128)(2,1)S(1)} %get-tuple-element.545, bf16[4,256,2048]{2,1,0:T(8,128)(2,1)} %get-tuple-element.507), kind=kLoop, calls=%fused_computation.59 | loop fusion | flops 22020096 | bytes 18874368 | tf_op jit(solution)/shard_map/convert_element_type | solution.py:189
  483.8 8.7 fusion.168
  501.7 9.2 convolution_convert_fusion.4
  510.8 6.8 dynamic-slice_bitcast_fusion.6
  542.0 8.4 slice.490
  550.3 4.7 slice.489
  555.0 10.3 add_convert_fusion.2
  565.4 8.4 fusion.169
  583.0 9.5 convolution_convert_fusion.3
  592.4 6.7 dynamic-slice_bitcast_fusion.4
  602.6 8.1 fusion.59
  610.7 9.2 convolution_convert_fusion.13
  620.0 8.3 slice.495
  628.3 5.1 slice.494
  638.5 9.6 convolution_convert_fusion.12
  652.4 9.4 convolution_convert_fusion.11
  661.8 10.3 add_convert_fusion.1
  672.1 8.3 fusion.170
  680.4 5.0 multiply_convert_fusion.7
  690.5 9.7 convolution_convert_fusion.10
  700.3 5.4 fusion.70
  711.0 6.9 fusion.67
  717.9 10.9 convolution_convert_fusion.2
  728.8 5.6 convolution_convert_fusion.6
  737.6 19.6 %collective-permute-done.22 = f32[4,256]{1,0:T(4,128)S(1)} collective-permute-done((f32[4,256]{1,0:T(4,128)S(1)}, f32[4,256]{1,0:T(4,128)S(1)}, u32[]{:S(2)}, u32[]{:S(2)}) %collective-permute-start.22) | collective-permute-done | bytes 4128 | tf_op jit(solution)/shard_map/ppermute | solution.py:61
  764.3 5.7 fusion.74
  783.2 4.8 collective-permute-done.28
  797.7 51.4 %while.29 = (s32[]{:T(128)}, f32[1024,4,128]{0,2,1:T(8,128)S(1)}, f32[1024,4,128]{0,2,1:T(8,128)}, bf16[2,512,4,128]{3,1,2,0:T(8,128)(2,1)}, s32[2]{0:T(128)S(1)...) while((s32[]{:T(128)}, f32[1024,4,128]{0,2,1:T(8,128)S(1)}, ...), condition=%wide.region_26.27_spmd.clone, body=%wide.region_24.26_spmd.clone.sunk | while | flops 2719744000 | bytes 181490704 | solution.py:420
  844.1 5.0 bitcast_add_fusion.5
  884.5 12.1 %fusion.156 = (bf16[1024,2048]{1,0:T(8,128)(2,1)}, bf16[2048]{0:T(1024)(128)(2,1)S(1)}) fusion(f32[1024]{0:T(1024)S(1)} %bitcast.686, bf16[4,256,2048]{2,1,0:T(8,128)(2,1)S(1)} %copy-done.20, bf16[2048,1568]{0,1:T(8,128)(2,1)} %all-gather.7.cloned.1.call-done, bf16[1024,512]{1,0:T(8,128)(2,1)S(1)} %copy-done.67, ...), kind=kOutput, calls=%fused_computation.437 | convolution fusion | flops 6462371840 | bytes 17833984 | tf_op jit(solution)/shard_map/te,de->td/dot_general | solution.py:134
  897.1 10.8 convolution_convert_fusion.1
  907.9 6.7 pad_maximum_fusion
  914.6 8.1 collective-permute-done.36
  928.0 7.4 dynamic-slice_bitcast_fusion.2
  947.2 47.5 %collective-permute-done.45 = bf16[2048,512]{0,1:T(8,128)(2,1)S(1)} collective-permute-done((bf16[2048,512]{0,1:T(8,128)(2,1)}, bf16[2048,512]{0,1:T(8,128)(2,1)S(1)}, u32[]{:S(2)}, u32[]{:S(2)}) %collective-permute-start.45) | collective-permute-done | bytes 2097184 | tf_op jit(solution)/shard_map/ppermute | solution.py:61
  994.8 5.5 add_convert_fusion.4
  1001.8 10.4 add_convert_fusion
  1030.9 13.8 %collective-permute-done.39 = bf16[256,2048]{1,0:T(8,128)(2,1)S(1)} collective-permute-done((bf16[256,2048]{1,0:T(8,128)(2,1)S(1)}, bf16[256,2048]{1,0:T(8,128)(2,1)S(1)}, u32[]{:S(2)}, u32[]{:S(2)}) %collective-permute-start.39) | collective-permute-done | bytes 1048608 | tf_op jit(solution)/shard_map/ppermute | solution.py:61
  1044.7 21.4 %collective-permute-done.40 = bf16[256,2048]{1,0:T(8,128)(2,1)S(1)} collective-permute-done((bf16[256,2048]{1,0:T(8,128)(2,1)S(1)}, bf16[256,2048]{1,0:T(8,128)(2,1)S(1)}, u32[]{:S(2)}, u32[]{:S(2)}) %collective-permute-start.40) | collective-permute-done | bytes 1048608 | tf_op jit(solution)/shard_map/ppermute | solution.py:61
  1087.3 5.7 collective-permute-done.47
  1096.9 11.6 collective-permute-done.42
  1108.6 19.7 %collective-permute-done.43 = bf16[256,1568]{0,1:T(8,128)(2,1)S(1)} collective-permute-done((bf16[256,1568]{0,1:T(8,128)(2,1)}, bf16[256,1568]{0,1:T(8,128)(2,1)S(1)}, u32[]{:S(2)}, u32[]{:S(2)}) %collective-permute-start.43) | collective-permute-done | bytes 802848 | tf_op jit(solution)/shard_map/ppermute | solution.py:61
  1133.3 6.6 copy.265
  1140.6 4.8 reduce-scatter.13.cloned.1.call-done
  (724 shorter events, 406.6 us)
Async XLA Ops:
  7.2 77.3 %all-gather.7.cloned.1.call-start = ((), (), s32[]{:S(2)}) async-start(), calls=%async_computation.6 | async-start | bytes 7225344 | tf_op jit(solution)/shard_map/all_gather | solution.py:251
  15.5 148.2 %all-gather.9.cloned.1.call-start = ((), (), s32[]{:S(2)}) async-start(), calls=%async_computation.7 | async-start | bytes 2359296 | tf_op jit(solution)/shard_map/all_gather | solution.py:254
  16.4 382.8 %all-gather.11.cloned.1.call-start = ((), (), s32[]{:S(2)}) async-start(), calls=%async_computation.8 | async-start | bytes 14155776 | tf_op jit(solution)/shard_map/all_gather | solution.py:255
  84.6 374.1 %all-gather.13.cloned.1.call-start = ((), (), s32[]{:S(2)}) async-start(), calls=%async_computation.9 | async-start | bytes 14155776 | tf_op jit(solution)/shard_map/all_gather | solution.py:255
  84.7 26.1 %collective-permute-start = (bf16[256,2048]{1,0:T(8,128)(2,1)S(1)}, bf16[256,2048]{1,0:T(8,128)(2,1)S(1)}, u32[]{:S(2)}, u32[]{:S(2)}) collective-permute-start(bf16[256,2048]{1,0:T(8,128)(2,1)S(1)} %bitcast.576), channel_id=1, source_target_pairs={{0,8},{8,0},{16,24},{24,16},{1,9},{9,1},{17,25},{25,17},{2,10},{10... | collective-permute-start | bytes 3145736 | tf_op jit(solution)/shard_map/ppermute | solution.py:61
  86.2 47.5 %collective-permute-start.1 = (bf16[256,2048]{1,0:T(8,128)(2,1)S(1)}, bf16[256,2048]{1,0:T(8,128)(2,1)S(1)}, u32[]{:S(2)}, u32[]{:S(2)}) collective-permute-start(bf16[256,2048]{1,0:T(8,128)(2,1)S(1)} %bitcast.577), channel_id=1, source_target_pairs={{0,16},{8,24},{16,0},{24,8},{1,17},{9,25},{17,1},{25,9},{2,18},{10... | collective-permute-start | bytes 3145736 | tf_op jit(solution)/shard_map/ppermute | solution.py:61
  87.7 46.0 %collective-permute-start.2 = (bf16[256,2048]{1,0:T(8,128)(2,1)S(1)}, bf16[256,2048]{1,0:T(8,128)(2,1)S(1)}, u32[]{:S(2)}, u32[]{:S(2)}) collective-permute-start(bf16[256,2048]{1,0:T(8,128)(2,1)S(1)} %bitcast.578), channel_id=1, source_target_pairs={{0,24},{8,16},{16,8},{24,0},{1,25},{9,17},{17,9},{25,1},{2,26},{10... | collective-permute-start | bytes 3145736 | tf_op jit(solution)/shard_map/ppermute | solution.py:61
  135.4 249.7 %copy-start.71 = (bf16[20,2048]{1,0:T(8,128)(2,1)}, bf16[20,2048]{1,0:T(8,128)(2,1)S(1)}, u32[]{:S(2)}) copy-start(bf16[20,2048]{1,0:T(8,128)(2,1)S(1)} %slice_bitcast_fusion.47) | copy-start | bytes 245764
  135.4 209.1 %copy-start.83 = (f32[1,2048]{1,0:T(1,128)}, f32[1,2048]{1,0:T(1,128)S(1)}, u32[]{:S(2)}) copy-start(f32[1,2048]{1,0:T(1,128)S(1)} %get-tuple-element.586) | copy-start | bytes 24580
  148.0 3.7 collective-permute-start.6
  149.3 3.7 collective-permute-start.7
  150.1 4.5 collective-permute-start.8
  161.2 380.8 %all-gather.15.cloned.1.call-start = ((), (), s32[]{:S(2)}) async-start(), calls=%async_computation.10 | async-start | bytes 14155776 | tf_op jit(solution)/shard_map/all_gather | solution.py:255
  163.7 105.4 %collective-permute-start.12 = (bf16[2048,512]{0,1:T(8,128)(2,1)}, bf16[2048,512]{0,1:T(8,128)(2,1)}, u32[]{:S(2)}, u32[]{:S(2)}) collective-permute-start(bf16[2048,512]{0,1:T(8,128)(2,1)} %all-gather.9.cloned.1.call-done), channel_id=1, source_target_pairs={{0,8},{8,0},{16,24},{24,16},{1,9},{9,1},{17,25},{25,17},{2,10},{10... | collective-permute-start | bytes 6291464 | tf_op jit(solution)/shard_map/ppermute | solution.py:61
  165.2 107.4 %collective-permute-start.13 = (bf16[2048,512]{0,1:T(8,128)(2,1)}, bf16[2048,512]{0,1:T(8,128)(2,1)}, u32[]{:S(2)}, u32[]{:S(2)}) collective-permute-start(bf16[2048,512]{0,1:T(8,128)(2,1)} %all-gather.9.cloned.1.call-done), channel_id=1, source_target_pairs={{0,16},{8,24},{16,0},{24,8},{1,17},{9,25},{17,1},{25,9},{2,18},{10... | collective-permute-start | bytes 6291464 | tf_op jit(solution)/shard_map/ppermute | solution.py:61
  196.0 22.2 %collective-permute-start.9 = (bf16[256,512]{1,0:T(8,128)(2,1)}, bf16[256,512]{1,0:T(8,128)(2,1)}, u32[]{:S(2)}, u32[]{:S(2)}) collective-permute-start(bf16[256,512]{1,0:T(8,128)(2,1)} %get-tuple-element.580), channel_id=1, source_target_pairs={{0,8},{8,0},{16,24},{24,16},{1,9},{9,1},{17,25},{25,17},{2,10},{10... | collective-permute-start | bytes 786440 | tf_op jit(solution)/shard_map/ppermute | solution.py:61
  197.3 78.5 %collective-permute-start.14 = (bf16[2048,512]{0,1:T(8,128)(2,1)}, bf16[2048,512]{0,1:T(8,128)(2,1)}, u32[]{:S(2)}, u32[]{:S(2)}) collective-permute-start(bf16[2048,512]{0,1:T(8,128)(2,1)} %all-gather.9.cloned.1.call-done), channel_id=1, source_target_pairs={{0,24},{8,16},{16,8},{24,0},{1,25},{9,17},{17,9},{25,1},{2,26},{10... | collective-permute-start | bytes 6291464 | tf_op jit(solution)/shard_map/ppermute | solution.py:61
  199.1 67.7 %collective-permute-start.10 = (bf16[256,512]{1,0:T(8,128)(2,1)}, bf16[256,512]{1,0:T(8,128)(2,1)}, u32[]{:S(2)}, u32[]{:S(2)}) collective-permute-start(bf16[256,512]{1,0:T(8,128)(2,1)} %get-tuple-element.579), channel_id=1, source_target_pairs={{0,16},{8,24},{16,0},{24,8},{1,17},{9,25},{17,1},{25,9},{2,18},{10... | collective-permute-start | bytes 786440 | tf_op jit(solution)/shard_map/ppermute | solution.py:61
  218.2 49.7 %collective-permute-start.11 = (bf16[256,512]{1,0:T(8,128)(2,1)}, bf16[256,512]{1,0:T(8,128)(2,1)}, u32[]{:S(2)}, u32[]{:S(2)}) collective-permute-start(bf16[256,512]{1,0:T(8,128)(2,1)} %get-tuple-element.578), channel_id=1, source_target_pairs={{0,24},{8,16},{16,8},{24,0},{1,25},{9,17},{17,9},{25,1},{2,26},{10... | collective-permute-start | bytes 786440 | tf_op jit(solution)/shard_map/ppermute | solution.py:61
  286.8 333.1 %all-gather.17.cloned.1.call-start = ((), (), s32[]{:S(2)}) async-start(), calls=%async_computation.11 | async-start | bytes 14155776 | tf_op jit(solution)/shard_map/all_gather | solution.py:255
  289.5 27.1 %collective-permute-start.3 = (bf16[257,2048]{1,0:T(8,128)(2,1)}, bf16[257,2048]{1,0:T(8,128)(2,1)}, u32[]{:S(2)}, u32[]{:S(2)}) collective-permute-start(bf16[257,2048]{1,0:T(8,128)(2,1)} %pad_maximum_fusion.30), channel_id=1, source_target_pairs={{0,8},{8,0},{16,24},{24,16},{1,9},{9,1},{17,25},{25,17},{2,10},{10... | collective-permute-start | bytes 3158024 | tf_op jit(solution)/shard_map/ppermute | solution.py:61
  290.1 44.9 %collective-permute-start.4 = (bf16[257,2048]{1,0:T(8,128)(2,1)}, bf16[257,2048]{1,0:T(8,128)(2,1)}, u32[]{:S(2)}, u32[]{:S(2)}) collective-permute-start(bf16[257,2048]{1,0:T(8,128)(2,1)} %pad_maximum_fusion.30), channel_id=1, source_target_pairs={{0,16},{8,24},{16,0},{24,8},{1,17},{9,25},{17,1},{25,9},{2,18},{10... | collective-permute-start | bytes 3158024 | tf_op jit(solution)/shard_map/ppermute | solution.py:61
  291.5 43.5 %collective-permute-start.5 = (bf16[257,2048]{1,0:T(8,128)(2,1)}, bf16[257,2048]{1,0:T(8,128)(2,1)}, u32[]{:S(2)}, u32[]{:S(2)}) collective-permute-start(bf16[257,2048]{1,0:T(8,128)(2,1)} %pad_maximum_fusion.30), channel_id=1, source_target_pairs={{0,24},{8,16},{16,8},{24,0},{1,25},{9,17},{17,9},{25,1},{2,26},{10... | collective-permute-start | bytes 3158024 | tf_op jit(solution)/shard_map/ppermute | solution.py:61
  339.2 26.3 %collective-permute-start.15 = (bf16[256,2048]{1,0:T(8,128)(2,1)}, bf16[256,2048]{1,0:T(8,128)(2,1)S(1)}, u32[]{:S(2)}, u32[]{:S(2)}) collective-permute-start(bf16[256,2048]{1,0:T(8,128)(2,1)} %multiply_convert_fusion.20), channel_id=1, source_target_pairs={{0,8},{8,0},{16,24},{24,16},{1,9},{9,1},{17,25},{25,17},{2,10},{10... | collective-permute-start | bytes 3145736 | tf_op jit(solution)/shard_map/ppermute | solution.py:61
  340.8 40.4 %collective-permute-start.16 = (bf16[256,2048]{1,0:T(8,128)(2,1)}, bf16[256,2048]{1,0:T(8,128)(2,1)S(1)}, u32[]{:S(2)}, u32[]{:S(2)}) collective-permute-start(bf16[256,2048]{1,0:T(8,128)(2,1)} %multiply_convert_fusion.20), channel_id=1, source_target_pairs={{0,16},{8,24},{16,0},{24,8},{1,17},{9,25},{17,1},{25,9},{2,18},{10... | collective-permute-start | bytes 3145736 | tf_op jit(solution)/shard_map/ppermute | solution.py:61
  341.1 41.7 %collective-permute-start.17 = (bf16[256,2048]{1,0:T(8,128)(2,1)}, bf16[256,2048]{1,0:T(8,128)(2,1)S(1)}, u32[]{:S(2)}, u32[]{:S(2)}) collective-permute-start(bf16[256,2048]{1,0:T(8,128)(2,1)} %multiply_convert_fusion.20), channel_id=1, source_target_pairs={{0,24},{8,16},{16,8},{24,0},{1,25},{9,17},{17,9},{25,1},{2,26},{10... | collective-permute-start | bytes 3145736 | tf_op jit(solution)/shard_map/ppermute | solution.py:61
  344.5 193.0 %copy-start.35 = (pred[4,4,144,256]{3,2,1,0:T(8,128)(4,1)}, pred[4,4,144,256]{3,2,1,0:T(8,128)(4,1)S(1)}, u32[]{:S(2)}) copy-start(pred[4,4,144,256]{3,2,1,0:T(8,128)(4,1)S(1)} %get-tuple-element.601) | copy-start | bytes 1769476
  399.2 398.4 %reduce-scatter.7.cloned.1.call-start = ((), (), s32[]{:S(2)}) async-start(), calls=%async_computation.12 | async-start | bytes 7864320 | tf_op jit(solution)/shard_map/reduce_scatter | solution.py:195
  449.9 22.0 %collective-permute-start.18 = (bf16[4,384,2048]{2,1,0:T(8,128)(2,1)}, bf16[4,384,2048]{2,1,0:T(8,128)(2,1)}, u32[]{:S(2)}, u32[]{:S(2)}) collective-permute-start(bf16[4,384,2048]{2,1,0:T(8,128)(2,1)} %pad_maximum_fusion.1), channel_id=1, source_target_pairs={{0,1},{1,0},{2,3},{3,2},{4,5},{5,4},{6,7},{7,6},{8,9},{9,8},{10,11... | collective-permute-start | bytes 18874376 | tf_op jit(solution)/shard_map/ppermute | solution.py:187
  521.0 34.0 %collective-permute-start.19 = (bf16[4,384,2048]{2,1,0:T(8,128)(2,1)}, bf16[4,384,2048]{2,1,0:T(8,128)(2,1)}, u32[]{:S(2)}, u32[]{:S(2)}) collective-permute-start(bf16[4,384,2048]{2,1,0:T(8,128)(2,1)} %pad_maximum_fusion.2), channel_id=1, source_target_pairs={{0,1},{1,0},{2,3},{3,2},{4,5},{5,4},{6,7},{7,6},{8,9},{9,8},{10,11... | collective-permute-start | bytes 18874376 | tf_op jit(solution)/shard_map/ppermute | solution.py:187
  532.7 391.2 %reduce-scatter.9.cloned.1.call-start = ((), (), s32[]{:S(2)}) async-start(), calls=%async_computation.13 | async-start | bytes 7864320 | tf_op jit(solution)/shard_map/reduce_scatter | solution.py:195
  602.6 59.2 %collective-permute-start.20 = (bf16[4,384,2048]{2,1,0:T(8,128)(2,1)}, bf16[4,384,2048]{2,1,0:T(8,128)(2,1)}, u32[]{:S(2)}, u32[]{:S(2)}) collective-permute-start(bf16[4,384,2048]{2,1,0:T(8,128)(2,1)} %pad_maximum_fusion.3), channel_id=1, source_target_pairs={{0,1},{1,0},{2,3},{3,2},{4,5},{5,4},{6,7},{7,6},{8,9},{9,8},{10,11... | collective-permute-start | bytes 18874376 | tf_op jit(solution)/shard_map/ppermute | solution.py:187
  652.3 347.9 %reduce-scatter.15.cloned.1.call-start = ((), (), s32[]{:S(2)}) async-start(), calls=%async_computation.16 | async-start | bytes 7864320 | tf_op jit(solution)/shard_map/reduce_scatter | solution.py:195
  690.1 45.9 %collective-permute-start.21 = (f32[4,256]{1,0:T(4,128)S(1)}, f32[4,256]{1,0:T(4,128)S(1)}, u32[]{:S(2)}, u32[]{:S(2)}) collective-permute-start(f32[4,256]{1,0:T(4,128)S(1)} %get-tuple-element.598), channel_id=1, source_target_pairs={{0,8},{8,0},{16,24},{24,16},{1,9},{9,1},{17,25},{25,17},{2,10},{10... | collective-permute-start | bytes 12296 | tf_op jit(solution)/shard_map/ppermute | solution.py:61
  707.5 49.8 %collective-permute-start.24 = (bf16[256,2048]{1,0:T(8,128)(2,1)}, bf16[256,2048]{1,0:T(8,128)(2,1)}, u32[]{:S(2)}, u32[]{:S(2)}) collective-permute-start(bf16[256,2048]{1,0:T(8,128)(2,1)} %get-tuple-element.535), channel_id=1, source_target_pairs={{0,8},{8,0},{16,24},{24,16},{1,9},{9,1},{17,25},{25,17},{2,10},{10... | collective-permute-start | bytes 3145736 | tf_op jit(solution)/shard_map/ppermute | solution.py:61
  709.2 48.1 %collective-permute-start.25 = (bf16[256,2048]{1,0:T(8,128)(2,1)}, bf16[256,2048]{1,0:T(8,128)(2,1)}, u32[]{:S(2)}, u32[]{:S(2)}) collective-permute-start(bf16[256,2048]{1,0:T(8,128)(2,1)} %get-tuple-element.534), channel_id=1, source_target_pairs={{0,16},{8,24},{16,0},{24,8},{1,17},{9,25},{17,1},{25,9},{2,18},{10... | collective-permute-start | bytes 3145736 | tf_op jit(solution)/shard_map/ppermute | solution.py:61
  709.4 47.8 %collective-permute-start.26 = (bf16[256,2048]{1,0:T(8,128)(2,1)}, bf16[256,2048]{1,0:T(8,128)(2,1)}, u32[]{:S(2)}, u32[]{:S(2)}) collective-permute-start(bf16[256,2048]{1,0:T(8,128)(2,1)} %get-tuple-element.533), channel_id=1, source_target_pairs={{0,24},{8,16},{16,8},{24,0},{1,25},{9,17},{17,9},{25,1},{2,26},{10... | collective-permute-start | bytes 3145736 | tf_op jit(solution)/shard_map/ppermute | solution.py:61
  734.4 22.8 %collective-permute-start.22 = (f32[4,256]{1,0:T(4,128)S(1)}, f32[4,256]{1,0:T(4,128)S(1)}, u32[]{:S(2)}, u32[]{:S(2)}) collective-permute-start(f32[4,256]{1,0:T(4,128)S(1)} %get-tuple-element.597), channel_id=1, source_target_pairs={{0,16},{8,24},{16,0},{24,8},{1,17},{9,25},{17,1},{25,9},{2,18},{10... | collective-permute-start | bytes 12296 | tf_op jit(solution)/shard_map/ppermute | solution.py:61
  735.9 21.3 %collective-permute-start.23 = (f32[4,256]{1,0:T(4,128)S(1)}, f32[4,256]{1,0:T(4,128)S(1)}, u32[]{:S(2)}, u32[]{:S(2)}) collective-permute-start(f32[4,256]{1,0:T(4,128)S(1)} %get-tuple-element.596), channel_id=1, source_target_pairs={{0,24},{8,16},{16,8},{24,0},{1,25},{9,17},{17,9},{25,1},{2,26},{10... | collective-permute-start | bytes 12296 | tf_op jit(solution)/shard_map/ppermute | solution.py:61
  773.9 9.3 collective-permute-start.27
  774.3 13.7 %collective-permute-start.28 = (bf16[256,512]{1,0:T(8,128)(2,1)S(1)}, bf16[256,512]{1,0:T(8,128)(2,1)}, u32[]{:S(2)}, u32[]{:S(2)}) collective-permute-start(bf16[256,512]{1,0:T(8,128)(2,1)S(1)} %bitcast.645), channel_id=1, source_target_pairs={{0,16},{8,24},{16,0},{24,8},{1,17},{9,25},{17,1},{25,9},{2,18},{10... | collective-permute-start | bytes 786440 | tf_op jit(solution)/shard_map/ppermute | solution.py:61
  776.0 12.0 %collective-permute-start.29 = (bf16[256,512]{1,0:T(8,128)(2,1)S(1)}, bf16[256,512]{1,0:T(8,128)(2,1)}, u32[]{:S(2)}, u32[]{:S(2)}) collective-permute-start(bf16[256,512]{1,0:T(8,128)(2,1)S(1)} %bitcast.646), channel_id=1, source_target_pairs={{0,24},{8,16},{16,8},{24,0},{1,25},{9,17},{17,9},{25,1},{2,26},{10... | collective-permute-start | bytes 786440 | tf_op jit(solution)/shard_map/ppermute | solution.py:61
  794.0 59.0 %collective-permute-start.30 = (bf16[256,2048]{1,0:T(8,128)(2,1)}, bf16[256,2048]{1,0:T(8,128)(2,1)}, u32[]{:S(2)}, u32[]{:S(2)}) collective-permute-start(bf16[256,2048]{1,0:T(8,128)(2,1)} %get-tuple-element.532), channel_id=1, source_target_pairs={{0,8},{8,0},{16,24},{24,16},{1,9},{9,1},{17,25},{25,17},{2,10},{10... | collective-permute-start | bytes 3145736 | tf_op jit(solution)/shard_map/ppermute | solution.py:61
  795.6 57.5 %collective-permute-start.31 = (bf16[256,2048]{1,0:T(8,128)(2,1)}, bf16[256,2048]{1,0:T(8,128)(2,1)}, u32[]{:S(2)}, u32[]{:S(2)}) collective-permute-start(bf16[256,2048]{1,0:T(8,128)(2,1)} %get-tuple-element.531), channel_id=1, source_target_pairs={{0,16},{8,24},{16,0},{24,8},{1,17},{9,25},{17,1},{25,9},{2,18},{10... | collective-permute-start | bytes 3145736 | tf_op jit(solution)/shard_map/ppermute | solution.py:61
  796.2 56.9 %collective-permute-start.32 = (bf16[256,2048]{1,0:T(8,128)(2,1)}, bf16[256,2048]{1,0:T(8,128)(2,1)}, u32[]{:S(2)}, u32[]{:S(2)}) collective-permute-start(bf16[256,2048]{1,0:T(8,128)(2,1)} %get-tuple-element.530), channel_id=1, source_target_pairs={{0,24},{8,16},{16,8},{24,0},{1,25},{9,17},{17,9},{25,1},{2,26},{10... | collective-permute-start | bytes 3145736 | tf_op jit(solution)/shard_map/ppermute | solution.py:61
  797.6 214.7 %reduce-scatter.11.cloned.1.call-start = ((), (), s32[]{:S(2)}) async-start(), calls=%async_computation.14 | async-start | bytes 7225344 | tf_op jit(solution)/shard_map/reduce_scatter | solution.py:371
  863.1 3.7 collective-permute-start.33
  864.6 3.7 collective-permute-start.34
  865.3 4.5 collective-permute-start.35
  878.8 43.8 %collective-permute-start.36 = (bf16[2048,512]{0,1:T(8,128)(2,1)}, bf16[2048,512]{0,1:T(8,128)(2,1)}, u32[]{:S(2)}, u32[]{:S(2)}) collective-permute-start(bf16[2048,512]{0,1:T(8,128)(2,1)} %get-tuple-element.497), channel_id=1, source_target_pairs={{0,8},{8,0},{16,24},{24,16},{1,9},{9,1},{17,25},{25,17},{2,10},{10... | collective-permute-start | bytes 6291464 | tf_op jit(solution)/shard_map/ppermute | solution.py:61
  880.3 43.6 %collective-permute-start.37 = (bf16[2048,512]{0,1:T(8,128)(2,1)}, bf16[2048,512]{0,1:T(8,128)(2,1)}, u32[]{:S(2)}, u32[]{:S(2)}) collective-permute-start(bf16[2048,512]{0,1:T(8,128)(2,1)} %get-tuple-element.496), channel_id=1, source_target_pairs={{0,16},{8,24},{16,0},{24,8},{1,17},{9,25},{17,1},{25,9},{2,18},{10... | collective-permute-start | bytes 6291464 | tf_op jit(solution)/shard_map/ppermute | solution.py:61
  923.9 152.7 %reduce-scatter.17.cloned.1.call-start = ((), (), s32[]{:S(2)}) async-start(), calls=%async_computation.17 | async-start | bytes 2359296 | tf_op jit(solution)/shard_map/reduce_scatter | solution.py:371
  939.0 61.5 %collective-permute-start.38 = (bf16[4,384,2048]{2,1,0:T(8,128)(2,1)}, bf16[4,384,2048]{2,1,0:T(8,128)(2,1)}, u32[]{:S(2)}, u32[]{:S(2)}) collective-permute-start(bf16[4,384,2048]{2,1,0:T(8,128)(2,1)} %pad_maximum_fusion.4), channel_id=1, source_target_pairs={{0,1},{1,0},{2,3},{3,2},{4,5},{5,4},{6,7},{7,6},{8,9},{9,8},{10,11... | collective-permute-start | bytes 18874376 | tf_op jit(solution)/shard_map/ppermute | solution.py:187
  945.6 49.1 %collective-permute-start.45 = (bf16[2048,512]{0,1:T(8,128)(2,1)}, bf16[2048,512]{0,1:T(8,128)(2,1)S(1)}, u32[]{:S(2)}, u32[]{:S(2)}) collective-permute-start(bf16[2048,512]{0,1:T(8,128)(2,1)} %copy.261), channel_id=1, source_target_pairs={{0,24},{8,16},{16,8},{24,0},{1,25},{9,17},{17,9},{25,1},{2,26},{10... | collective-permute-start | bytes 6291464 | tf_op jit(solution)/shard_map/ppermute | solution.py:61
  1000.3 145.1 %reduce-scatter.13.cloned.1.call-start = ((), (), s32[]{:S(2)}) async-start(), calls=%async_computation.15 | async-start | bytes 7864320 | tf_op jit(solution)/shard_map/reduce_scatter | solution.py:195
  1018.6 26.1 %collective-permute-start.39 = (bf16[256,2048]{1,0:T(8,128)(2,1)S(1)}, bf16[256,2048]{1,0:T(8,128)(2,1)S(1)}, u32[]{:S(2)}, u32[]{:S(2)}) collective-permute-start(bf16[256,2048]{1,0:T(8,128)(2,1)S(1)} %get-tuple-element.525), channel_id=1, source_target_pairs={{0,8},{8,0},{16,24},{24,16},{1,9},{9,1},{17,25},{25,17},{2,10},{10... | collective-permute-start | bytes 3145736 | tf_op jit(solution)/shard_map/ppermute | solution.py:61
  1018.9 47.2 %collective-permute-start.40 = (bf16[256,2048]{1,0:T(8,128)(2,1)S(1)}, bf16[256,2048]{1,0:T(8,128)(2,1)S(1)}, u32[]{:S(2)}, u32[]{:S(2)}) collective-permute-start(bf16[256,2048]{1,0:T(8,128)(2,1)S(1)} %get-tuple-element.527), channel_id=1, source_target_pairs={{0,16},{8,24},{16,0},{24,8},{1,17},{9,25},{17,1},{25,9},{2,18},{10... | collective-permute-start | bytes 3145736 | tf_op jit(solution)/shard_map/ppermute | solution.py:61
  1020.9 45.2 %collective-permute-start.41 = (bf16[256,2048]{1,0:T(8,128)(2,1)S(1)}, bf16[256,2048]{1,0:T(8,128)(2,1)S(1)}, u32[]{:S(2)}, u32[]{:S(2)}) collective-permute-start(bf16[256,2048]{1,0:T(8,128)(2,1)S(1)} %get-tuple-element.526), channel_id=1, source_target_pairs={{0,24},{8,16},{16,8},{24,0},{1,25},{9,17},{17,9},{25,1},{2,26},{10... | collective-permute-start | bytes 3145736 | tf_op jit(solution)/shard_map/ppermute | solution.py:61
  1076.6 8.4 collective-permute-start.46
  1080.4 12.6 %collective-permute-start.47 = (bf16[256,512]{0,1:T(8,128)(2,1)}, bf16[256,512]{0,1:T(8,128)(2,1)S(1)}, u32[]{:S(2)}, u32[]{:S(2)}) collective-permute-start(bf16[256,512]{0,1:T(8,128)(2,1)} %reduce-scatter.17.cloned.1.call-done), channel_id=1, source_target_pairs={{0,16},{8,24},{16,0},{24,8},{1,17},{9,25},{17,1},{25,9},{2,18},{10... | collective-permute-start | bytes 786440 | tf_op jit(solution)/shard_map/ppermute | solution.py:61
  1081.0 12.0 %collective-permute-start.48 = (bf16[256,512]{0,1:T(8,128)(2,1)}, bf16[256,512]{0,1:T(8,128)(2,1)S(1)}, u32[]{:S(2)}, u32[]{:S(2)}) collective-permute-start(bf16[256,512]{0,1:T(8,128)(2,1)} %reduce-scatter.17.cloned.1.call-done), channel_id=1, source_target_pairs={{0,24},{8,16},{16,8},{24,0},{1,25},{9,17},{17,9},{25,1},{2,26},{10... | collective-permute-start | bytes 786440 | tf_op jit(solution)/shard_map/ppermute | solution.py:61
  1085.0 23.5 %collective-permute-start.42 = (bf16[256,1568]{0,1:T(8,128)(2,1)}, bf16[256,1568]{0,1:T(8,128)(2,1)S(1)}, u32[]{:S(2)}, u32[]{:S(2)}) collective-permute-start(bf16[256,1568]{0,1:T(8,128)(2,1)} %reduce-scatter.11.cloned.1.call-done), channel_id=1, source_target_pairs={{0,8},{8,0},{16,24},{24,16},{1,9},{9,1},{17,25},{25,17},{2,10},{10... | collective-permute-start | bytes 2408456 | tf_op jit(solution)/shard_map/ppermute | solution.py:61
  1093.3 35.0 %collective-permute-start.43 = (bf16[256,1568]{0,1:T(8,128)(2,1)}, bf16[256,1568]{0,1:T(8,128)(2,1)S(1)}, u32[]{:S(2)}, u32[]{:S(2)}) collective-permute-start(bf16[256,1568]{0,1:T(8,128)(2,1)} %reduce-scatter.11.cloned.1.call-done), channel_id=1, source_target_pairs={{0,16},{8,24},{16,0},{24,8},{1,17},{9,25},{17,1},{25,9},{2,18},{10... | collective-permute-start | bytes 2408456 | tf_op jit(solution)/shard_map/ppermute | solution.py:61
  1093.6 34.7 %collective-permute-start.44 = (bf16[256,1568]{0,1:T(8,128)(2,1)}, bf16[256,1568]{0,1:T(8,128)(2,1)S(1)}, u32[]{:S(2)}, u32[]{:S(2)}) collective-permute-start(bf16[256,1568]{0,1:T(8,128)(2,1)} %reduce-scatter.11.cloned.1.call-done), channel_id=1, source_target_pairs={{0,24},{8,16},{16,8},{24,0},{1,25},{9,17},{17,9},{25,1},{2,26},{10... | collective-permute-start | bytes 2408456 | tf_op jit(solution)/shard_map/ppermute | solution.py:61
  (160 other events, 2056.0 us)
Sparse Core Ops, SparseCore 0:
  15.6 68.9 all-gather.6
  86.7 28.7 all-gather.8
  117.2 115.6 all-gather.10
  234.4 114.8 all-gather.12
  350.8 114.8 all-gather.14
  467.2 114.8 all-gather.16
  584.4 108.9 reduce-scatter.6
  695.7 111.2 reduce-scatter.8
  809.4 111.2 reduce-scatter.14
  924.0 70.8 reduce-scatter.10
  1000.4 33.4 reduce-scatter.16
  1036.1 109.3 reduce-scatter.12

commit v6 on v5

--- a/solution.py
+++ b/solution.py
@@ -173,11 +173,11 @@
     return (stacked[:, :up_rows].reshape(-1, width), stacked[:, up_rows:].reshape(-1, width))
 
 
-def chip_sums(gate_up, down):
+def chip_sums(*grads):
     count = lax.axis_size("fsdp")
     core = lax.axis_index("fsdp") % 2
-    width = gate_up.shape[-1]
-    parts = [grad.reshape(count // 2, 2, -1, width) for grad in (gate_up, down)]
+    width = grads[0].shape[-1]
+    parts = [grad.reshape(count // 2, 2, -1, width) for grad in grads]
 
     def side(number):
         return jnp.concatenate(
@@ -186,7 +186,7 @@
 
     swapped = lax.ppermute(side(1 - core), "fsdp", [(index, index ^ 1) for index in range(count)])
     total = side(core).astype(jnp.float32) + swapped.astype(jnp.float32)
-    return total.astype(gate_up.dtype).reshape(-1, width)
+    return total.astype(grads[0].dtype).reshape(-1, width)
 
 
 def scatter_chips(rows):
@@ -257,11 +257,8 @@
     )
     weights = [gather_expert(0, front_full)]
     id_rows = experts[0].astype(bf16).reshape(-1, model_width)
-    cot_parts = gather_blocks(
-        after(jnp.concatenate([cotangent[0], id_rows], axis=0), token_blocks)
-    )
-    cot_blocks = cot_parts[:, :tok_count]
-    id_blocks = cot_parts[:, tok_count:].reshape(seq_count, tok_count, -1).astype(jnp.int32)
+    cot_rows = after(jnp.concatenate([cotangent[0], id_rows], axis=0), token_blocks)
+    cot_parts = [from_peer(cot_rows, step) for step in range(min(3, seq_count))]
 
     qkv_own = front_full[:, : 3 * own_width]
     small_full = front_full[:, 3 * own_width : 3 * own_width + small_count].T
@@ -306,6 +303,10 @@
     )
     log_sums = sums_blocks.reshape(key_span, own_heads)
     weights.append(gather_expert(1, heads_in))
+    cot_parts += [from_peer(after(cot_rows, heads_in), step) for step in range(3, seq_count)]
+    cot_parts = jnp.stack(cot_parts)
+    cot_blocks = cot_parts[:, :tok_count]
+    id_blocks = cot_parts[:, tok_count:].reshape(seq_count, tok_count, -1).astype(jnp.int32)
     out_cut = after(out_cut, heads_in)
     out_parts = [from_peer(out_cut, step) for step in range(seq_count)]
 
@@ -475,7 +476,7 @@
     grad_front = jnp.concatenate([grad_qkv, grad_small.T.astype(bf16)], axis=1)
     grad_front = after(grad_front, near_cuts)
 
-    front_sum = scatter(after(grad_front, *sums[:-1]))
+    front_sum = scatter_chips(after(chip_sums(grad_front), *sums[:-1]))
     grad_cut = sum(part.astype(f32) for part in near_cuts + far_cuts).astype(bf16)
     out_sum = scatter(after(grad_cut, *sums, grad_front))
     last_grads = chip_sums(*after(last_grads, grad_front))

time: 1170 us -> 1220 us (1.043)
  local copies, waits for them, and re-layouts: 218 us -> 271 us
    dynamic_slice x0 -> x1, local copies, waits for them, and re-layouts: none -> 17.1 us  [side(): lax.dynamic_index_in_dim(part, number, 1, False)]
    reshape x0 -> x1, local copies, waits for them, and re-layouts: none -> 15.3 us  [chip_sums(): parts = [grad.reshape(count // 2, 2, -1, width) for grad in grads]]
    unnamed x303 -> x304, local copies, waits for them, and re-layouts: 46 us -> 49 us
    convert_element_type x4 -> x5, other arithmetic: 43 us -> 45.7 us  [chip_sums(): return total.astype(grads[0].dtype).reshape(-1, width)]
  transfers between devices with their start and end apart: 61 -> 62, of which waited for: 29 -> 28; matrix products, arithmetic and copies ran while one was open for 54% -> 56% of each run, Pallas kernels for 0% -> 0%
where the time goes in v6:
time: 1220 us
  waiting for transfers between devices  408 us (33%)
  matrix products  304 us (25%)
  local copies, waits for them, and re-layouts  271 us (22%)
  other arithmetic  152 us (12%)
  starting transfers between devices  55.4 us (5%)
  between operations  17.5 us (1%)
    ppermute x45, waiting for transfers between devices, from_peer(): lax.ppermute(values, 'seq', [(rank, rank ^ step) for rank in range(count)])  340 us
    dot_general x40, matrix products, mixed_dot(): return jnp.einsum(form, left, right, preferred_element_type=jnp.float32)  252 us
    all_gather x1, waiting for transfers between devices, local(): front_full = lax.all_gather(front, 'fsdp', axis=0, tiled=True)  62.1 us
    ppermute x45, starting transfers between devices, from_peer(): lax.ppermute(values, 'seq', [(rank, rank ^ step) for rank in range(count)])  53.8 us
    unnamed x304, local copies, waits for them, and re-layouts  49 us
    convert_element_type x5, other arithmetic, chip_sums(): return total.astype(grads[0].dtype).reshape(-1, width)  45.7 us
    slice x4, local copies, waits for them, and re-layouts, split_rows(): stacked[:, :up_rows].reshape(-1, width)  33.4 us
    squeeze x8, local copies, waits for them, and re-layouts, side(): lax.dynamic_index_in_dim(part, number, 1, False)  32.9 us
  transfers between devices with their start and end apart: 62, of which 28 were waited for; matrix products, arithmetic and copies ran while one was open for 56% of the time, Pallas kernels for 0%

profile of v6, /device:TPU:0, one launch (start us, length us, event | category | flops | bytes accessed | tf_op | source)
XLA Modules:
  0.0 1216.8 jit_solution(14249873835817809696)
XLA Ops:
  22.5 62.1 %all-gather.7.cloned.1.call-done = bf16[2048,1568]{0,1:T(8,128)(2,1)} async-done(((bf16[256,1568]{0,1:T(8,128)(2,1)}), bf16[2048,1568]{0,1:T(8,128)(2,1)}) %all-gather.7.cloned.1.call-update) | async-done | bytes 6422544 | tf_op jit(solution)/shard_map/all_gather | solution.py:251
  94.8 16.0 %collective-permute-done = bf16[256,2048]{1,0:T(8,128)(2,1)S(1)} collective-permute-done((bf16[256,2048]{1,0:T(8,128)(2,1)S(1)}, bf16[256,2048]{1,0:T(8,128)(2,1)S(1)}, u32[]{:S(2)}, u32[]{:S(2)}) %collective-permute-start) | collective-permute-done | bytes 1048608 | tf_op jit(solution)/shard_map/ppermute | solution.py:61
  110.8 22.9 %collective-permute-done.1 = bf16[256,2048]{1,0:T(8,128)(2,1)S(1)} collective-permute-done((bf16[256,2048]{1,0:T(8,128)(2,1)S(1)}, bf16[256,2048]{1,0:T(8,128)(2,1)S(1)}, u32[]{:S(2)}, u32[]{:S(2)}) %collective-permute-start.1) | collective-permute-done | bytes 1048608 | tf_op jit(solution)/shard_map/ppermute | solution.py:61
  138.2 6.7 fusion.55
  165.7 24.9 %while.28 = (s32[]{:T(128)}, bf16[2,512,4,128]{3,2,1,0:T(4,128)(2,1)}, f32[2,512,4]{1,2,0:T(4,128)S(1)}, s32[2]{0:T(128)S(1)}, s32[1024]{0:T(1024)S(1)}, /*index...) while((s32[]{:T(128)}, ...), condition=%wide.region_9.10_spmd.clone, body=%wide.region_6.9_spmd.clone.sunk | while | flops 1100218368 | bytes 31552204 | solution.py:301
  199.6 18.6 %collective-permute-done.9 = bf16[256,512]{1,0:T(8,128)(2,1)} collective-permute-done((bf16[256,512]{1,0:T(8,128)(2,1)}, bf16[256,512]{1,0:T(8,128)(2,1)}, u32[]{:S(2)}, u32[]{:S(2)}) %collective-permute-start.9) | collective-permute-done | bytes 262176 | tf_op jit(solution)/shard_map/ppermute | solution.py:61
  225.7 41.1 %collective-permute-done.10 = bf16[256,512]{1,0:T(8,128)(2,1)} collective-permute-done((bf16[256,512]{1,0:T(8,128)(2,1)}, bf16[256,512]{1,0:T(8,128)(2,1)}, u32[]{:S(2)}, u32[]{:S(2)}) %collective-permute-start.10) | collective-permute-done | bytes 262176 | tf_op jit(solution)/shard_map/ppermute | solution.py:61
  279.2 6.2 multiply_reduce_fusion.8
  295.5 21.1 %collective-permute-done.3 = bf16[257,2048]{1,0:T(8,128)(2,1)} collective-permute-done((bf16[257,2048]{1,0:T(8,128)(2,1)}, bf16[257,2048]{1,0:T(8,128)(2,1)}, u32[]{:S(2)}, u32[]{:S(2)}) %collective-permute-start.3) | collective-permute-done | bytes 1052704 | tf_op jit(solution)/shard_map/ppermute | solution.py:61
  316.6 18.4 %collective-permute-done.4 = bf16[257,2048]{1,0:T(8,128)(2,1)} collective-permute-done((bf16[257,2048]{1,0:T(8,128)(2,1)}, bf16[257,2048]{1,0:T(8,128)(2,1)}, u32[]{:S(2)}, u32[]{:S(2)}) %collective-permute-start.4) | collective-permute-done | bytes 1052704 | tf_op jit(solution)/shard_map/ppermute | solution.py:61
  344.9 20.7 %collective-permute-done.15 = bf16[256,2048]{1,0:T(8,128)(2,1)S(1)} collective-permute-done((bf16[256,2048]{1,0:T(8,128)(2,1)}, bf16[256,2048]{1,0:T(8,128)(2,1)S(1)}, u32[]{:S(2)}, u32[]{:S(2)}) %collective-permute-start.15) | collective-permute-done | bytes 1048608 | tf_op jit(solution)/shard_map/ppermute | solution.py:61
  365.6 15.6 %collective-permute-done.16 = bf16[256,2048]{1,0:T(8,128)(2,1)S(1)} collective-permute-done((bf16[256,2048]{1,0:T(8,128)(2,1)}, bf16[256,2048]{1,0:T(8,128)(2,1)S(1)}, u32[]{:S(2)}, u32[]{:S(2)}) %collective-permute-start.16) | collective-permute-done | bytes 1048608 | tf_op jit(solution)/shard_map/ppermute | solution.py:61
  392.3 6.8 multiply_convert_fusion.3
  399.2 8.5 slice.480
  414.0 5.1 fusion.166
  430.0 9.4 convolution_convert_fusion.5
  439.4 6.9 dynamic-slice_bitcast_fusion.8
  458.7 8.3 slice.485
  471.7 11.7 add_convert_fusion.3
  483.4 8.7 fusion.167
  501.4 9.2 convolution_convert_fusion.4
  510.5 6.8 dynamic-slice_bitcast_fusion.6
  541.8 8.4 slice.490
  554.9 10.4 add_convert_fusion.2
  565.3 8.4 fusion.168
  582.9 9.6 convolution_convert_fusion.3
  592.4 7.0 dynamic-slice_bitcast_fusion.4
  602.8 8.0 fusion.60
  610.9 9.2 convolution_convert_fusion.13
  620.1 8.3 slice.495
  628.4 5.1 slice.494
  638.7 9.5 convolution_convert_fusion.12
  652.6 9.4 convolution_convert_fusion.11
  662.0 10.2 add_convert_fusion.1
  672.2 8.3 fusion.169
  684.2 6.7 convolution_convert_fusion.10
  690.9 9.2 convolution_convert_fusion.2
  705.3 6.1 fusion.71
  716.6 7.2 fusion.68
  723.9 5.6 convolution_convert_fusion.6
  732.5 30.2 %collective-permute-done.22 = f32[4,256]{1,0:T(4,128)S(1)} collective-permute-done((f32[4,256]{1,0:T(4,128)S(1)}, f32[4,256]{1,0:T(4,128)S(1)}, u32[]{:S(2)}, u32[]{:S(2)}) %collective-permute-start.22) | collective-permute-done | bytes 4128 | tf_op jit(solution)/shard_map/ppermute | solution.py:61
  769.8 5.8 fusion.75
  802.6 50.4 %while.29 = (s32[]{:T(128)}, f32[1024,4,128]{0,2,1:T(8,128)S(1)}, f32[1024,4,128]{0,2,1:T(8,128)}, bf16[2,512,4,128]{3,1,2,0:T(8,128)(2,1)}, s32[2]{0:T(128)S(1)...) while((s32[]{:T(128)}, f32[1024,4,128]{0,2,1:T(8,128)S(1)}, ...), condition=%wide.region_26.27_spmd.clone, body=%wide.region_24.26_spmd.clone.sunk | while | flops 2719744000 | bytes 181490704 | solution.py:421
  848.0 5.0 bitcast_add_fusion.5
  889.8 12.0 fusion.156
  902.4 11.2 convolution_convert_fusion.1
  913.6 6.7 pad_maximum_fusion
  920.2 6.6 collective-permute-done.36
  928.1 15.3 %reshape.584 = bf16[4,2,256,1568]{2,1,0,3:T(2,128)(2,1)} reshape(bf16[2048,1568]{0,1:T(8,128)(2,1)} %pad_maximum_fusion) | data formatting | bytes 12845056 | tf_op jit(solution)/shard_map/reshape | solution.py:180
  943.4 17.1 %constant_dynamic-slice_fusion.3 = (bf16[4,1,256,1568]{2,1,0,3:T(2,128)(2,1)S(1)}, bf16[4,1,256,1568]{2,1,0,3:T(2,128)(2,1)S(1)}) fusion(bf16[4,2,256,1568]{2,1,0,3:T(2,128)(2,1)} %reshape.584, s32[]{:T(128)S(6)} %select_n.179, s32[]{:T(128)S(6)} %select_n.180), kind=kLoop, calls=%fused_computation.376 | loop fusion | bytes 12845064 | tf_op jit(solution)/shard_map/jit(dynamic_index_in_dim)/dynamic_slice | solution.py:184
  961.6 5.7 collective-permute-done.39
  970.4 5.3 copy.407
  979.9 6.9 dynamic-slice_bitcast_fusion.2
  999.1 47.0 %collective-permute-done.46 = bf16[2048,512]{0,1:T(8,128)(2,1)S(1)} collective-permute-done((bf16[2048,512]{0,1:T(8,128)(2,1)}, bf16[2048,512]{0,1:T(8,128)(2,1)S(1)}, u32[]{:S(2)}, u32[]{:S(2)}) %collective-permute-start.46) | collective-permute-done | bytes 2097184 | tf_op jit(solution)/shard_map/ppermute | solution.py:61
  1046.1 5.3 add_convert_fusion.4
  1053.0 10.4 add_convert_fusion
  1082.1 13.8 %collective-permute-done.40 = bf16[256,2048]{1,0:T(8,128)(2,1)S(1)} collective-permute-done((bf16[256,2048]{1,0:T(8,128)(2,1)S(1)}, bf16[256,2048]{1,0:T(8,128)(2,1)S(1)}, u32[]{:S(2)}, u32[]{:S(2)}) %collective-permute-start.40) | collective-permute-done | bytes 1048608 | tf_op jit(solution)/shard_map/ppermute | solution.py:61
  1095.9 21.6 %collective-permute-done.41 = bf16[256,2048]{1,0:T(8,128)(2,1)S(1)} collective-permute-done((bf16[256,2048]{1,0:T(8,128)(2,1)S(1)}, bf16[256,2048]{1,0:T(8,128)(2,1)S(1)}, u32[]{:S(2)}, u32[]{:S(2)}) %collective-permute-start.41) | collective-permute-done | bytes 1048608 | tf_op jit(solution)/shard_map/ppermute | solution.py:61
  1137.8 11.9 collective-permute-done.43
  1150.5 15.0 %collective-permute-done.44 = bf16[256,1568]{0,1:T(8,128)(2,1)} collective-permute-done((bf16[256,1568]{0,1:T(8,128)(2,1)S(1)}, bf16[256,1568]{0,1:T(8,128)(2,1)}, u32[]{:S(2)}, u32[]{:S(2)}) %collective-permute-start.44) | collective-permute-done | bytes 802848 | tf_op jit(solution)/shard_map/ppermute | solution.py:61
  1173.5 5.2 convert_bitcast_fusion
  1179.3 5.9 copy.420
  1185.3 6.6 copy.421
  1194.9 6.7 collective-permute-done.48
  (738 shorter events, 436.2 us)
Async XLA Ops:
  7.2 77.3 %all-gather.7.cloned.1.call-start = ((), (), s32[]{:S(2)}) async-start(), calls=%async_computation.6 | async-start | bytes 7225344 | tf_op jit(solution)/shard_map/all_gather | solution.py:251
  15.5 148.2 %all-gather.9.cloned.1.call-start = ((), (), s32[]{:S(2)}) async-start(), calls=%async_computation.7 | async-start | bytes 2359296 | tf_op jit(solution)/shard_map/all_gather | solution.py:254
  16.4 382.8 %all-gather.11.cloned.1.call-start = ((), (), s32[]{:S(2)}) async-start(), calls=%async_computation.8 | async-start | bytes 14155776 | tf_op jit(solution)/shard_map/all_gather | solution.py:255
  84.6 374.1 %all-gather.13.cloned.1.call-start = ((), (), s32[]{:S(2)}) async-start(), calls=%async_computation.9 | async-start | bytes 14155776 | tf_op jit(solution)/shard_map/all_gather | solution.py:255
  84.7 26.1 %collective-permute-start = (bf16[256,2048]{1,0:T(8,128)(2,1)S(1)}, bf16[256,2048]{1,0:T(8,128)(2,1)S(1)}, u32[]{:S(2)}, u32[]{:S(2)}) collective-permute-start(bf16[256,2048]{1,0:T(8,128)(2,1)S(1)} %bitcast.581), channel_id=1, source_target_pairs={{0,8},{8,0},{16,24},{24,16},{1,9},{9,1},{17,25},{25,17},{2,10},{10... | collective-permute-start | bytes 3145736 | tf_op jit(solution)/shard_map/ppermute | solution.py:61
  86.2 47.5 %collective-permute-start.1 = (bf16[256,2048]{1,0:T(8,128)(2,1)S(1)}, bf16[256,2048]{1,0:T(8,128)(2,1)S(1)}, u32[]{:S(2)}, u32[]{:S(2)}) collective-permute-start(bf16[256,2048]{1,0:T(8,128)(2,1)S(1)} %bitcast.582), channel_id=1, source_target_pairs={{0,16},{8,24},{16,0},{24,8},{1,17},{9,25},{17,1},{25,9},{2,18},{10... | collective-permute-start | bytes 3145736 | tf_op jit(solution)/shard_map/ppermute | solution.py:61
  87.7 46.0 %collective-permute-start.2 = (bf16[256,2048]{1,0:T(8,128)(2,1)S(1)}, bf16[256,2048]{1,0:T(8,128)(2,1)S(1)}, u32[]{:S(2)}, u32[]{:S(2)}) collective-permute-start(bf16[256,2048]{1,0:T(8,128)(2,1)S(1)} %bitcast.583), channel_id=1, source_target_pairs={{0,24},{8,16},{16,8},{24,0},{1,25},{9,17},{17,9},{25,1},{2,26},{10... | collective-permute-start | bytes 3145736 | tf_op jit(solution)/shard_map/ppermute | solution.py:61
  135.4 249.7 %copy-start.70 = (bf16[20,2048]{1,0:T(8,128)(2,1)}, bf16[20,2048]{1,0:T(8,128)(2,1)S(1)}, u32[]{:S(2)}) copy-start(bf16[20,2048]{1,0:T(8,128)(2,1)S(1)} %slice_bitcast_fusion.47) | copy-start | bytes 245764
  135.4 209.2 %copy-start.82 = (f32[1,2048]{1,0:T(1,128)}, f32[1,2048]{1,0:T(1,128)S(1)}, u32[]{:S(2)}) copy-start(f32[1,2048]{1,0:T(1,128)S(1)} %get-tuple-element.662) | copy-start | bytes 24580
  148.0 3.7 collective-permute-start.5
  149.3 3.7 collective-permute-start.6
  150.1 4.5 collective-permute-start.7
  161.2 380.6 %all-gather.15.cloned.1.call-start = ((), (), s32[]{:S(2)}) async-start(), calls=%async_computation.10 | async-start | bytes 14155776 | tf_op jit(solution)/shard_map/all_gather | solution.py:255
  163.7 105.4 %collective-permute-start.12 = (bf16[2048,512]{0,1:T(8,128)(2,1)}, bf16[2048,512]{0,1:T(8,128)(2,1)}, u32[]{:S(2)}, u32[]{:S(2)}) collective-permute-start(bf16[2048,512]{0,1:T(8,128)(2,1)} %all-gather.9.cloned.1.call-done), channel_id=1, source_target_pairs={{0,8},{8,0},{16,24},{24,16},{1,9},{9,1},{17,25},{25,17},{2,10},{10... | collective-permute-start | bytes 6291464 | tf_op jit(solution)/shard_map/ppermute | solution.py:61
  165.2 107.4 %collective-permute-start.13 = (bf16[2048,512]{0,1:T(8,128)(2,1)}, bf16[2048,512]{0,1:T(8,128)(2,1)}, u32[]{:S(2)}, u32[]{:S(2)}) collective-permute-start(bf16[2048,512]{0,1:T(8,128)(2,1)} %all-gather.9.cloned.1.call-done), channel_id=1, source_target_pairs={{0,16},{8,24},{16,0},{24,8},{1,17},{9,25},{17,1},{25,9},{2,18},{10... | collective-permute-start | bytes 6291464 | tf_op jit(solution)/shard_map/ppermute | solution.py:61
  196.0 22.2 %collective-permute-start.9 = (bf16[256,512]{1,0:T(8,128)(2,1)}, bf16[256,512]{1,0:T(8,128)(2,1)}, u32[]{:S(2)}, u32[]{:S(2)}) collective-permute-start(bf16[256,512]{1,0:T(8,128)(2,1)} %get-tuple-element.656), channel_id=1, source_target_pairs={{0,8},{8,0},{16,24},{24,16},{1,9},{9,1},{17,25},{25,17},{2,10},{10... | collective-permute-start | bytes 786440 | tf_op jit(solution)/shard_map/ppermute | solution.py:61
  197.3 78.5 %collective-permute-start.14 = (bf16[2048,512]{0,1:T(8,128)(2,1)}, bf16[2048,512]{0,1:T(8,128)(2,1)}, u32[]{:S(2)}, u32[]{:S(2)}) collective-permute-start(bf16[2048,512]{0,1:T(8,128)(2,1)} %all-gather.9.cloned.1.call-done), channel_id=1, source_target_pairs={{0,24},{8,16},{16,8},{24,0},{1,25},{9,17},{17,9},{25,1},{2,26},{10... | collective-permute-start | bytes 6291464 | tf_op jit(solution)/shard_map/ppermute | solution.py:61
  199.1 67.7 %collective-permute-start.10 = (bf16[256,512]{1,0:T(8,128)(2,1)}, bf16[256,512]{1,0:T(8,128)(2,1)}, u32[]{:S(2)}, u32[]{:S(2)}) collective-permute-start(bf16[256,512]{1,0:T(8,128)(2,1)} %get-tuple-element.655), channel_id=1, source_target_pairs={{0,16},{8,24},{16,0},{24,8},{1,17},{9,25},{17,1},{25,9},{2,18},{10... | collective-permute-start | bytes 786440 | tf_op jit(solution)/shard_map/ppermute | solution.py:61
  218.2 49.7 %collective-permute-start.11 = (bf16[256,512]{1,0:T(8,128)(2,1)}, bf16[256,512]{1,0:T(8,128)(2,1)}, u32[]{:S(2)}, u32[]{:S(2)}) collective-permute-start(bf16[256,512]{1,0:T(8,128)(2,1)} %get-tuple-element.654), channel_id=1, source_target_pairs={{0,24},{8,16},{16,8},{24,0},{1,25},{9,17},{17,9},{25,1},{2,26},{10... | collective-permute-start | bytes 786440 | tf_op jit(solution)/shard_map/ppermute | solution.py:61
  286.8 333.3 %all-gather.17.cloned.1.call-start = ((), (), s32[]{:S(2)}) async-start(), calls=%async_computation.11 | async-start | bytes 14155776 | tf_op jit(solution)/shard_map/all_gather | solution.py:255
  289.5 27.0 %collective-permute-start.3 = (bf16[257,2048]{1,0:T(8,128)(2,1)}, bf16[257,2048]{1,0:T(8,128)(2,1)}, u32[]{:S(2)}, u32[]{:S(2)}) collective-permute-start(bf16[257,2048]{1,0:T(8,128)(2,1)} %pad_maximum_fusion.30), channel_id=1, source_target_pairs={{0,8},{8,0},{16,24},{24,16},{1,9},{9,1},{17,25},{25,17},{2,10},{10... | collective-permute-start | bytes 3158024 | tf_op jit(solution)/shard_map/ppermute | solution.py:61
  290.1 44.9 %collective-permute-start.4 = (bf16[257,2048]{1,0:T(8,128)(2,1)}, bf16[257,2048]{1,0:T(8,128)(2,1)}, u32[]{:S(2)}, u32[]{:S(2)}) collective-permute-start(bf16[257,2048]{1,0:T(8,128)(2,1)} %pad_maximum_fusion.30), channel_id=1, source_target_pairs={{0,16},{8,24},{16,0},{24,8},{1,17},{9,25},{17,1},{25,9},{2,18},{10... | collective-permute-start | bytes 3158024 | tf_op jit(solution)/shard_map/ppermute | solution.py:61
  291.5 43.5 %collective-permute-start.8 = (bf16[257,2048]{1,0:T(8,128)(2,1)}, bf16[257,2048]{1,0:T(8,128)(2,1)}, u32[]{:S(2)}, u32[]{:S(2)}) collective-permute-start(bf16[257,2048]{1,0:T(8,128)(2,1)} %pad_maximum_fusion.30), channel_id=1, source_target_pairs={{0,24},{8,16},{16,8},{24,0},{1,25},{9,17},{17,9},{25,1},{2,26},{10... | collective-permute-start | bytes 3158024 | tf_op jit(solution)/shard_map/ppermute | solution.py:61
  339.3 26.3 %collective-permute-start.15 = (bf16[256,2048]{1,0:T(8,128)(2,1)}, bf16[256,2048]{1,0:T(8,128)(2,1)S(1)}, u32[]{:S(2)}, u32[]{:S(2)}) collective-permute-start(bf16[256,2048]{1,0:T(8,128)(2,1)} %multiply_convert_fusion.20), channel_id=1, source_target_pairs={{0,8},{8,0},{16,24},{24,16},{1,9},{9,1},{17,25},{25,17},{2,10},{10... | collective-permute-start | bytes 3145736 | tf_op jit(solution)/shard_map/ppermute | solution.py:61
  340.8 40.4 %collective-permute-start.16 = (bf16[256,2048]{1,0:T(8,128)(2,1)}, bf16[256,2048]{1,0:T(8,128)(2,1)S(1)}, u32[]{:S(2)}, u32[]{:S(2)}) collective-permute-start(bf16[256,2048]{1,0:T(8,128)(2,1)} %multiply_convert_fusion.20), channel_id=1, source_target_pairs={{0,16},{8,24},{16,0},{24,8},{1,17},{9,25},{17,1},{25,9},{2,18},{10... | collective-permute-start | bytes 3145736 | tf_op jit(solution)/shard_map/ppermute | solution.py:61
  341.1 41.7 %collective-permute-start.17 = (bf16[256,2048]{1,0:T(8,128)(2,1)}, bf16[256,2048]{1,0:T(8,128)(2,1)S(1)}, u32[]{:S(2)}, u32[]{:S(2)}) collective-permute-start(bf16[256,2048]{1,0:T(8,128)(2,1)} %multiply_convert_fusion.20), channel_id=1, source_target_pairs={{0,24},{8,16},{16,8},{24,0},{1,25},{9,17},{17,9},{25,1},{2,26},{10... | collective-permute-start | bytes 3145736 | tf_op jit(solution)/shard_map/ppermute | solution.py:61
  399.1 454.6 %reduce-scatter.7.cloned.1.call-start = ((), (), s32[]{:S(2)}) async-start(), calls=%async_computation.12 | async-start | bytes 7864320 | tf_op jit(solution)/shard_map/reduce_scatter | solution.py:195
  449.7 22.1 %collective-permute-start.18 = (bf16[4,384,2048]{2,1,0:T(8,128)(2,1)}, bf16[4,384,2048]{2,1,0:T(8,128)(2,1)}, u32[]{:S(2)}, u32[]{:S(2)}) collective-permute-start(bf16[4,384,2048]{2,1,0:T(8,128)(2,1)} %pad_maximum_fusion.1), channel_id=1, source_target_pairs={{0,1},{1,0},{2,3},{3,2},{4,5},{5,4},{6,7},{7,6},{8,9},{9,8},{10,11... | collective-permute-start | bytes 18874376 | tf_op jit(solution)/shard_map/ppermute | solution.py:187
  520.8 34.1 %collective-permute-start.19 = (bf16[4,384,2048]{2,1,0:T(8,128)(2,1)}, bf16[4,384,2048]{2,1,0:T(8,128)(2,1)}, u32[]{:S(2)}, u32[]{:S(2)}) collective-permute-start(bf16[4,384,2048]{2,1,0:T(8,128)(2,1)} %pad_maximum_fusion.2), channel_id=1, source_target_pairs={{0,1},{1,0},{2,3},{3,2},{4,5},{5,4},{6,7},{7,6},{8,9},{9,8},{10,11... | collective-permute-start | bytes 18874376 | tf_op jit(solution)/shard_map/ppermute | solution.py:187
  532.5 443.2 %reduce-scatter.9.cloned.1.call-start = ((), (), s32[]{:S(2)}) async-start(), calls=%async_computation.13 | async-start | bytes 7864320 | tf_op jit(solution)/shard_map/reduce_scatter | solution.py:195
  602.8 59.2 %collective-permute-start.20 = (bf16[4,384,2048]{2,1,0:T(8,128)(2,1)}, bf16[4,384,2048]{2,1,0:T(8,128)(2,1)}, u32[]{:S(2)}, u32[]{:S(2)}) collective-permute-start(bf16[4,384,2048]{2,1,0:T(8,128)(2,1)} %pad_maximum_fusion.3), channel_id=1, source_target_pairs={{0,1},{1,0},{2,3},{3,2},{4,5},{5,4},{6,7},{7,6},{8,9},{9,8},{10,11... | collective-permute-start | bytes 18874376 | tf_op jit(solution)/shard_map/ppermute | solution.py:187
  652.5 398.9 %reduce-scatter.15.cloned.1.call-start = ((), (), s32[]{:S(2)}) async-start(), calls=%async_computation.16 | async-start | bytes 7864320 | tf_op jit(solution)/shard_map/reduce_scatter | solution.py:195
  704.8 26.3 %collective-permute-start.21 = (f32[4,256]{1,0:T(4,128)S(1)}, f32[4,256]{1,0:T(4,128)S(1)}, u32[]{:S(2)}, u32[]{:S(2)}) collective-permute-start(f32[4,256]{1,0:T(4,128)S(1)} %get-tuple-element.670), channel_id=1, source_target_pairs={{0,8},{8,0},{16,24},{24,16},{1,9},{9,1},{17,25},{25,17},{2,10},{10... | collective-permute-start | bytes 12296 | tf_op jit(solution)/shard_map/ppermute | solution.py:61
  713.1 49.6 %collective-permute-start.24 = (bf16[256,2048]{1,0:T(8,128)(2,1)}, bf16[256,2048]{1,0:T(8,128)(2,1)}, u32[]{:S(2)}, u32[]{:S(2)}) collective-permute-start(bf16[256,2048]{1,0:T(8,128)(2,1)} %get-tuple-element.611), channel_id=1, source_target_pairs={{0,8},{8,0},{16,24},{24,16},{1,9},{9,1},{17,25},{25,17},{2,10},{10... | collective-permute-start | bytes 3145736 | tf_op jit(solution)/shard_map/ppermute | solution.py:61
  714.7 48.0 %collective-permute-start.25 = (bf16[256,2048]{1,0:T(8,128)(2,1)}, bf16[256,2048]{1,0:T(8,128)(2,1)}, u32[]{:S(2)}, u32[]{:S(2)}) collective-permute-start(bf16[256,2048]{1,0:T(8,128)(2,1)} %get-tuple-element.610), channel_id=1, source_target_pairs={{0,16},{8,24},{16,0},{24,8},{1,17},{9,25},{17,1},{25,9},{2,18},{10... | collective-permute-start | bytes 3145736 | tf_op jit(solution)/shard_map/ppermute | solution.py:61
  715.4 47.4 %collective-permute-start.26 = (bf16[256,2048]{1,0:T(8,128)(2,1)}, bf16[256,2048]{1,0:T(8,128)(2,1)}, u32[]{:S(2)}, u32[]{:S(2)}) collective-permute-start(bf16[256,2048]{1,0:T(8,128)(2,1)} %get-tuple-element.609), channel_id=1, source_target_pairs={{0,24},{8,16},{16,8},{24,0},{1,25},{9,17},{17,9},{25,1},{2,26},{10... | collective-permute-start | bytes 3145736 | tf_op jit(solution)/shard_map/ppermute | solution.py:61
  729.4 33.2 %collective-permute-start.22 = (f32[4,256]{1,0:T(4,128)S(1)}, f32[4,256]{1,0:T(4,128)S(1)}, u32[]{:S(2)}, u32[]{:S(2)}) collective-permute-start(f32[4,256]{1,0:T(4,128)S(1)} %get-tuple-element.669), channel_id=1, source_target_pairs={{0,16},{8,24},{16,0},{24,8},{1,17},{9,25},{17,1},{25,9},{2,18},{10... | collective-permute-start | bytes 12296 | tf_op jit(solution)/shard_map/ppermute | solution.py:61
  731.1 31.6 %collective-permute-start.23 = (f32[4,256]{1,0:T(4,128)S(1)}, f32[4,256]{1,0:T(4,128)S(1)}, u32[]{:S(2)}, u32[]{:S(2)}) collective-permute-start(f32[4,256]{1,0:T(4,128)S(1)} %get-tuple-element.668), channel_id=1, source_target_pairs={{0,24},{8,16},{16,8},{24,0},{1,25},{9,17},{17,9},{25,1},{2,26},{10... | collective-permute-start | bytes 12296 | tf_op jit(solution)/shard_map/ppermute | solution.py:61
  779.5 9.4 collective-permute-start.27
  780.0 13.0 %collective-permute-start.28 = (bf16[256,512]{1,0:T(8,128)(2,1)S(1)}, bf16[256,512]{1,0:T(8,128)(2,1)}, u32[]{:S(2)}, u32[]{:S(2)}) collective-permute-start(bf16[256,512]{1,0:T(8,128)(2,1)S(1)} %bitcast.653), channel_id=1, source_target_pairs={{0,16},{8,24},{16,0},{24,8},{1,17},{9,25},{17,1},{25,9},{2,18},{10... | collective-permute-start | bytes 786440 | tf_op jit(solution)/shard_map/ppermute | solution.py:61
  781.9 11.1 collective-permute-start.29
  799.1 57.8 %collective-permute-start.30 = (bf16[256,2048]{1,0:T(8,128)(2,1)}, bf16[256,2048]{1,0:T(8,128)(2,1)}, u32[]{:S(2)}, u32[]{:S(2)}) collective-permute-start(bf16[256,2048]{1,0:T(8,128)(2,1)} %get-tuple-element.608), channel_id=1, source_target_pairs={{0,8},{8,0},{16,24},{24,16},{1,9},{9,1},{17,25},{25,17},{2,10},{10... | collective-permute-start | bytes 3145736 | tf_op jit(solution)/shard_map/ppermute | solution.py:61
  800.6 56.3 %collective-permute-start.31 = (bf16[256,2048]{1,0:T(8,128)(2,1)}, bf16[256,2048]{1,0:T(8,128)(2,1)}, u32[]{:S(2)}, u32[]{:S(2)}) collective-permute-start(bf16[256,2048]{1,0:T(8,128)(2,1)} %get-tuple-element.607), channel_id=1, source_target_pairs={{0,16},{8,24},{16,0},{24,8},{1,17},{9,25},{17,1},{25,9},{2,18},{10... | collective-permute-start | bytes 3145736 | tf_op jit(solution)/shard_map/ppermute | solution.py:61
  800.9 56.0 %collective-permute-start.32 = (bf16[256,2048]{1,0:T(8,128)(2,1)}, bf16[256,2048]{1,0:T(8,128)(2,1)}, u32[]{:S(2)}, u32[]{:S(2)}) collective-permute-start(bf16[256,2048]{1,0:T(8,128)(2,1)} %get-tuple-element.606), channel_id=1, source_target_pairs={{0,24},{8,16},{16,8},{24,0},{1,25},{9,17},{17,9},{25,1},{2,26},{10... | collective-permute-start | bytes 3145736 | tf_op jit(solution)/shard_map/ppermute | solution.py:61
  856.8 206.6 %reduce-scatter.11.cloned.1.call-start = ((), (), s32[]{:S(2)}) async-start(), calls=%async_computation.14 | async-start | bytes 4259840 | tf_op jit(solution)/shard_map/reduce_scatter | solution.py:195
  868.4 3.7 collective-permute-start.33
  869.9 3.7 collective-permute-start.34
  870.0 4.5 collective-permute-start.35
  883.6 43.3 %collective-permute-start.36 = (bf16[2048,512]{0,1:T(8,128)(2,1)}, bf16[2048,512]{0,1:T(8,128)(2,1)}, u32[]{:S(2)}, u32[]{:S(2)}) collective-permute-start(bf16[2048,512]{0,1:T(8,128)(2,1)} %get-tuple-element.571), channel_id=1, source_target_pairs={{0,8},{8,0},{16,24},{24,16},{1,9},{9,1},{17,25},{25,17},{2,10},{10... | collective-permute-start | bytes 6291464 | tf_op jit(solution)/shard_map/ppermute | solution.py:61
  885.5 42.6 %collective-permute-start.37 = (bf16[2048,512]{0,1:T(8,128)(2,1)}, bf16[2048,512]{0,1:T(8,128)(2,1)}, u32[]{:S(2)}, u32[]{:S(2)}) collective-permute-start(bf16[2048,512]{0,1:T(8,128)(2,1)} %get-tuple-element.570), channel_id=1, source_target_pairs={{0,16},{8,24},{16,0},{24,8},{1,17},{9,25},{17,1},{25,9},{2,18},{10... | collective-permute-start | bytes 6291464 | tf_op jit(solution)/shard_map/ppermute | solution.py:61
  961.6 5.8 collective-permute-start.39
  975.7 203.0 %reduce-scatter.17.cloned.1.call-start = ((), (), s32[]{:S(2)}) async-start(), calls=%async_computation.17 | async-start | bytes 2359296 | tf_op jit(solution)/shard_map/reduce_scatter | solution.py:372
  990.3 61.3 %collective-permute-start.38 = (bf16[4,384,2048]{2,1,0:T(8,128)(2,1)}, bf16[4,384,2048]{2,1,0:T(8,128)(2,1)}, u32[]{:S(2)}, u32[]{:S(2)}) collective-permute-start(bf16[4,384,2048]{2,1,0:T(8,128)(2,1)} %pad_maximum_fusion.4), channel_id=1, source_target_pairs={{0,1},{1,0},{2,3},{3,2},{4,5},{5,4},{6,7},{7,6},{8,9},{9,8},{10,11... | collective-permute-start | bytes 18874376 | tf_op jit(solution)/shard_map/ppermute | solution.py:187
  997.2 48.9 %collective-permute-start.46 = (bf16[2048,512]{0,1:T(8,128)(2,1)}, bf16[2048,512]{0,1:T(8,128)(2,1)S(1)}, u32[]{:S(2)}, u32[]{:S(2)}) collective-permute-start(bf16[2048,512]{0,1:T(8,128)(2,1)} %copy.416), channel_id=1, source_target_pairs={{0,24},{8,16},{16,8},{24,0},{1,25},{9,17},{17,9},{25,1},{2,26},{10... | collective-permute-start | bytes 6291464 | tf_op jit(solution)/shard_map/ppermute | solution.py:61
  1051.5 150.5 %reduce-scatter.13.cloned.1.call-start = ((), (), s32[]{:S(2)}) async-start(), calls=%async_computation.15 | async-start | bytes 7864320 | tf_op jit(solution)/shard_map/reduce_scatter | solution.py:195
  1069.8 26.1 %collective-permute-start.40 = (bf16[256,2048]{1,0:T(8,128)(2,1)S(1)}, bf16[256,2048]{1,0:T(8,128)(2,1)S(1)}, u32[]{:S(2)}, u32[]{:S(2)}) collective-permute-start(bf16[256,2048]{1,0:T(8,128)(2,1)S(1)} %get-tuple-element.601), channel_id=1, source_target_pairs={{0,8},{8,0},{16,24},{24,16},{1,9},{9,1},{17,25},{25,17},{2,10},{10... | collective-permute-start | bytes 3145736 | tf_op jit(solution)/shard_map/ppermute | solution.py:61
  1070.8 46.7 %collective-permute-start.41 = (bf16[256,2048]{1,0:T(8,128)(2,1)S(1)}, bf16[256,2048]{1,0:T(8,128)(2,1)S(1)}, u32[]{:S(2)}, u32[]{:S(2)}) collective-permute-start(bf16[256,2048]{1,0:T(8,128)(2,1)S(1)} %get-tuple-element.603), channel_id=1, source_target_pairs={{0,16},{8,24},{16,0},{24,8},{1,17},{9,25},{17,1},{25,9},{2,18},{10... | collective-permute-start | bytes 3145736 | tf_op jit(solution)/shard_map/ppermute | solution.py:61
  1072.3 45.2 %collective-permute-start.42 = (bf16[256,2048]{1,0:T(8,128)(2,1)S(1)}, bf16[256,2048]{1,0:T(8,128)(2,1)S(1)}, u32[]{:S(2)}, u32[]{:S(2)}) collective-permute-start(bf16[256,2048]{1,0:T(8,128)(2,1)S(1)} %get-tuple-element.602), channel_id=1, source_target_pairs={{0,24},{8,16},{16,8},{24,0},{1,25},{9,17},{17,9},{25,1},{2,26},{10... | collective-permute-start | bytes 3145736 | tf_op jit(solution)/shard_map/ppermute | solution.py:61
  1128.7 20.9 %collective-permute-start.43 = (bf16[256,1568]{0,1:T(8,128)(2,1)S(1)}, bf16[256,1568]{0,1:T(8,128)(2,1)}, u32[]{:S(2)}, u32[]{:S(2)}) collective-permute-start(bf16[256,1568]{0,1:T(8,128)(2,1)S(1)} %copy.408), channel_id=1, source_target_pairs={{0,8},{8,0},{16,24},{24,16},{1,9},{9,1},{17,25},{25,17},{2,10},{10... | collective-permute-start | bytes 2408456 | tf_op jit(solution)/shard_map/ppermute | solution.py:61
  1130.0 35.5 %collective-permute-start.44 = (bf16[256,1568]{0,1:T(8,128)(2,1)S(1)}, bf16[256,1568]{0,1:T(8,128)(2,1)}, u32[]{:S(2)}, u32[]{:S(2)}) collective-permute-start(bf16[256,1568]{0,1:T(8,128)(2,1)S(1)} %copy.408), channel_id=1, source_target_pairs={{0,16},{8,24},{16,0},{24,8},{1,17},{9,25},{17,1},{25,9},{2,18},{10... | collective-permute-start | bytes 2408456 | tf_op jit(solution)/shard_map/ppermute | solution.py:61
  1130.9 35.5 %collective-permute-start.45 = (bf16[256,1568]{0,1:T(8,128)(2,1)S(1)}, bf16[256,1568]{0,1:T(8,128)(2,1)}, u32[]{:S(2)}, u32[]{:S(2)}) collective-permute-start(bf16[256,1568]{0,1:T(8,128)(2,1)S(1)} %copy.408), channel_id=1, source_target_pairs={{0,24},{8,16},{16,8},{24,0},{1,25},{9,17},{17,9},{25,1},{2,26},{10... | collective-permute-start | bytes 2408456 | tf_op jit(solution)/shard_map/ppermute | solution.py:61
  1178.7 16.2 %collective-permute-start.47 = (bf16[256,512]{0,1:T(8,128)(2,1)}, bf16[256,512]{0,1:T(8,128)(2,1)S(1)}, u32[]{:S(2)}, u32[]{:S(2)}) collective-permute-start(bf16[256,512]{0,1:T(8,128)(2,1)} %reduce-scatter.17.cloned.1.call-done), channel_id=1, source_target_pairs={{0,8},{8,0},{16,24},{24,16},{1,9},{9,1},{17,25},{25,17},{2,10},{10... | collective-permute-start | bytes 786440 | tf_op jit(solution)/shard_map/ppermute | solution.py:61
  1191.9 9.7 collective-permute-start.48
  1192.2 9.5 collective-permute-start.49
  (159 other events, 2290.6 us)
Sparse Core Ops, SparseCore 0:
  15.6 68.9 all-gather.6
  86.7 28.7 all-gather.8
  117.2 115.6 all-gather.10
  234.4 114.8 all-gather.12
  350.8 114.8 all-gather.14
  467.2 114.8 all-gather.16
  584.4 108.9 reduce-scatter.6
  695.7 111.3 reduce-scatter.8
  857.0 109.1 reduce-scatter.14
  975.8 62.4 reduce-scatter.10
  1051.6 34.4 reduce-scatter.16
  1088.2 109.3 reduce-scatter.12
